TPU v7x, 32 devices: a whole 2x2x4 slice. The times are simulated.
32 devices in a mesh: groups: 2 (over x), bus: 16 (over z, y, core).
Axes of the slice: x: 2, y: 2, z: 4, core: 2. Of those that a mesh axis runs over, the one named last changes fastest.
Arguments:
- generation: float32 [512, 32], P('bus', 'groups'), parts along dimension 1, may hold values from 0 to 1
- charging: float32 [32, 512], P('groups', 'bus'), parts along dimension 0, may hold values from -1.5 to 1.5
- flow_dual: float32 [4096, 32], P('bus', 'groups'), parts along dimension 1, may hold values from -3 to 3
- energy_dual: float32 [32, 512], P('groups', 'bus'), parts along dimension 0, may hold values from -1.6 to 1.6
- shift_factors: float32 [4096, 16384], P(None, 'bus'), may hold values from -0.0625 to 0.0625
- load_units: int32 [16384, 32], P('bus', 'groups'), parts along dimension 1, may hold values from 0 to 59
- generator_bus: int32 [512], P('bus'), may hold values from 0 to 16383, as said below
- storage_bus: int32 [512], P('bus'), may hold values from 0 to 16383, as said below
- generator_cost: float32 [512], P('bus'), may hold values from 0.05 to 0.5
- generator_max: float32 [512], P('bus'), may hold values from 1 to 4
- charging_max: float32 [512], replicated, may hold values from 2 to 4
- energy_init: float32 [512], replicated, may hold values from 0.5 to 2
- energy_max: float32 [512], replicated, may hold values from 2.5 to 4
- line_max: float32 [4096], P('bus'), may hold values from 0.5 to 3
Outputs:
- generation_new: float32 [512, 32], P('bus', 'groups'), parts along dimension 1
- charging_new: float32 [32, 512], P('groups', 'bus'), parts along dimension 0
- flow_dual_new: float32 [4096, 32], P('bus', 'groups'), parts along dimension 1
- energy_dual_new: float32 [32, 512], P('groups', 'bus'), parts along dimension 0
There are 2 independent parts, one for each index of `groups`. A program takes and returns all parts, laid end to end along the dimension named above; an argument that names none is the same for every part. Nothing has to cross between parts.
Inputs may be any that keep to these rules, and one draw needn't show every extreme that they name: `generator_bus`: generator g sits at one of the buses g // 32 * 1024 to (g // 32 + 1) * 1024 - 1. `storage_bus`: storage unit k sits at one of the buses k // 32 * 1024 to (k // 32 + 1) * 1024 - 1.
All inputs are finite; a program needn't handle non-finite values.
Results may differ from a plain program's by a relative error of at most 0.00023.
Values sent between devices are 32-bit elements; how exact they have to be, the bound alone decides.
No kernel may reach another device: no remote copies, remote signals or barrier semaphores. Data moves between devices by JAX's collectives and lax.ppermute only.
A program may use at most 64 MiB of HBM per device.

v0:
```python
import functools

import jax
import jax.numpy as jnp
from jax import lax
from jax.experimental import pallas as pl
from jax.experimental.pallas import tpu as pltpu
from jax.sharding import PartitionSpec as P


ITERS = 3

QUAD = 4
primal_step = 0.5
dual_step = 0.5
energy_step = 0.05
efficiency = 0.95
interval = 0.125
load_unit = 0.05
rows_by_cols = (((1,), (0,)), ((), ()))
rows_by_rows = (((1,), (1,)), ((), ()))


def split_halves(values):
    high = values.astype(jnp.bfloat16)
    low = (values - high.astype(jnp.float32)).astype(jnp.bfloat16)
    return high, low


def matmul(left, right, dims):
    return lax.dot_general(left, right, dims, preferred_element_type=jnp.float32)


def clip_dual(shifted, step_size, low_bound, high_bound):
    return shifted - step_size * jnp.clip(shifted / step_size, low_bound, high_bound)


def running_sum(values, reverse):
    count = values.shape[0]
    shift = 1
    while shift < count:
        zeros = jnp.zeros((shift, values.shape[1]), values.dtype)
        if reverse:
            moved = jnp.concatenate([values[shift:], zeros], axis=0)
        else:
            moved = jnp.concatenate([zeros, values[:-shift]], axis=0)
        values = values + moved
        shift *= 2
    return values


def near_array(shape, dtype=jnp.float32):
    return pltpu.VMEM(shape, dtype)


def near(values):
    return pltpu.with_memory_space_constraint(values, pltpu.VMEM)


def far_array(values):
    return pltpu.with_memory_space_constraint(values, pltpu.HBM)


whole_block = pl.BlockSpec(memory_space=pltpu.VMEM)
grant = pltpu.CompilerParams(vmem_limit_bytes=24 << 20)


def as_column(row):
    width = row.shape[1]
    across = lax.broadcasted_iota(jnp.int32, (width, width), 1)
    down = lax.broadcasted_iota(jnp.int32, (width, width), 0)
    return jnp.sum(jnp.where(across == down, row, 0), axis=1, keepdims=True)


def scan_kernel(
    generator_bus, storage_bus, loads, factors, after, columns, demand,
    stage, arrived, ids_a, ids_b, counts, small,
    *, wanted, own_lines, far,
):
    buses = factors.shape[1]
    own = lax.axis_index("bus")
    member = own % QUAD
    few = []
    for index, (source, target) in enumerate(
        ((generator_bus, ids_a), (storage_bus, ids_b), (loads, counts))
    ):
        few.append(pltpu.make_async_copy(source, target, small.at[index]))
    copies = []
    for at, r in enumerate(wanted):
        for z in range(far):
            first = (z * QUAD + (member ^ r)) * own_lines
            index = at * far + z
            copies.append(
                pltpu.make_async_copy(
                    factors.at[pl.ds(pl.multiple_of(first, own_lines), own_lines)],
                    stage.at[pl.ds(index * own_lines, own_lines)],
                    arrived.at[index],
                )
            )
    for copy in few + copies:
        copy.start()
    for copy in few:
        copy.wait()
    ids = jnp.concatenate([as_column(ids_a[...]), as_column(ids_b[...])], axis=0)
    ids = ids - own * buses
    spots = lax.broadcasted_iota(jnp.int32, (ids.shape[0], buses), 1)
    picks = (spots == ids).astype(jnp.float32)
    weights = jnp.concatenate([picks, counts[...].astype(jnp.float32)], axis=0)
    weights = weights.astype(jnp.bfloat16)
    units = ids.shape[0]
    quarter = far * own_lines
    tile = max(own_lines, min(512, quarter))
    per_tile = tile // own_lines
    for t in range(len(wanted) * quarter // tile):
        first = t * per_tile
        for copy in copies[first : first + per_tile]:
            copy.wait()
        rows = stage[pl.ds(first * own_lines, tile), :]
        high, low = split_halves(rows)
        found = matmul(weights, high, rows_by_rows) + matmul(weights, low, rows_by_rows)
        at, lane = divmod(t * tile, quarter)
        spot = pl.ds(lane, tile)
        columns[at * units : (at + 1) * units, spot] = found[:units]
        horizon = loads.shape[0]
        demand[at * horizon : (at + 1) * horizon, spot] = load_unit * found[units:]


def scan_factors(generator_bus, storage_bus, loads, factors, after, wanted, own_lines, far):
    units = generator_bus.shape[1] + storage_bus.shape[1]
    copies = len(wanted) * far
    quarter = far * own_lines
    arrays = (generator_bus, storage_bus, loads, factors)
    return pl.pallas_call(
        functools.partial(scan_kernel, wanted=wanted, own_lines=own_lines, far=far),
        in_specs=[pl.BlockSpec(memory_space=pltpu.HBM)] * 4 + [pl.BlockSpec(memory_space=pl.ANY)],
        out_specs=[whole_block] * 2,
        out_shape=[
            near_array((len(wanted) * units, quarter)),
            near_array((len(wanted) * loads.shape[0], quarter)),
        ],
        scratch_shapes=[
            pltpu.VMEM((copies * own_lines, factors.shape[1]), jnp.float32),
            pltpu.SemaphoreType.DMA((copies,)),
            pltpu.VMEM(generator_bus.shape, jnp.int32),
            pltpu.VMEM(storage_bus.shape, jnp.int32),
            pltpu.VMEM(loads.shape, jnp.int32),
            pltpu.SemaphoreType.DMA((3,)),
        ],
        compiler_params=grant,
        name="scan_factors",
    )(*[far_array(a) for a in arrays], after)


def place_kernel(generation, charging, energy_dual, cost, ceiling, dual, limit, state, lines):
    own = lax.axis_index("bus")
    rows = jnp.concatenate(
        [generation[...], charging[...], energy_dual[...], cost[...], ceiling[...]], axis=0
    )
    for values, out, slot in ((rows, state, own % QUAD), (None, lines, own // QUAD)):
        if values is None:
            values = jnp.concatenate([dual[...], limit[...]], axis=0)
        width = values.shape[1]
        repeats = out.shape[1] // width
        spread = jnp.concatenate([values] * repeats, axis=1)
        where = lax.broadcasted_iota(jnp.int32, spread.shape, 1) // width
        out[...] = jnp.where(where == slot, spread, 0.0)


def place(generation, charging, energy_dual, cost, ceiling, dual, limit, far):
    horizon, gens = generation.shape
    return pl.pallas_call(
        place_kernel,
        out_specs=[whole_block] * 2,
        out_shape=[
            near_array((3 * horizon + 2, QUAD * gens)),
            near_array((horizon + 1, far * dual.shape[1])),
        ],
        compiler_params=grant,
        name="place",
    )(generation, charging, energy_dual, cost, ceiling, dual, limit)


def local_prices(dual, columns):
    horizon = dual.shape[0]
    units = columns.shape[0] // 2
    stacked = jnp.concatenate(split_halves(dual), axis=0)
    parts = matmul(stacked, columns, rows_by_rows)
    return parts[:horizon, :units] + parts[:horizon, units:] + parts[horizon:, :units]


def gather_kernel(block0, block1, block2, block3, dual, columns, prices):
    horizon = prices.shape[0]
    units = columns.shape[0] // (2 * QUAD)
    group = units // 2
    member = lax.axis_index("bus") % QUAD
    for r, block in enumerate((block0, block1, block2, block3)):
        high, low = split_halves(block[:units, :])
        for kind in range(2):
            first = kind * QUAD * group + (member ^ r) * group
            spot = pl.ds(pl.multiple_of(first, group), group)
            columns[spot, :] = high[kind * group : (kind + 1) * group]
            first = first + QUAD * units
            spot = pl.ds(pl.multiple_of(first, group), group)
            columns[spot, :] = low[kind * group : (kind + 1) * group]
    prices[...] = local_prices(dual[:horizon, :], columns[...])


def gather_columns(blocks, dual, horizon):
    units, quarter = blocks[3].shape
    return pl.pallas_call(
        gather_kernel,
        in_specs=[whole_block] * 5,
        out_specs=[whole_block] * 2,
        out_shape=[
            near_array((2 * QUAD * units, quarter), jnp.bfloat16),
            near_array((horizon, QUAD * units)),
        ],
        compiler_params=grant,
        name="gather_columns",
    )(*[near(block) for block in blocks], near(dual))


def unit_kernel(
    prices_a, prices_b, state, bounds, columns, base_flow, new_state, flows, *held_flows, order
):
    horizon = flows.shape[0]
    gens = state.shape[1]
    prices = prices_a[...] + prices_b[...]
    old = state[:horizon, :]
    held = state[horizon : 2 * horizon, :]
    duals = state[2 * horizon : 3 * horizon, :]
    cost = state[3 * horizon : 3 * horizon + 1, :]
    ceiling = state[3 * horizon + 1 : 3 * horizon + 2, :]
    charge_limit = bounds[0:1, :]
    start_energy = bounds[1:2, :]
    energy_limit = bounds[2:3, :]
    gen_step = jnp.clip(old - primal_step * (cost + prices[:, :gens]), 0.0, ceiling)
    gen_bar = 2.0 * gen_step - old
    gradient = efficiency * interval * running_sum(duals, True) - prices[:, gens:]
    charge_step = jnp.clip(held - primal_step * gradient, -charge_limit, charge_limit)
    charge_bar = 2.0 * charge_step - held
    bars_high, bars_low = split_halves(jnp.concatenate([gen_bar, -charge_bar], axis=1))
    bars = jnp.concatenate(
        [
            jnp.concatenate([bars_high, bars_high], axis=1),
            jnp.concatenate([bars_low, jnp.zeros_like(bars_low)], axis=1),
        ],
        axis=0,
    )
    both = matmul(bars, columns[...], rows_by_cols)
    target = held_flows[0] if order else flows
    target[...] = both[:horizon] + both[horizon:] - base_flow[...]
    if order:
        width = flows.shape[1] // len(order)
        own_far = lax.axis_index("bus") // QUAD
        for at, r in enumerate(order):
            first = pl.multiple_of((own_far ^ r) * width, width)
            flows[:, at * width : (at + 1) * width] = target[:, pl.ds(first, width)]
    energy = start_energy + efficiency * interval * running_sum(charge_bar, False)
    new_state[:horizon, :] = gen_step
    new_state[horizon : 2 * horizon, :] = charge_step
    new_state[2 * horizon : 3 * horizon, :] = clip_dual(
        duals + energy_step * energy, energy_step, 0.0, energy_limit
    )
    new_state[3 * horizon :, :] = state[3 * horizon :, :]


def step_units(prices_a, prices_b, state, bounds, columns, base_flow, order=()):
    return pl.pallas_call(
        functools.partial(unit_kernel, order=order),
        in_specs=[whole_block] * 6,
        out_specs=[whole_block] * 2,
        out_shape=[near_array(state.shape), near_array(base_flow.shape)],
        scratch_shapes=[pltpu.VMEM(base_flow.shape, jnp.float32)] if order else [],
        compiler_params=grant,
        name="step_units",
    )(*[near(a) for a in (prices_a, prices_b, state, bounds, columns, base_flow)])


def moved_dual(dual, limit, flows):
    return clip_dual(dual + dual_step * flows, dual_step, -limit, limit)


def line_kernel(lines, flows_a, flows_b, columns, new_lines, prices):
    horizon = flows_a.shape[0]
    limit = lines[horizon:, :]
    dual = moved_dual(lines[:horizon, :], limit, flows_a[...] + flows_b[...])
    new_lines[:horizon, :] = dual
    new_lines[horizon:, :] = limit
    prices[...] = local_prices(dual, columns[...])


def step_lines(lines, flows_a, flows_b, columns):
    return pl.pallas_call(
        line_kernel,
        in_specs=[whole_block] * 4,
        out_specs=[whole_block] * 2,
        out_shape=[
            near_array(lines.shape),
            near_array((flows_a.shape[0], columns.shape[0] // 2)),
        ],
        compiler_params=grant,
        name="step_lines",
    )(*[near(a) for a in (lines, flows_a, flows_b, columns)])


def on_device(
    generation,
    charging,
    flow_dual,
    energy_dual,
    shift_factors,
    load_units,
    generator_bus,
    storage_bus,
    generator_cost,
    generator_max,
    charging_max,
    energy_init,
    energy_max,
    line_max,
    *,
    count,
):
    own_lines, horizon = flow_dual.shape
    own_units = storage_bus.shape[0]
    far = count // QUAD
    own = lax.axis_index("bus")
    member = own % QUAD
    place_of_quad = own // QUAD
    far_bits = [bit for bit in (1 << k for k in range(2, 30)) if bit < count]

    def exchange(values, bit):
        return lax.ppermute(values, "bus", [(i, i ^ bit) for i in range(count)])

    def half_sum(values, bits):
        for bit in bits[:-1]:
            values = values + exchange(values, bit)
        return values, exchange(values, bits[-1])

    scan = functools.partial(
        scan_factors,
        generator_bus[None, :],
        storage_bus[None, :],
        load_units.T,
        shift_factors,
        own_lines=own_lines,
        far=far,
    )
    units = 2 * own_units
    for_diagonal, demand_3 = scan(generator_bus[None, :], wanted=(3,))
    from_diagonal = exchange(for_diagonal, 3)
    state, lines = place(
        generation.T,
        charging,
        energy_dual,
        generator_cost[None, :],
        generator_max[None, :],
        flow_dual.T,
        line_max[None, :],
        far,
    )
    for bit in far_bits:
        lines = lines + exchange(lines, bit)
    for_y, demand_2 = scan(for_diagonal, wanted=(2,))
    from_y = exchange(for_y, 2)
    rest, demand_1_0 = scan(for_y, wanted=(0, 1))
    from_core = exchange(jnp.concatenate([rest[units:], demand_1_0[horizon:], demand_3], axis=0), 1)
    demand_own = demand_1_0[:horizon] + from_core[units : units + horizon]
    demand_other = demand_2 + from_core[units + horizon :]
    base_flow = demand_own + exchange(demand_other, 2)
    state = sum(half_sum(state, (1, 2)))
    bounds = lax.dynamic_slice_in_dim(
        jnp.stack([charging_max, energy_init, energy_max]),
        place_of_quad * QUAD * own_units,
        QUAD * own_units,
        axis=1,
    )

    columns, prices = gather_columns((rest, from_core, from_y, from_diagonal), lines, horizon)
    for _ in range(ITERS - 1):
        state, flows = step_units(*half_sum(prices, (1, 2)), state, bounds, columns, base_flow)
        lines, prices = step_lines(lines, *half_sum(flows, far_bits), columns)
    mine = lambda a: lax.dynamic_slice_in_dim(a, place_of_quad * own_lines, own_lines, axis=1)
    if own_lines % 128 == 0:
        steps = len(far_bits)
        order = tuple(
            sum(((at >> k) & 1) << (steps - 1 - k) for k in range(steps)) for at in range(far)
        )
    else:
        order = ()
    state, flows = step_units(*half_sum(prices, (1, 2)), state, bounds, columns, base_flow, order)
    if order:
        for bit in far_bits:
            half = flows.shape[1] // 2
            flows = flows[:, :half] + exchange(flows[:, half:], bit)
    else:
        flows = mine(sum(half_sum(flows, far_bits)))
    own_dual = moved_dual(mine(lines[:horizon]), mine(lines[horizon:]), flows)
    ends = lax.dynamic_slice_in_dim(state, member * own_units, own_units, axis=1)
    return (
        ends[:horizon].T,
        ends[horizon : 2 * horizon],
        own_dual.T,
        ends[2 * horizon : 3 * horizon],
    )


def solution(mesh):
    placed = (
        P("bus", "groups"),
        P("groups", "bus"),
        P("bus", "groups"),
        P("groups", "bus"),
        P(None, "bus"),
        P("bus", "groups"),
        P("bus"),
        P("bus"),
        P("bus"),
        P("bus"),
        P(),
        P(),
        P(),
        P("bus"),
    )
    count = mesh.shape["bus"]

    def body(*args):
        return on_device(*args, count=count)

    return jax.shard_map(
        body,
        mesh=mesh,
        in_specs=placed,
        out_specs=(P("bus", "groups"), P("groups", "bus"), P("bus", "groups"), P("groups", "bus")),
        check_vma=False,
    )
```

profile of v0, /device:TPU:0, one launch (start us, length us, event | category | flops | bytes accessed | tf_op | source)
XLA Modules:
  0.0 75.9 jit_solution(1126828418633826889)
XLA Ops:
  0.6 3.2 %scan_factors.3 = (f32[64,1024]{1,0:T(8,128)S(1)}, f32[16,1024]{1,0:T(8,128)S(1)}) custom-call(s32[1,32]{1,0:T(1,128)} %bitcast.25, s32[1,32]{1,0:T(1,128)} %bitcast.29, s32[16,1024]{1,0:T(8,128)} %bitcast.22, f32[4096,1024]{1,0:T(8,128)} %factors.5, s32[1,32]{1,0:T(1,128)} %bitcast.26), custom_call_target="tpu_custom_call" | custom-call | tf_op jit(solution)/shard_map/scan_factors/pallas_call | solution.py:133
  3.9 0.0 copy-start.1
  4.0 3.3 %scan_factors.4 = (f32[64,1024]{1,0:T(8,128)S(1)}, f32[16,1024]{1,0:T(8,128)S(1)}) custom-call(s32[1,32]{1,0:T(1,128)} %bitcast.27, s32[1,32]{1,0:T(1,128)} %bitcast.30, s32[16,1024]{1,0:T(8,128)} %bitcast.23, f32[4096,1024]{1,0:T(8,128)} %factors.5, f32[64,1024]{1,0:T(8,128)S(1)} %get-tuple-element.25.after), custom_call_target="tpu_custom_call" | custom-call | tf_op jit(solution)/shard_map/scan_factors/pallas_call | solution.py:133
  7.2 6.4 %scan_factors.5 = (f32[128,1024]{1,0:T(8,128)S(1)}, f32[32,1024]{1,0:T(8,128)S(1)}) custom-call(s32[1,32]{1,0:T(1,128)} %bitcast.28, s32[1,32]{1,0:T(1,128)} %bitcast.31, s32[16,1024]{1,0:T(8,128)} %bitcast.24, f32[4096,1024]{1,0:T(8,128)} %factors.5, f32[64,1024]{1,0:T(8,128)S(1)} %get-tuple-element.26.after), custom_call_target="tpu_custom_call" | custom-call | tf_op jit(solution)/shard_map/scan_factors/pallas_call | solution.py:133
  13.8 0.6 collective-permute-start.2
  14.3 2.6 %collective-permute-start.3 = (f32[64,1024]{1,0:T(8,128)S(1)}, f32[64,1024]{1,0:T(8,128)S(1)}, u32[]{:S(2)}, u32[]{:S(2)}) collective-permute-start(f32[64,1024]{1,0:T(8,128)S(1)} %get-tuple-element.26.after), channel_id=1, source_target_pairs={{0,2},{1,3},{2,0},{3,1},{4,6},{5,7},{6,4},{7,5},{8,10},{9,11},{10,... | collective-permute-start | bytes 786440 | tf_op jit(solution)/shard_map/ppermute | solution.py:334
  16.9 0.0 collective-permute-start.4
  17.0 0.1 place.1
  17.1 1.9 %collective-permute-start = (f32[17,1024]{1,0:T(8,128)S(1)}, f32[17,1024]{1,0:T(8,128)S(1)}, u32[]{:S(2)}, u32[]{:S(2)}) collective-permute-start(f32[17,1024]{1,0:T(8,128)S(1)} %get-tuple-element.24), channel_id=1, source_target_pairs={{0,4},{1,5},{2,6},{3,7},{4,0},{5,1},{6,2},{7,3},{8,12},{9,13},{10,... | collective-permute-start | bytes 208904 | tf_op jit(solution)/shard_map/ppermute | solution.py:334
  19.0 3.3 %collective-permute-done = f32[17,1024]{1,0:T(8,128)S(1)} collective-permute-done((f32[17,1024]{1,0:T(8,128)S(1)}, f32[17,1024]{1,0:T(8,128)S(1)}, u32[]{:S(2)}, u32[]{:S(2)}) %collective-permute-start) | collective-permute-done | bytes 69664 | tf_op jit(solution)/shard_map/ppermute | solution.py:334
  22.3 2.8 %collective-permute-start.1 = (f32[17,1024]{1,0:T(8,128)S(1)}, f32[17,1024]{1,0:T(8,128)S(1)}, u32[]{:S(2)}, u32[]{:S(2)}) collective-permute-start(f32[17,1024]{1,0:T(8,128)S(1)} %add.60), channel_id=1, source_target_pairs={{0,8},{1,9},{2,10},{3,11},{4,12},{5,13},{6,14},{7,15},{8,0},{9,1},... | collective-permute-start | bytes 208904 | tf_op jit(solution)/shard_map/ppermute | solution.py:334
  25.1 1.2 %collective-permute-done.7 = f32[50,128]{1,0:T(8,128)S(1)} collective-permute-done((f32[50,128]{1,0:T(8,128)S(1)}, f32[50,128]{1,0:T(8,128)S(1)}, u32[]{:S(2)}, u32[]{:S(2)}) %collective-permute-start.7) | collective-permute-done | bytes 25632 | tf_op jit(solution)/shard_map/ppermute | solution.py:334
  26.3 1.5 %collective-permute-start.8 = (f32[50,128]{1,0:T(8,128)S(1)}, f32[50,128]{1,0:T(8,128)S(1)}, u32[]{:S(2)}, u32[]{:S(2)}) collective-permute-start(f32[50,128]{1,0:T(8,128)S(1)} %add.63), channel_id=1, source_target_pairs={{0,2},{1,3},{2,0},{3,1},{4,6},{5,7},{6,4},{7,5},{8,10},{9,11},{10,... | collective-permute-start | bytes 76808 | tf_op jit(solution)/shard_map/ppermute | solution.py:334
  27.8 1.8 %collective-permute-done.1 = f32[17,1024]{1,0:T(8,128)S(1)} collective-permute-done((f32[17,1024]{1,0:T(8,128)S(1)}, f32[17,1024]{1,0:T(8,128)S(1)}, u32[]{:S(2)}, u32[]{:S(2)}) %collective-permute-start.1) | collective-permute-done | bytes 69664 | tf_op jit(solution)/shard_map/ppermute | solution.py:334
  29.7 0.6 gather_columns.1
  30.3 0.1 collective-permute-start.5
  30.5 1.6 %collective-permute-start.9 = (f32[16,1024]{1,0:T(8,128)S(1)}, f32[16,1024]{1,0:T(8,128)S(1)}, u32[]{:S(2)}, u32[]{:S(2)}) collective-permute-start(f32[16,1024]{1,0:T(8,128)S(1)} %slice_add_fusion), channel_id=1, source_target_pairs={{0,2},{1,3},{2,0},{3,1},{4,6},{5,7},{6,4},{7,5},{8,10},{9,11},{10,... | collective-permute-start | bytes 196616 | tf_op jit(solution)/shard_map/ppermute | solution.py:334
  32.1 0.1 fusion.4.bounds
  32.2 0.9 %collective-permute-start.6 = (f32[16,256]{1,0:T(8,128)S(1)}, f32[16,256]{1,0:T(8,128)S(1)}, u32[]{:S(2)}, u32[]{:S(2)}) collective-permute-start(f32[16,256]{1,0:T(8,128)S(1)} %add.62.prices_a), channel_id=1, source_target_pairs={{0,2},{1,3},{2,0},{3,1},{4,6},{5,7},{6,4},{7,5},{8,10},{9,11},{10,... | collective-permute-start | bytes 49160 | tf_op jit(solution)/shard_map/ppermute | solution.py:334
  33.1 1.8 %collective-permute-done.9 = f32[16,1024]{1,0:T(8,128)S(1)} collective-permute-done((f32[16,1024]{1,0:T(8,128)S(1)}, f32[16,1024]{1,0:T(8,128)S(1)}, u32[]{:S(2)}, u32[]{:S(2)}) %collective-permute-start.9) | collective-permute-done | bytes 65568 | tf_op jit(solution)/shard_map/ppermute | solution.py:334
  35.0 1.0 %collective-permute-done.6.prices_b = f32[16,256]{1,0:T(8,128)S(1)} collective-permute-done((f32[16,256]{1,0:T(8,128)S(1)}, f32[16,256]{1,0:T(8,128)S(1)}, u32[]{:S(2)}, u32[]{:S(2)}) %collective-permute-start.6) | collective-permute-done | bytes 16416 | tf_op jit(solution)/shard_map/ppermute | solution.py:334
  36.0 0.3 step_units.3
  36.3 1.5 %collective-permute-start.10 = (f32[16,1024]{1,0:T(8,128)S(1)}, f32[16,1024]{1,0:T(8,128)S(1)}, u32[]{:S(2)}, u32[]{:S(2)}) collective-permute-start(f32[16,1024]{1,0:T(8,128)S(1)} %get-tuple-element.34), channel_id=1, source_target_pairs={{0,4},{1,5},{2,6},{3,7},{4,0},{5,1},{6,2},{7,3},{8,12},{9,13},{10,... | collective-permute-start | bytes 196616 | tf_op jit(solution)/shard_map/ppermute | solution.py:334
  37.8 2.8 %collective-permute-done.10 = f32[16,1024]{1,0:T(8,128)S(1)} collective-permute-done((f32[16,1024]{1,0:T(8,128)S(1)}, f32[16,1024]{1,0:T(8,128)S(1)}, u32[]{:S(2)}, u32[]{:S(2)}) %collective-permute-start.10) | collective-permute-done | bytes 65568 | tf_op jit(solution)/shard_map/ppermute | solution.py:334
  40.6 2.6 %collective-permute-start.11 = (f32[16,1024]{1,0:T(8,128)S(1)}, f32[16,1024]{1,0:T(8,128)S(1)}, u32[]{:S(2)}, u32[]{:S(2)}) collective-permute-start(f32[16,1024]{1,0:T(8,128)S(1)} %add.69.flows_a), channel_id=1, source_target_pairs={{0,8},{1,9},{2,10},{3,11},{4,12},{5,13},{6,14},{7,15},{8,0},{9,1},... | collective-permute-start | bytes 196616 | tf_op jit(solution)/shard_map/ppermute | solution.py:334
  43.2 2.6 %collective-permute-done.11.flows_b = f32[16,1024]{1,0:T(8,128)S(1)} collective-permute-done((f32[16,1024]{1,0:T(8,128)S(1)}, f32[16,1024]{1,0:T(8,128)S(1)}, u32[]{:S(2)}, u32[]{:S(2)}) %collective-permute-start.11) | collective-permute-done | bytes 65568 | tf_op jit(solution)/shard_map/ppermute | solution.py:334
  45.8 0.4 step_lines.2
  46.2 0.1 collective-permute-start.12
  46.2 1.2 %collective-permute-done.12 = f32[16,256]{1,0:T(8,128)S(1)} collective-permute-done((f32[16,256]{1,0:T(8,128)S(1)}, f32[16,256]{1,0:T(8,128)S(1)}, u32[]{:S(2)}, u32[]{:S(2)}) %collective-permute-start.12) | collective-permute-done | bytes 16416 | tf_op jit(solution)/shard_map/ppermute | solution.py:334
  47.4 0.9 %collective-permute-start.13 = (f32[16,256]{1,0:T(8,128)S(1)}, f32[16,256]{1,0:T(8,128)S(1)}, u32[]{:S(2)}, u32[]{:S(2)}) collective-permute-start(f32[16,256]{1,0:T(8,128)S(1)} %add.70.prices_a), channel_id=1, source_target_pairs={{0,2},{1,3},{2,0},{3,1},{4,6},{5,7},{6,4},{7,5},{8,10},{9,11},{10,... | collective-permute-start | bytes 49160 | tf_op jit(solution)/shard_map/ppermute | solution.py:334
  48.3 2.9 %collective-permute-done.13.prices_b = f32[16,256]{1,0:T(8,128)S(1)} collective-permute-done((f32[16,256]{1,0:T(8,128)S(1)}, f32[16,256]{1,0:T(8,128)S(1)}, u32[]{:S(2)}, u32[]{:S(2)}) %collective-permute-start.13) | collective-permute-done | bytes 16416 | tf_op jit(solution)/shard_map/ppermute | solution.py:334
  51.2 0.3 step_units.4
  51.4 1.5 %collective-permute-start.14 = (f32[16,1024]{1,0:T(8,128)S(1)}, f32[16,1024]{1,0:T(8,128)S(1)}, u32[]{:S(2)}, u32[]{:S(2)}) collective-permute-start(f32[16,1024]{1,0:T(8,128)S(1)} %get-tuple-element.38), channel_id=1, source_target_pairs={{0,4},{1,5},{2,6},{3,7},{4,0},{5,1},{6,2},{7,3},{8,12},{9,13},{10,... | collective-permute-start | bytes 196616 | tf_op jit(solution)/shard_map/ppermute | solution.py:334
  53.0 2.8 %collective-permute-done.14 = f32[16,1024]{1,0:T(8,128)S(1)} collective-permute-done((f32[16,1024]{1,0:T(8,128)S(1)}, f32[16,1024]{1,0:T(8,128)S(1)}, u32[]{:S(2)}, u32[]{:S(2)}) %collective-permute-start.14) | collective-permute-done | bytes 65568 | tf_op jit(solution)/shard_map/ppermute | solution.py:334
  55.7 2.7 %collective-permute-start.15 = (f32[16,1024]{1,0:T(8,128)S(1)}, f32[16,1024]{1,0:T(8,128)S(1)}, u32[]{:S(2)}, u32[]{:S(2)}) collective-permute-start(f32[16,1024]{1,0:T(8,128)S(1)} %add.71.flows_a), channel_id=1, source_target_pairs={{0,8},{1,9},{2,10},{3,11},{4,12},{5,13},{6,14},{7,15},{8,0},{9,1},... | collective-permute-start | bytes 196616 | tf_op jit(solution)/shard_map/ppermute | solution.py:334
  58.5 2.5 %collective-permute-done.15.flows_b = f32[16,1024]{1,0:T(8,128)S(1)} collective-permute-done((f32[16,1024]{1,0:T(8,128)S(1)}, f32[16,1024]{1,0:T(8,128)S(1)}, u32[]{:S(2)}, u32[]{:S(2)}) %collective-permute-start.15) | collective-permute-done | bytes 65568 | tf_op jit(solution)/shard_map/ppermute | solution.py:334
  61.0 0.4 step_lines.3
  61.3 0.1 collective-permute-start.16
  61.4 1.2 %collective-permute-done.16 = f32[16,256]{1,0:T(8,128)S(1)} collective-permute-done((f32[16,256]{1,0:T(8,128)S(1)}, f32[16,256]{1,0:T(8,128)S(1)}, u32[]{:S(2)}, u32[]{:S(2)}) %collective-permute-start.16) | collective-permute-done | bytes 16416 | tf_op jit(solution)/shard_map/ppermute | solution.py:334
  62.6 0.9 %collective-permute-start.17 = (f32[16,256]{1,0:T(8,128)S(1)}, f32[16,256]{1,0:T(8,128)S(1)}, u32[]{:S(2)}, u32[]{:S(2)}) collective-permute-start(f32[16,256]{1,0:T(8,128)S(1)} %add.72.prices_a), channel_id=1, source_target_pairs={{0,2},{1,3},{2,0},{3,1},{4,6},{5,7},{6,4},{7,5},{8,10},{9,11},{10,... | collective-permute-start | bytes 49160 | tf_op jit(solution)/shard_map/ppermute | solution.py:334
  63.4 2.9 %collective-permute-done.17.prices_b = f32[16,256]{1,0:T(8,128)S(1)} collective-permute-done((f32[16,256]{1,0:T(8,128)S(1)}, f32[16,256]{1,0:T(8,128)S(1)}, u32[]{:S(2)}, u32[]{:S(2)}) %collective-permute-start.17) | collective-permute-done | bytes 16416 | tf_op jit(solution)/shard_map/ppermute | solution.py:334
  66.3 0.3 step_units.5
  66.6 1.8 %collective-permute-start.18 = (f32[16,512]{1,0:T(8,128)S(1)}, f32[16,512]{1,0:T(8,128)S(1)}, u32[]{:S(2)}, u32[]{:S(2)}) collective-permute-start(f32[16,512]{1,0:T(8,128)S(1)} %slice.51), channel_id=1, source_target_pairs={{0,4},{1,5},{2,6},{3,7},{4,0},{5,1},{6,2},{7,3},{8,12},{9,13},{10,... | collective-permute-start | bytes 98312 | tf_op jit(solution)/shard_map/ppermute | solution.py:334
  68.5 2.1 %collective-permute-done.18 = f32[16,512]{1,0:T(8,128)S(1)} collective-permute-done((f32[16,512]{1,0:T(8,128)S(1)}, f32[16,512]{1,0:T(8,128)S(1)}, u32[]{:S(2)}, u32[]{:S(2)}) %collective-permute-start.18) | collective-permute-done | bytes 32800 | tf_op jit(solution)/shard_map/ppermute | solution.py:334
  70.6 2.9 %collective-permute-start.19 = (f32[16,256]{1,0:T(8,128)S(1)}, f32[16,256]{1,0:T(8,128)S(1)}, u32[]{:S(2)}, u32[]{:S(2)}) collective-permute-start(f32[16,256]{1,0:T(8,128)S(1)} %slice.59), channel_id=1, source_target_pairs={{0,8},{1,9},{2,10},{3,11},{4,12},{5,13},{6,14},{7,15},{8,0},{9,1},... | collective-permute-start | bytes 49160 | tf_op jit(solution)/shard_map/ppermute | solution.py:334
  73.5 0.7 fusion.6
  74.2 1.1 %collective-permute-done.19 = f32[16,256]{1,0:T(8,128)S(1)} collective-permute-done((f32[16,256]{1,0:T(8,128)S(1)}, f32[16,256]{1,0:T(8,128)S(1)}, u32[]{:S(2)}, u32[]{:S(2)}) %collective-permute-start.19) | collective-permute-done | bytes 16416 | tf_op jit(solution)/shard_map/ppermute | solution.py:334
  75.3 0.6 subtract_bitcast_fusion
  (45 shorter events, 0.3 us)
Async XLA Ops:
  3.9 13.1 %copy-start = (f32[256,16]{0,1:T(8,128)S(1)}, f32[256,16]{0,1:T(8,128)}, u32[]{:S(2)}) copy-start(f32[256,16]{0,1:T(8,128)} %param.16) | copy-start | bytes 49156
  3.9 13.1 %copy-start.1 = (f32[32,16]{0,1:T(8,128)S(1)}, f32[32,16]{0,1:T(8,128)}, u32[]{:S(2)}) copy-start(f32[32,16]{0,1:T(8,128)} %param.14) | copy-start | bytes 6148
  3.9 13.1 %copy-start.2 = (f32[16,32]{1,0:T(8,128)S(1)}, f32[16,32]{1,0:T(8,128)}, u32[]{:S(2)}) copy-start(f32[16,32]{1,0:T(8,128)} %charging.1) | copy-start | bytes 6148
  3.9 13.1 %copy-start.3 = (f32[16,32]{1,0:T(8,128)S(1)}, f32[16,32]{1,0:T(8,128)}, u32[]{:S(2)}) copy-start(f32[16,32]{1,0:T(8,128)} %energy_dual.1) | copy-start | bytes 6148
  3.9 13.1 %copy-start.4 = (f32[256]{0:T(256)S(1)}, f32[256]{0:T(256)}, u32[]{:S(2)}) copy-start(f32[256]{0:T(256)} %param.27) | copy-start | bytes 3076
  3.9 13.1 %copy-start.5 = (f32[32]{0:T(128)S(1)}, f32[32]{0:T(128)}, u32[]{:S(2)}) copy-start(f32[32]{0:T(128)} %param.22) | copy-start | bytes 388
  3.9 13.1 %copy-start.6 = (f32[32]{0:T(128)S(1)}, f32[32]{0:T(128)}, u32[]{:S(2)}) copy-start(f32[32]{0:T(128)} %param.23) | copy-start | bytes 388
  3.9 28.1 %copy-start.7 = (f32[512]{0:T(512)S(1)}, f32[512]{0:T(512)}, u32[]{:S(2)}) copy-start(f32[512]{0:T(512)} %param.24) | copy-start | bytes 6148
  4.0 28.1 %copy-start.8 = (f32[512]{0:T(512)S(1)}, f32[512]{0:T(512)}, u32[]{:S(2)}) copy-start(f32[512]{0:T(512)} %param.25) | copy-start | bytes 6148
  4.0 28.1 %copy-start.9 = (f32[512]{0:T(512)S(1)}, f32[512]{0:T(512)}, u32[]{:S(2)}) copy-start(f32[512]{0:T(512)} %param.26) | copy-start | bytes 6148
  13.8 16.0 %collective-permute-start.2 = (f32[96,1024]{1,0:T(8,128)S(1)}, f32[96,1024]{1,0:T(8,128)S(1)}, u32[]{:S(2)}, u32[]{:S(2)}) collective-permute-start(f32[96,1024]{1,0:T(8,128)S(1)} %pad_maximum_fusion), channel_id=1, source_target_pairs={{0,1},{1,0},{2,3},{3,2},{4,5},{5,4},{6,7},{7,6},{8,9},{9,8},{10,11... | collective-permute-start | bytes 1179656 | tf_op jit(solution)/shard_map/ppermute | solution.py:334
  14.3 15.4 %collective-permute-start.3 = (f32[64,1024]{1,0:T(8,128)S(1)}, f32[64,1024]{1,0:T(8,128)S(1)}, u32[]{:S(2)}, u32[]{:S(2)}) collective-permute-start(f32[64,1024]{1,0:T(8,128)S(1)} %get-tuple-element.26.after), channel_id=1, source_target_pairs={{0,2},{1,3},{2,0},{3,1},{4,6},{5,7},{6,4},{7,5},{8,10},{9,11},{10,... | collective-permute-start | bytes 786440 | tf_op jit(solution)/shard_map/ppermute | solution.py:334
  16.9 12.8 %collective-permute-start.4 = (f32[64,1024]{1,0:T(8,128)S(1)}, f32[64,1024]{1,0:T(8,128)S(1)}, u32[]{:S(2)}, u32[]{:S(2)}) collective-permute-start(f32[64,1024]{1,0:T(8,128)S(1)} %get-tuple-element.25.after), channel_id=1, source_target_pairs={{0,3},{1,2},{2,1},{3,0},{4,7},{5,6},{6,5},{7,4},{8,11},{9,10},{10,... | collective-permute-start | bytes 786440 | tf_op jit(solution)/shard_map/ppermute | solution.py:334
  17.1 5.2 %collective-permute-start = (f32[17,1024]{1,0:T(8,128)S(1)}, f32[17,1024]{1,0:T(8,128)S(1)}, u32[]{:S(2)}, u32[]{:S(2)}) collective-permute-start(f32[17,1024]{1,0:T(8,128)S(1)} %get-tuple-element.24), channel_id=1, source_target_pairs={{0,4},{1,5},{2,6},{3,7},{4,0},{5,1},{6,2},{7,3},{8,12},{9,13},{10,... | collective-permute-start | bytes 208904 | tf_op jit(solution)/shard_map/ppermute | solution.py:334
  22.3 7.4 %collective-permute-start.1 = (f32[17,1024]{1,0:T(8,128)S(1)}, f32[17,1024]{1,0:T(8,128)S(1)}, u32[]{:S(2)}, u32[]{:S(2)}) collective-permute-start(f32[17,1024]{1,0:T(8,128)S(1)} %add.60), channel_id=1, source_target_pairs={{0,8},{1,9},{2,10},{3,11},{4,12},{5,13},{6,14},{7,15},{8,0},{9,1},... | collective-permute-start | bytes 208904 | tf_op jit(solution)/shard_map/ppermute | solution.py:334
  25.1 1.2 %collective-permute-start.7 = (f32[50,128]{1,0:T(8,128)S(1)}, f32[50,128]{1,0:T(8,128)S(1)}, u32[]{:S(2)}, u32[]{:S(2)}) collective-permute-start(f32[50,128]{1,0:T(8,128)S(1)} %get-tuple-element.31), channel_id=1, source_target_pairs={{0,1},{1,0},{2,3},{3,2},{4,5},{5,4},{6,7},{7,6},{8,9},{9,8},{10,11... | collective-permute-start | bytes 76808 | tf_op jit(solution)/shard_map/ppermute | solution.py:334
  26.3 5.9 %collective-permute-start.8 = (f32[50,128]{1,0:T(8,128)S(1)}, f32[50,128]{1,0:T(8,128)S(1)}, u32[]{:S(2)}, u32[]{:S(2)}) collective-permute-start(f32[50,128]{1,0:T(8,128)S(1)} %add.63), channel_id=1, source_target_pairs={{0,2},{1,3},{2,0},{3,1},{4,6},{5,7},{6,4},{7,5},{8,10},{9,11},{10,... | collective-permute-start | bytes 76808 | tf_op jit(solution)/shard_map/ppermute | solution.py:334
  30.3 1.9 %collective-permute-start.5 = (f32[16,256]{1,0:T(8,128)S(1)}, f32[16,256]{1,0:T(8,128)S(1)}, u32[]{:S(2)}, u32[]{:S(2)}) collective-permute-start(f32[16,256]{1,0:T(8,128)S(1)} %get-tuple-element.30), channel_id=1, source_target_pairs={{0,1},{1,0},{2,3},{3,2},{4,5},{5,4},{6,7},{7,6},{8,9},{9,8},{10,11... | collective-permute-start | bytes 49160 | tf_op jit(solution)/shard_map/ppermute | solution.py:334
  30.5 4.5 %collective-permute-start.9 = (f32[16,1024]{1,0:T(8,128)S(1)}, f32[16,1024]{1,0:T(8,128)S(1)}, u32[]{:S(2)}, u32[]{:S(2)}) collective-permute-start(f32[16,1024]{1,0:T(8,128)S(1)} %slice_add_fusion), channel_id=1, source_target_pairs={{0,2},{1,3},{2,0},{3,1},{4,6},{5,7},{6,4},{7,5},{8,10},{9,11},{10,... | collective-permute-start | bytes 196616 | tf_op jit(solution)/shard_map/ppermute | solution.py:334
  32.2 3.8 %collective-permute-start.6 = (f32[16,256]{1,0:T(8,128)S(1)}, f32[16,256]{1,0:T(8,128)S(1)}, u32[]{:S(2)}, u32[]{:S(2)}) collective-permute-start(f32[16,256]{1,0:T(8,128)S(1)} %add.62.prices_a), channel_id=1, source_target_pairs={{0,2},{1,3},{2,0},{3,1},{4,6},{5,7},{6,4},{7,5},{8,10},{9,11},{10,... | collective-permute-start | bytes 49160 | tf_op jit(solution)/shard_map/ppermute | solution.py:334
  36.3 4.3 %collective-permute-start.10 = (f32[16,1024]{1,0:T(8,128)S(1)}, f32[16,1024]{1,0:T(8,128)S(1)}, u32[]{:S(2)}, u32[]{:S(2)}) collective-permute-start(f32[16,1024]{1,0:T(8,128)S(1)} %get-tuple-element.34), channel_id=1, source_target_pairs={{0,4},{1,5},{2,6},{3,7},{4,0},{5,1},{6,2},{7,3},{8,12},{9,13},{10,... | collective-permute-start | bytes 196616 | tf_op jit(solution)/shard_map/ppermute | solution.py:334
  40.6 5.2 %collective-permute-start.11 = (f32[16,1024]{1,0:T(8,128)S(1)}, f32[16,1024]{1,0:T(8,128)S(1)}, u32[]{:S(2)}, u32[]{:S(2)}) collective-permute-start(f32[16,1024]{1,0:T(8,128)S(1)} %add.69.flows_a), channel_id=1, source_target_pairs={{0,8},{1,9},{2,10},{3,11},{4,12},{5,13},{6,14},{7,15},{8,0},{9,1},... | collective-permute-start | bytes 196616 | tf_op jit(solution)/shard_map/ppermute | solution.py:334
  46.2 1.2 %collective-permute-start.12 = (f32[16,256]{1,0:T(8,128)S(1)}, f32[16,256]{1,0:T(8,128)S(1)}, u32[]{:S(2)}, u32[]{:S(2)}) collective-permute-start(f32[16,256]{1,0:T(8,128)S(1)} %get-tuple-element.36), channel_id=1, source_target_pairs={{0,1},{1,0},{2,3},{3,2},{4,5},{5,4},{6,7},{7,6},{8,9},{9,8},{10,11... | collective-permute-start | bytes 49160 | tf_op jit(solution)/shard_map/ppermute | solution.py:334
  47.4 3.7 %collective-permute-start.13 = (f32[16,256]{1,0:T(8,128)S(1)}, f32[16,256]{1,0:T(8,128)S(1)}, u32[]{:S(2)}, u32[]{:S(2)}) collective-permute-start(f32[16,256]{1,0:T(8,128)S(1)} %add.70.prices_a), channel_id=1, source_target_pairs={{0,2},{1,3},{2,0},{3,1},{4,6},{5,7},{6,4},{7,5},{8,10},{9,11},{10,... | collective-permute-start | bytes 49160 | tf_op jit(solution)/shard_map/ppermute | solution.py:334
  51.4 4.3 %collective-permute-start.14 = (f32[16,1024]{1,0:T(8,128)S(1)}, f32[16,1024]{1,0:T(8,128)S(1)}, u32[]{:S(2)}, u32[]{:S(2)}) collective-permute-start(f32[16,1024]{1,0:T(8,128)S(1)} %get-tuple-element.38), channel_id=1, source_target_pairs={{0,4},{1,5},{2,6},{3,7},{4,0},{5,1},{6,2},{7,3},{8,12},{9,13},{10,... | collective-permute-start | bytes 196616 | tf_op jit(solution)/shard_map/ppermute | solution.py:334
  55.7 5.2 %collective-permute-start.15 = (f32[16,1024]{1,0:T(8,128)S(1)}, f32[16,1024]{1,0:T(8,128)S(1)}, u32[]{:S(2)}, u32[]{:S(2)}) collective-permute-start(f32[16,1024]{1,0:T(8,128)S(1)} %add.71.flows_a), channel_id=1, source_target_pairs={{0,8},{1,9},{2,10},{3,11},{4,12},{5,13},{6,14},{7,15},{8,0},{9,1},... | collective-permute-start | bytes 196616 | tf_op jit(solution)/shard_map/ppermute | solution.py:334
  61.3 1.2 %collective-permute-start.16 = (f32[16,256]{1,0:T(8,128)S(1)}, f32[16,256]{1,0:T(8,128)S(1)}, u32[]{:S(2)}, u32[]{:S(2)}) collective-permute-start(f32[16,256]{1,0:T(8,128)S(1)} %get-tuple-element.39), channel_id=1, source_target_pairs={{0,1},{1,0},{2,3},{3,2},{4,5},{5,4},{6,7},{7,6},{8,9},{9,8},{10,11... | collective-permute-start | bytes 49160 | tf_op jit(solution)/shard_map/ppermute | solution.py:334
  62.6 3.7 %collective-permute-start.17 = (f32[16,256]{1,0:T(8,128)S(1)}, f32[16,256]{1,0:T(8,128)S(1)}, u32[]{:S(2)}, u32[]{:S(2)}) collective-permute-start(f32[16,256]{1,0:T(8,128)S(1)} %add.72.prices_a), channel_id=1, source_target_pairs={{0,2},{1,3},{2,0},{3,1},{4,6},{5,7},{6,4},{7,5},{8,10},{9,11},{10,... | collective-permute-start | bytes 49160 | tf_op jit(solution)/shard_map/ppermute | solution.py:334
  66.6 4.0 %collective-permute-start.18 = (f32[16,512]{1,0:T(8,128)S(1)}, f32[16,512]{1,0:T(8,128)S(1)}, u32[]{:S(2)}, u32[]{:S(2)}) collective-permute-start(f32[16,512]{1,0:T(8,128)S(1)} %slice.51), channel_id=1, source_target_pairs={{0,4},{1,5},{2,6},{3,7},{4,0},{5,1},{6,2},{7,3},{8,12},{9,13},{10,... | collective-permute-start | bytes 98312 | tf_op jit(solution)/shard_map/ppermute | solution.py:334
  70.6 4.7 %collective-permute-start.19 = (f32[16,256]{1,0:T(8,128)S(1)}, f32[16,256]{1,0:T(8,128)S(1)}, u32[]{:S(2)}, u32[]{:S(2)}) collective-permute-start(f32[16,256]{1,0:T(8,128)S(1)} %slice.59), channel_id=1, source_target_pairs={{0,8},{1,9},{2,10},{3,11},{4,12},{5,13},{6,14},{7,15},{8,0},{9,1},... | collective-permute-start | bytes 49160 | tf_op jit(solution)/shard_map/ppermute | solution.py:334
where the time goes:
time: 76.1 us; the launch traced here: 75.9 us
  waiting for transfers between devices  31.3 us (41%)
  starting transfers between devices  27 us (35%)
  Pallas kernels  15.1 us (20%)
  between operations  0.9 us (1%)
  other arithmetic  0.83 us (1%)
  local copies, waits for them, and re-layouts  0.8 us (1%)
    ppermute x20, waiting for transfers between devices, exchange(): return lax.ppermute(values, 'bus', [(i, i ^ bit) for i in range(count)])  31.3 us
    ppermute x20, starting transfers between devices, exchange(): return lax.ppermute(values, 'bus', [(i, i ^ bit) for i in range(count)])  27 us
    pallas_call x3, Pallas kernels, scan_factors(): pl.pallas_call(functools.partial(scan_kernel, wanted=wanted, own_lines=ow...  12.9 us
  transfers between devices with their start and end apart: 20, of which 15 were waited for; matrix products, arithmetic and copies ran while one was open for 1% of the time, Pallas kernels for 1%

commit v1 on v0

--- a/solution.py
+++ b/solution.py
@@ -72,19 +72,30 @@
     return jnp.sum(jnp.where(across == down, row, 0), axis=1, keepdims=True)
 
 
-def scan_kernel(
-    generator_bus, storage_bus, loads, factors, after, columns, demand,
-    stage, arrived, ids_a, ids_b, counts, small,
-    *, wanted, own_lines, far,
-):
-    buses = factors.shape[1]
+def build_weights(generator_bus, storage_bus, loads, own):
+    buses = loads.shape[1]
+    ids = jnp.concatenate([as_column(generator_bus), as_column(storage_bus)], axis=0)
+    ids = ids - own * buses
+    spots = lax.broadcasted_iota(jnp.int32, (ids.shape[0], buses), 1)
+    picks = (spots == ids).astype(jnp.float32)
+    rows = jnp.concatenate([picks, loads.astype(jnp.float32)], axis=0)
+    return rows.astype(jnp.bfloat16)
+
+
+def scan_kernel(*refs, wanted, own_lines, far, units, first_call):
+    if first_call:
+        generator_bus, storage_bus, loads, factors, columns, demand, weights = refs[:7]
+        stage, arrived, ids_a, ids_b, counts, small = refs[7:]
+    else:
+        weights, factors, _, columns, demand, stage, arrived = refs
     own = lax.axis_index("bus")
     member = own % QUAD
     few = []
-    for index, (source, target) in enumerate(
-        ((generator_bus, ids_a), (storage_bus, ids_b), (loads, counts))
-    ):
-        few.append(pltpu.make_async_copy(source, target, small.at[index]))
+    if first_call:
+        for index, (source, target) in enumerate(
+            ((generator_bus, ids_a), (storage_bus, ids_b), (loads, counts))
+        ):
+            few.append(pltpu.make_async_copy(source, target, small.at[index]))
     copies = []
     for at, r in enumerate(wanted):
         for z in range(far):
@@ -99,15 +110,12 @@
             )
     for copy in few + copies:
         copy.start()
-    for copy in few:
-        copy.wait()
-    ids = jnp.concatenate([as_column(ids_a[...]), as_column(ids_b[...])], axis=0)
-    ids = ids - own * buses
-    spots = lax.broadcasted_iota(jnp.int32, (ids.shape[0], buses), 1)
-    picks = (spots == ids).astype(jnp.float32)
-    weights = jnp.concatenate([picks, counts[...].astype(jnp.float32)], axis=0)
-    weights = weights.astype(jnp.bfloat16)
-    units = ids.shape[0]
+    if first_call:
+        for copy in few:
+            copy.wait()
+        weights[...] = build_weights(ids_a[...], ids_b[...], counts[...], own)
+    rows_wanted = weights[...]
+    horizon = rows_wanted.shape[0] - units
     quarter = far * own_lines
     tile = max(own_lines, min(512, quarter))
     per_tile = tile // own_lines
@@ -115,66 +123,106 @@
         first = t * per_tile
         for copy in copies[first : first + per_tile]:
             copy.wait()
-        rows = stage[pl.ds(first * own_lines, tile), :]
-        high, low = split_halves(rows)
-        found = matmul(weights, high, rows_by_rows) + matmul(weights, low, rows_by_rows)
+        high, low = split_halves(stage[pl.ds(first * own_lines, tile), :])
+        found = matmul(rows_wanted, high, rows_by_rows) + matmul(rows_wanted, low, rows_by_rows)
         at, lane = divmod(t * tile, quarter)
         spot = pl.ds(lane, tile)
         columns[at * units : (at + 1) * units, spot] = found[:units]
-        horizon = loads.shape[0]
         demand[at * horizon : (at + 1) * horizon, spot] = load_unit * found[units:]
 
 
-def scan_factors(generator_bus, storage_bus, loads, factors, after, wanted, own_lines, far):
-    units = generator_bus.shape[1] + storage_bus.shape[1]
+def scan_factors(
+    factors, own_lines, far, units, horizon, wanted, sources=(), weights=None, after=None
+):
     copies = len(wanted) * far
     quarter = far * own_lines
-    arrays = (generator_bus, storage_bus, loads, factors)
+    first_call = weights is None
+    distant = pl.BlockSpec(memory_space=pltpu.HBM)
+    out_shape = [
+        near_array((len(wanted) * units, quarter)),
+        near_array((len(wanted) * horizon, quarter)),
+    ]
+    scratch = [
+        pltpu.VMEM((copies * own_lines, factors.shape[1]), jnp.float32),
+        pltpu.SemaphoreType.DMA((copies,)),
+    ]
+    if first_call:
+        in_specs = [distant] * 4
+        arrays = [far_array(a) for a in (*sources, factors)]
+        out_shape.append(near_array((units + horizon, factors.shape[1]), jnp.bfloat16))
+        scratch += [pltpu.VMEM(a.shape, jnp.int32) for a in sources]
+        scratch.append(pltpu.SemaphoreType.DMA((3,)))
+    else:
+        in_specs = [whole_block, distant, pl.BlockSpec(memory_space=pl.ANY)]
+        arrays = [near(weights), far_array(factors), after]
     return pl.pallas_call(
-        functools.partial(scan_kernel, wanted=wanted, own_lines=own_lines, far=far),
-        in_specs=[pl.BlockSpec(memory_space=pltpu.HBM)] * 4 + [pl.BlockSpec(memory_space=pl.ANY)],
-        out_specs=[whole_block] * 2,
-        out_shape=[
-            near_array((len(wanted) * units, quarter)),
-            near_array((len(wanted) * loads.shape[0], quarter)),
-        ],
-        scratch_shapes=[
-            pltpu.VMEM((copies * own_lines, factors.shape[1]), jnp.float32),
-            pltpu.SemaphoreType.DMA((copies,)),
-            pltpu.VMEM(generator_bus.shape, jnp.int32),
-            pltpu.VMEM(storage_bus.shape, jnp.int32),
-            pltpu.VMEM(loads.shape, jnp.int32),
-            pltpu.SemaphoreType.DMA((3,)),
-        ],
+        functools.partial(
+            scan_kernel,
+            wanted=wanted,
+            own_lines=own_lines,
+            far=far,
+            units=units,
+            first_call=first_call,
+        ),
+        in_specs=in_specs,
+        out_specs=[whole_block] * len(out_shape),
+        out_shape=out_shape,
+        scratch_shapes=scratch,
         compiler_params=grant,
         name="scan_factors",
-    )(*[far_array(a) for a in arrays], after)
+    )(*arrays)
+
+
+def fold(rows, width):
+    pieces = [rows[first : first + 8, :] for first in range(0, rows.shape[0], 8)]
+    per_row = width // rows.shape[1]
+    while len(pieces) % per_row:
+        pieces.append(jnp.zeros_like(pieces[0]))
+    groups = [
+        jnp.concatenate(pieces[first : first + per_row], axis=1)
+        for first in range(0, len(pieces), per_row)
+    ]
+    return jnp.concatenate(groups, axis=0)
+
+
+def unfold(folded, width):
+    return jnp.concatenate(
+        [
+            folded[first : first + 8, lane : lane + width]
+            for first in range(0, folded.shape[0], 8)
+            for lane in range(0, folded.shape[1], width)
+        ],
+        axis=0,
+    )
 
 
 def place_kernel(generation, charging, energy_dual, cost, ceiling, dual, limit, state, lines):
     own = lax.axis_index("bus")
-    rows = jnp.concatenate(
-        [generation[...], charging[...], energy_dual[...], cost[...], ceiling[...]], axis=0
-    )
-    for values, out, slot in ((rows, state, own % QUAD), (None, lines, own // QUAD)):
-        if values is None:
-            values = jnp.concatenate([dual[...], limit[...]], axis=0)
-        width = values.shape[1]
-        repeats = out.shape[1] // width
-        spread = jnp.concatenate([values] * repeats, axis=1)
-        where = lax.broadcasted_iota(jnp.int32, spread.shape, 1) // width
-        out[...] = jnp.where(where == slot, spread, 0.0)
+
+    def spread(values, repeats, slot):
+        wide = jnp.concatenate([values] * repeats, axis=1)
+        where = lax.broadcasted_iota(jnp.int32, wide.shape, 1) // values.shape[1]
+        return jnp.where(where == slot, wide, 0.0)
+
+    rows = [generation[...], charging[...], energy_dual[...], cost[...], ceiling[...]]
+    count = sum(values.shape[0] for values in rows)
+    rows.append(jnp.zeros((-count % 8, generation.shape[1]), jnp.float32))
+    rows = jnp.concatenate(rows, axis=0)
+    state[...] = fold(spread(rows, QUAD, own % QUAD), state.shape[1])
+    own_lines = jnp.concatenate([dual[...], limit[...]], axis=0)
+    lines[...] = spread(own_lines, lines.shape[1] // own_lines.shape[1], own // QUAD)
 
 
 def place(generation, charging, energy_dual, cost, ceiling, dual, limit, far):
     horizon, gens = generation.shape
+    quarter = far * dual.shape[1]
+    pieces = (3 * horizon + 2 + 7) // 8
+    per_row = quarter // (QUAD * gens)
+    groups = (pieces + per_row - 1) // per_row
     return pl.pallas_call(
         place_kernel,
         out_specs=[whole_block] * 2,
-        out_shape=[
-            near_array((3 * horizon + 2, QUAD * gens)),
-            near_array((horizon + 1, far * dual.shape[1])),
-        ],
+        out_shape=[near_array((8 * groups, quarter)), near_array((horizon + 1, quarter))],
         compiler_params=grant,
         name="place",
     )(generation, charging, energy_dual, cost, ceiling, dual, limit)
@@ -224,13 +272,14 @@
     prices_a, prices_b, state, bounds, columns, base_flow, new_state, flows, *held_flows, order
 ):
     horizon = flows.shape[0]
-    gens = state.shape[1]
+    count, gens = new_state.shape
     prices = prices_a[...] + prices_b[...]
-    old = state[:horizon, :]
-    held = state[horizon : 2 * horizon, :]
-    duals = state[2 * horizon : 3 * horizon, :]
-    cost = state[3 * horizon : 3 * horizon + 1, :]
-    ceiling = state[3 * horizon + 1 : 3 * horizon + 2, :]
+    now = state[...] if state.shape == new_state.shape else unfold(state[...], gens)[:count]
+    old = now[:horizon]
+    held = now[horizon : 2 * horizon]
+    duals = now[2 * horizon : 3 * horizon]
+    cost = now[3 * horizon : 3 * horizon + 1]
+    ceiling = now[3 * horizon + 1 : 3 * horizon + 2]
     charge_limit = bounds[0:1, :]
     start_energy = bounds[1:2, :]
     energy_limit = bounds[2:3, :]
@@ -262,7 +311,7 @@
     new_state[2 * horizon : 3 * horizon, :] = clip_dual(
         duals + energy_step * energy, energy_step, 0.0, energy_limit
     )
-    new_state[3 * horizon :, :] = state[3 * horizon :, :]
+    new_state[3 * horizon :, :] = now[3 * horizon :]
 
 
 def step_units(prices_a, prices_b, state, bounds, columns, base_flow, order=()):
@@ -270,7 +319,10 @@
         functools.partial(unit_kernel, order=order),
         in_specs=[whole_block] * 6,
         out_specs=[whole_block] * 2,
-        out_shape=[near_array(state.shape), near_array(base_flow.shape)],
+        out_shape=[
+            near_array((3 * base_flow.shape[0] + 2, prices_a.shape[1] // 2)),
+            near_array(base_flow.shape),
+        ],
         scratch_shapes=[pltpu.VMEM(base_flow.shape, jnp.float32)] if order else [],
         compiler_params=grant,
         name="step_units",
@@ -338,17 +390,13 @@
             values = values + exchange(values, bit)
         return values, exchange(values, bits[-1])
 
+    units = 2 * own_units
     scan = functools.partial(
-        scan_factors,
-        generator_bus[None, :],
-        storage_bus[None, :],
-        load_units.T,
-        shift_factors,
-        own_lines=own_lines,
-        far=far,
-    )
-    units = 2 * own_units
-    for_diagonal, demand_3 = scan(generator_bus[None, :], wanted=(3,))
+        scan_factors, shift_factors, own_lines, far, units, horizon
+    )
+    for_diagonal, demand_3, weights = scan(
+        (3,), sources=(generator_bus[None, :], storage_bus[None, :], load_units.T)
+    )
     from_diagonal = exchange(for_diagonal, 3)
     state, lines = place(
         generation.T,
@@ -362,14 +410,17 @@
     )
     for bit in far_bits:
         lines = lines + exchange(lines, bit)
-    for_y, demand_2 = scan(for_diagonal, wanted=(2,))
+    for_y, demand_2 = scan((2,), weights=weights, after=for_diagonal)
     from_y = exchange(for_y, 2)
-    rest, demand_1_0 = scan(for_y, wanted=(0, 1))
-    from_core = exchange(jnp.concatenate([rest[units:], demand_1_0[horizon:], demand_3], axis=0), 1)
-    demand_own = demand_1_0[:horizon] + from_core[units : units + horizon]
-    demand_other = demand_2 + from_core[units + horizon :]
-    base_flow = demand_own + exchange(demand_other, 2)
-    state = sum(half_sum(state, (1, 2)))
+    rest, demand_1_0 = scan((0, 1), weights=weights, after=for_y)
+    from_core = exchange(
+        jnp.concatenate([rest[units:], demand_1_0[horizon:], demand_3, state], axis=0), 1
+    )
+    kept = demand_1_0[:horizon] + from_core[units : units + horizon]
+    sent = jnp.concatenate([demand_2, state], axis=0) + from_core[units + horizon :]
+    from_y_too = exchange(sent, 2)
+    base_flow = kept + from_y_too[:horizon]
+    state = sent[horizon:] + from_y_too[horizon:]
     bounds = lax.dynamic_slice_in_dim(
         jnp.stack([charging_max, energy_init, energy_max]),
         place_of_quad * QUAD * own_units,

time: 76.1 us -> 75.1 us (0.987)
  waiting for transfers between devices: 31.3 us -> 33.6 us
  Pallas kernels: 15.1 us -> 13.3 us
  starting transfers between devices: 27 us -> 25.5 us
    ppermute x20 -> x18, waiting for transfers between devices: 31.3 us -> 33.6 us  [exchange(): return lax.ppermute(values, 'bus', [(i, i ^ bit) for i in range(count)])]
    pallas_call x3, Pallas kernels: 12.9 us -> 11.1 us  [scan_factors(): pl.pallas_call(functools.partial(scan_kernel, wanted=wanted, own_lines=ow...]
    ppermute x20 -> x18, starting transfers between devices: 27 us -> 25.5 us  [exchange(): return lax.ppermute(values, 'bus', [(i, i ^ bit) for i in range(count)])]
  transfers between devices with their start and end apart: 20 -> 18, of which waited for: 15 -> 14; matrix products, arithmetic and copies ran while one was open for 1% -> 1% of each run, Pallas kernels for 1% -> 0%
where the time goes in v1:
time: 75.1 us; the launch traced here: 75 us
  waiting for transfers between devices  33.6 us (45%)
  starting transfers between devices  25.5 us (34%)
  Pallas kernels  13.3 us (18%)
  between operations  0.92 us (1%)
  other arithmetic  0.82 us (1%)
  local copies, waits for them, and re-layouts  0.8 us (1%)
    ppermute x18, waiting for transfers between devices, exchange(): return lax.ppermute(values, 'bus', [(i, i ^ bit) for i in range(count)])  33.6 us
    ppermute x18, starting transfers between devices, exchange(): return lax.ppermute(values, 'bus', [(i, i ^ bit) for i in range(count)])  25.5 us
    pallas_call x3, Pallas kernels, scan_factors(): pl.pallas_call(functools.partial(scan_kernel, wanted=wanted, own_lines=ow...  11.1 us
  transfers between devices with their start and end apart: 18, of which 14 were waited for; matrix products, arithmetic and copies ran while one was open for 1% of the time, Pallas kernels for 0%

profile of v1, /device:TPU:0, one launch (start us, length us, event | category | flops | bytes accessed | tf_op | source)
XLA Modules:
  0.0 75.0 jit_solution(14003094631173998006)
XLA Ops:
  0.6 3.2 %scan_factors.3 = (f32[64,1024]{1,0:T(8,128)S(1)}, f32[16,1024]{1,0:T(8,128)S(1)}, bf16[80,1024]{1,0:T(8,128)(2,1)S(1)}) custom-call(s32[1,32]{1,0:T(1,128)} %bitcast.28, s32[1,32]{1,0:T(1,128)} %bitcast.29, s32[16,1024]{1,0:T(8,128)} %bitcast.22, f32[4096,1024]{1,0:T(8,128)} %refs_1_.3), custom_call_target="tpu_custom_call" | custom-call | tf_op jit(solution)/shard_map/scan_factors/pallas_call | solution.py:158
  3.9 0.0 copy-start
  3.9 0.0 copy-start.3
  3.9 0.0 copy-start.4
  4.0 3.1 %scan_factors.4 = (f32[64,1024]{1,0:T(8,128)S(1)}, f32[16,1024]{1,0:T(8,128)S(1)}) custom-call(bf16[80,1024]{1,0:T(8,128)(2,1)S(1)} %get-tuple-element.26.refs_0_, f32[4096,1024]{1,0:T(8,128)} %refs_1_.3, f32[64,1024]{1,0:T(8,128)S(1)} %get-tuple-element.27.refs_2_), custom_call_target="tpu_custom_call" | custom-call | tf_op jit(solution)/shard_map/scan_factors/pallas_call | solution.py:158
  7.1 4.7 %scan_factors.5 = (f32[128,1024]{1,0:T(8,128)S(1)}, f32[32,1024]{1,0:T(8,128)S(1)}) custom-call(bf16[80,1024]{1,0:T(8,128)(2,1)S(1)} %get-tuple-element.26.refs_0_, f32[4096,1024]{1,0:T(8,128)} %refs_1_.3, f32[64,1024]{1,0:T(8,128)S(1)} %get-tuple-element.28.refs_2_), custom_call_target="tpu_custom_call" | custom-call | tf_op jit(solution)/shard_map/scan_factors/pallas_call | solution.py:158
  12.0 0.1 place.1
  12.1 0.6 collective-permute-start.2
  12.6 2.6 %collective-permute-start.3 = (f32[64,1024]{1,0:T(8,128)S(1)}, f32[64,1024]{1,0:T(8,128)S(1)}, u32[]{:S(2)}, u32[]{:S(2)}) collective-permute-start(f32[64,1024]{1,0:T(8,128)S(1)} %get-tuple-element.28.refs_2_), channel_id=1, source_target_pairs={{0,2},{1,3},{2,0},{3,1},{4,6},{5,7},{6,4},{7,5},{8,10},{9,11},{10,... | collective-permute-start | bytes 786440 | tf_op jit(solution)/shard_map/ppermute | solution.py:386
  15.2 0.0 collective-permute-start.4
  15.3 1.8 %collective-permute-start = (f32[17,1024]{1,0:T(8,128)S(1)}, f32[17,1024]{1,0:T(8,128)S(1)}, u32[]{:S(2)}, u32[]{:S(2)}) collective-permute-start(f32[17,1024]{1,0:T(8,128)S(1)} %get-tuple-element.25), channel_id=1, source_target_pairs={{0,4},{1,5},{2,6},{3,7},{4,0},{5,1},{6,2},{7,3},{8,12},{9,13},{10,... | collective-permute-start | bytes 208904 | tf_op jit(solution)/shard_map/ppermute | solution.py:386
  17.1 3.3 %collective-permute-done = f32[17,1024]{1,0:T(8,128)S(1)} collective-permute-done((f32[17,1024]{1,0:T(8,128)S(1)}, f32[17,1024]{1,0:T(8,128)S(1)}, u32[]{:S(2)}, u32[]{:S(2)}) %collective-permute-start) | collective-permute-done | bytes 69664 | tf_op jit(solution)/shard_map/ppermute | solution.py:386
  20.4 2.8 %collective-permute-start.1 = (f32[17,1024]{1,0:T(8,128)S(1)}, f32[17,1024]{1,0:T(8,128)S(1)}, u32[]{:S(2)}, u32[]{:S(2)}) collective-permute-start(f32[17,1024]{1,0:T(8,128)S(1)} %add.57), channel_id=1, source_target_pairs={{0,8},{1,9},{2,10},{3,11},{4,12},{5,13},{6,14},{7,15},{8,0},{9,1},... | collective-permute-start | bytes 208904 | tf_op jit(solution)/shard_map/ppermute | solution.py:386
  23.2 4.6 %collective-permute-done.1 = f32[17,1024]{1,0:T(8,128)S(1)} collective-permute-done((f32[17,1024]{1,0:T(8,128)S(1)}, f32[17,1024]{1,0:T(8,128)S(1)}, u32[]{:S(2)}, u32[]{:S(2)}) %collective-permute-start.1) | collective-permute-done | bytes 69664 | tf_op jit(solution)/shard_map/ppermute | solution.py:386
  27.8 0.6 gather_columns.1
  28.4 0.1 collective-permute-start.5
  28.5 1.7 %collective-permute-start.7 = (f32[24,1024]{1,0:T(8,128)S(1)}, f32[24,1024]{1,0:T(8,128)S(1)}, u32[]{:S(2)}, u32[]{:S(2)}) collective-permute-start(f32[24,1024]{1,0:T(8,128)S(1)} %slice_add_fusion), channel_id=1, source_target_pairs={{0,2},{1,3},{2,0},{3,1},{4,6},{5,7},{6,4},{7,5},{8,10},{9,11},{10,... | collective-permute-start | bytes 294920 | tf_op jit(solution)/shard_map/ppermute | solution.py:386
  30.2 0.1 fusion.3.bounds
  30.3 0.9 %collective-permute-start.6 = (f32[16,256]{1,0:T(8,128)S(1)}, f32[16,256]{1,0:T(8,128)S(1)}, u32[]{:S(2)}, u32[]{:S(2)}) collective-permute-start(f32[16,256]{1,0:T(8,128)S(1)} %add.59.prices_a), channel_id=1, source_target_pairs={{0,2},{1,3},{2,0},{3,1},{4,6},{5,7},{6,4},{7,5},{8,10},{9,11},{10,... | collective-permute-start | bytes 49160 | tf_op jit(solution)/shard_map/ppermute | solution.py:386
  31.2 2.7 %collective-permute-done.7 = f32[24,1024]{1,0:T(8,128)S(1)} collective-permute-done((f32[24,1024]{1,0:T(8,128)S(1)}, f32[24,1024]{1,0:T(8,128)S(1)}, u32[]{:S(2)}, u32[]{:S(2)}) %collective-permute-start.7) | collective-permute-done | bytes 98336 | tf_op jit(solution)/shard_map/ppermute | solution.py:386
  34.0 0.1 collective-permute-done.6.prices_b
  34.1 0.3 step_units.3
  34.4 1.4 %collective-permute-start.8 = (f32[16,1024]{1,0:T(8,128)S(1)}, f32[16,1024]{1,0:T(8,128)S(1)}, u32[]{:S(2)}, u32[]{:S(2)}) collective-permute-start(f32[16,1024]{1,0:T(8,128)S(1)} %get-tuple-element.36), channel_id=1, source_target_pairs={{0,4},{1,5},{2,6},{3,7},{4,0},{5,1},{6,2},{7,3},{8,12},{9,13},{10,... | collective-permute-start | bytes 196616 | tf_op jit(solution)/shard_map/ppermute | solution.py:386
  35.8 2.9 %collective-permute-done.8 = f32[16,1024]{1,0:T(8,128)S(1)} collective-permute-done((f32[16,1024]{1,0:T(8,128)S(1)}, f32[16,1024]{1,0:T(8,128)S(1)}, u32[]{:S(2)}, u32[]{:S(2)}) %collective-permute-start.8) | collective-permute-done | bytes 65568 | tf_op jit(solution)/shard_map/ppermute | solution.py:386
  38.7 2.5 %collective-permute-start.9 = (f32[16,1024]{1,0:T(8,128)S(1)}, f32[16,1024]{1,0:T(8,128)S(1)}, u32[]{:S(2)}, u32[]{:S(2)}) collective-permute-start(f32[16,1024]{1,0:T(8,128)S(1)} %add.65.flows_a), channel_id=1, source_target_pairs={{0,8},{1,9},{2,10},{3,11},{4,12},{5,13},{6,14},{7,15},{8,0},{9,1},... | collective-permute-start | bytes 196616 | tf_op jit(solution)/shard_map/ppermute | solution.py:386
  41.2 2.8 %collective-permute-done.9.flows_b = f32[16,1024]{1,0:T(8,128)S(1)} collective-permute-done((f32[16,1024]{1,0:T(8,128)S(1)}, f32[16,1024]{1,0:T(8,128)S(1)}, u32[]{:S(2)}, u32[]{:S(2)}) %collective-permute-start.9) | collective-permute-done | bytes 65568 | tf_op jit(solution)/shard_map/ppermute | solution.py:386
  43.9 0.4 step_lines.2
  44.3 0.1 collective-permute-start.10
  44.4 1.2 %collective-permute-done.10 = f32[16,256]{1,0:T(8,128)S(1)} collective-permute-done((f32[16,256]{1,0:T(8,128)S(1)}, f32[16,256]{1,0:T(8,128)S(1)}, u32[]{:S(2)}, u32[]{:S(2)}) %collective-permute-start.10) | collective-permute-done | bytes 16416 | tf_op jit(solution)/shard_map/ppermute | solution.py:386
  45.5 2.3 %collective-permute-start.11 = (f32[16,256]{1,0:T(8,128)S(1)}, f32[16,256]{1,0:T(8,128)S(1)}, u32[]{:S(2)}, u32[]{:S(2)}) collective-permute-start(f32[16,256]{1,0:T(8,128)S(1)} %add.66.prices_a), channel_id=1, source_target_pairs={{0,2},{1,3},{2,0},{3,1},{4,6},{5,7},{6,4},{7,5},{8,10},{9,11},{10,... | collective-permute-start | bytes 49160 | tf_op jit(solution)/shard_map/ppermute | solution.py:386
  47.8 1.7 %collective-permute-done.11.prices_b = f32[16,256]{1,0:T(8,128)S(1)} collective-permute-done((f32[16,256]{1,0:T(8,128)S(1)}, f32[16,256]{1,0:T(8,128)S(1)}, u32[]{:S(2)}, u32[]{:S(2)}) %collective-permute-start.11) | collective-permute-done | bytes 16416 | tf_op jit(solution)/shard_map/ppermute | solution.py:386
  49.5 0.3 step_units.4
  49.8 1.2 %collective-permute-start.12 = (f32[16,1024]{1,0:T(8,128)S(1)}, f32[16,1024]{1,0:T(8,128)S(1)}, u32[]{:S(2)}, u32[]{:S(2)}) collective-permute-start(f32[16,1024]{1,0:T(8,128)S(1)} %get-tuple-element.40), channel_id=1, source_target_pairs={{0,4},{1,5},{2,6},{3,7},{4,0},{5,1},{6,2},{7,3},{8,12},{9,13},{10,... | collective-permute-start | bytes 196616 | tf_op jit(solution)/shard_map/ppermute | solution.py:386
  50.9 3.1 %collective-permute-done.12 = f32[16,1024]{1,0:T(8,128)S(1)} collective-permute-done((f32[16,1024]{1,0:T(8,128)S(1)}, f32[16,1024]{1,0:T(8,128)S(1)}, u32[]{:S(2)}, u32[]{:S(2)}) %collective-permute-start.12) | collective-permute-done | bytes 65568 | tf_op jit(solution)/shard_map/ppermute | solution.py:386
  54.1 2.4 %collective-permute-start.13 = (f32[16,1024]{1,0:T(8,128)S(1)}, f32[16,1024]{1,0:T(8,128)S(1)}, u32[]{:S(2)}, u32[]{:S(2)}) collective-permute-start(f32[16,1024]{1,0:T(8,128)S(1)} %add.67.flows_a), channel_id=1, source_target_pairs={{0,8},{1,9},{2,10},{3,11},{4,12},{5,13},{6,14},{7,15},{8,0},{9,1},... | collective-permute-start | bytes 196616 | tf_op jit(solution)/shard_map/ppermute | solution.py:386
  56.4 2.9 %collective-permute-done.13.flows_b = f32[16,1024]{1,0:T(8,128)S(1)} collective-permute-done((f32[16,1024]{1,0:T(8,128)S(1)}, f32[16,1024]{1,0:T(8,128)S(1)}, u32[]{:S(2)}, u32[]{:S(2)}) %collective-permute-start.13) | collective-permute-done | bytes 65568 | tf_op jit(solution)/shard_map/ppermute | solution.py:386
  59.3 0.4 step_lines.3
  59.7 0.1 collective-permute-start.14
  59.7 1.2 %collective-permute-done.14 = f32[16,256]{1,0:T(8,128)S(1)} collective-permute-done((f32[16,256]{1,0:T(8,128)S(1)}, f32[16,256]{1,0:T(8,128)S(1)}, u32[]{:S(2)}, u32[]{:S(2)}) %collective-permute-start.14) | collective-permute-done | bytes 16416 | tf_op jit(solution)/shard_map/ppermute | solution.py:386
  60.9 2.7 %collective-permute-start.15 = (f32[16,256]{1,0:T(8,128)S(1)}, f32[16,256]{1,0:T(8,128)S(1)}, u32[]{:S(2)}, u32[]{:S(2)}) collective-permute-start(f32[16,256]{1,0:T(8,128)S(1)} %add.68.prices_a), channel_id=1, source_target_pairs={{0,2},{1,3},{2,0},{3,1},{4,6},{5,7},{6,4},{7,5},{8,10},{9,11},{10,... | collective-permute-start | bytes 49160 | tf_op jit(solution)/shard_map/ppermute | solution.py:386
  63.7 1.7 %collective-permute-done.15.prices_b = f32[16,256]{1,0:T(8,128)S(1)} collective-permute-done((f32[16,256]{1,0:T(8,128)S(1)}, f32[16,256]{1,0:T(8,128)S(1)}, u32[]{:S(2)}, u32[]{:S(2)}) %collective-permute-start.15) | collective-permute-done | bytes 16416 | tf_op jit(solution)/shard_map/ppermute | solution.py:386
  65.4 0.3 step_units.5
  65.7 0.8 %collective-permute-start.16 = (f32[16,512]{1,0:T(8,128)S(1)}, f32[16,512]{1,0:T(8,128)S(1)}, u32[]{:S(2)}, u32[]{:S(2)}) collective-permute-start(f32[16,512]{1,0:T(8,128)S(1)} %slice.63), channel_id=1, source_target_pairs={{0,4},{1,5},{2,6},{3,7},{4,0},{5,1},{6,2},{7,3},{8,12},{9,13},{10,... | collective-permute-start | bytes 98312 | tf_op jit(solution)/shard_map/ppermute | solution.py:386
  66.4 3.2 %collective-permute-done.16 = f32[16,512]{1,0:T(8,128)S(1)} collective-permute-done((f32[16,512]{1,0:T(8,128)S(1)}, f32[16,512]{1,0:T(8,128)S(1)}, u32[]{:S(2)}, u32[]{:S(2)}) %collective-permute-start.16) | collective-permute-done | bytes 32800 | tf_op jit(solution)/shard_map/ppermute | solution.py:386
  69.7 1.8 %collective-permute-start.17 = (f32[16,256]{1,0:T(8,128)S(1)}, f32[16,256]{1,0:T(8,128)S(1)}, u32[]{:S(2)}, u32[]{:S(2)}) collective-permute-start(f32[16,256]{1,0:T(8,128)S(1)} %slice.74), channel_id=1, source_target_pairs={{0,8},{1,9},{2,10},{3,11},{4,12},{5,13},{6,14},{7,15},{8,0},{9,1},... | collective-permute-start | bytes 49160 | tf_op jit(solution)/shard_map/ppermute | solution.py:386
  71.5 0.7 fusion.5
  72.2 2.2 %collective-permute-done.17 = f32[16,256]{1,0:T(8,128)S(1)} collective-permute-done((f32[16,256]{1,0:T(8,128)S(1)}, f32[16,256]{1,0:T(8,128)S(1)}, u32[]{:S(2)}, u32[]{:S(2)}) %collective-permute-start.17) | collective-permute-done | bytes 16416 | tf_op jit(solution)/shard_map/ppermute | solution.py:386
  74.4 0.6 subtract_bitcast_fusion
  (40 shorter events, 0.2 us)
Async XLA Ops:
  3.9 8.0 %copy-start = (f32[256,16]{0,1:T(8,128)S(1)}, f32[256,16]{0,1:T(8,128)}, u32[]{:S(2)}) copy-start(f32[256,16]{0,1:T(8,128)} %param.16) | copy-start | bytes 49156
  3.9 8.0 %copy-start.1 = (f32[32,16]{0,1:T(8,128)S(1)}, f32[32,16]{0,1:T(8,128)}, u32[]{:S(2)}) copy-start(f32[32,16]{0,1:T(8,128)} %param.14) | copy-start | bytes 6148
  3.9 8.0 %copy-start.2 = (f32[16,32]{1,0:T(8,128)S(1)}, f32[16,32]{1,0:T(8,128)}, u32[]{:S(2)}) copy-start(f32[16,32]{1,0:T(8,128)} %charging.1) | copy-start | bytes 6148
  3.9 8.0 %copy-start.3 = (f32[16,32]{1,0:T(8,128)S(1)}, f32[16,32]{1,0:T(8,128)}, u32[]{:S(2)}) copy-start(f32[16,32]{1,0:T(8,128)} %energy_dual.1) | copy-start | bytes 6148
  3.9 8.0 %copy-start.4 = (f32[256]{0:T(256)S(1)}, f32[256]{0:T(256)}, u32[]{:S(2)}) copy-start(f32[256]{0:T(256)} %param.27) | copy-start | bytes 3076
  3.9 8.0 %copy-start.5 = (f32[32]{0:T(128)S(1)}, f32[32]{0:T(128)}, u32[]{:S(2)}) copy-start(f32[32]{0:T(128)} %param.22) | copy-start | bytes 388
  3.9 8.0 %copy-start.6 = (f32[32]{0:T(128)S(1)}, f32[32]{0:T(128)}, u32[]{:S(2)}) copy-start(f32[32]{0:T(128)} %param.23) | copy-start | bytes 388
  3.9 26.3 %copy-start.7 = (f32[512]{0:T(512)S(1)}, f32[512]{0:T(512)}, u32[]{:S(2)}) copy-start(f32[512]{0:T(512)} %param.24) | copy-start | bytes 6148
  4.0 26.3 %copy-start.8 = (f32[512]{0:T(512)S(1)}, f32[512]{0:T(512)}, u32[]{:S(2)}) copy-start(f32[512]{0:T(512)} %param.25) | copy-start | bytes 6148
  4.0 26.2 %copy-start.9 = (f32[512]{0:T(512)S(1)}, f32[512]{0:T(512)}, u32[]{:S(2)}) copy-start(f32[512]{0:T(512)} %param.26) | copy-start | bytes 6148
  12.1 15.7 %collective-permute-start.2 = (f32[104,1024]{1,0:T(8,128)S(1)}, f32[104,1024]{1,0:T(8,128)S(1)}, u32[]{:S(2)}, u32[]{:S(2)}) collective-permute-start(f32[104,1024]{1,0:T(8,128)S(1)} %pad_maximum_fusion), channel_id=1, source_target_pairs={{0,1},{1,0},{2,3},{3,2},{4,5},{5,4},{6,7},{7,6},{8,9},{9,8},{10,11... | collective-permute-start | bytes 1277960 | tf_op jit(solution)/shard_map/ppermute | solution.py:386
  12.6 15.2 %collective-permute-start.3 = (f32[64,1024]{1,0:T(8,128)S(1)}, f32[64,1024]{1,0:T(8,128)S(1)}, u32[]{:S(2)}, u32[]{:S(2)}) collective-permute-start(f32[64,1024]{1,0:T(8,128)S(1)} %get-tuple-element.28.refs_2_), channel_id=1, source_target_pairs={{0,2},{1,3},{2,0},{3,1},{4,6},{5,7},{6,4},{7,5},{8,10},{9,11},{10,... | collective-permute-start | bytes 786440 | tf_op jit(solution)/shard_map/ppermute | solution.py:386
  15.2 12.6 %collective-permute-start.4 = (f32[64,1024]{1,0:T(8,128)S(1)}, f32[64,1024]{1,0:T(8,128)S(1)}, u32[]{:S(2)}, u32[]{:S(2)}) collective-permute-start(f32[64,1024]{1,0:T(8,128)S(1)} %get-tuple-element.27.refs_2_), channel_id=1, source_target_pairs={{0,3},{1,2},{2,1},{3,0},{4,7},{5,6},{6,5},{7,4},{8,11},{9,10},{10,... | collective-permute-start | bytes 786440 | tf_op jit(solution)/shard_map/ppermute | solution.py:386
  15.3 5.1 %collective-permute-start = (f32[17,1024]{1,0:T(8,128)S(1)}, f32[17,1024]{1,0:T(8,128)S(1)}, u32[]{:S(2)}, u32[]{:S(2)}) collective-permute-start(f32[17,1024]{1,0:T(8,128)S(1)} %get-tuple-element.25), channel_id=1, source_target_pairs={{0,4},{1,5},{2,6},{3,7},{4,0},{5,1},{6,2},{7,3},{8,12},{9,13},{10,... | collective-permute-start | bytes 208904 | tf_op jit(solution)/shard_map/ppermute | solution.py:386
  20.4 7.4 %collective-permute-start.1 = (f32[17,1024]{1,0:T(8,128)S(1)}, f32[17,1024]{1,0:T(8,128)S(1)}, u32[]{:S(2)}, u32[]{:S(2)}) collective-permute-start(f32[17,1024]{1,0:T(8,128)S(1)} %add.57), channel_id=1, source_target_pairs={{0,8},{1,9},{2,10},{3,11},{4,12},{5,13},{6,14},{7,15},{8,0},{9,1},... | collective-permute-start | bytes 208904 | tf_op jit(solution)/shard_map/ppermute | solution.py:386
  28.4 1.9 %collective-permute-start.5 = (f32[16,256]{1,0:T(8,128)S(1)}, f32[16,256]{1,0:T(8,128)S(1)}, u32[]{:S(2)}, u32[]{:S(2)}) collective-permute-start(f32[16,256]{1,0:T(8,128)S(1)} %get-tuple-element.33), channel_id=1, source_target_pairs={{0,1},{1,0},{2,3},{3,2},{4,5},{5,4},{6,7},{7,6},{8,9},{9,8},{10,11... | collective-permute-start | bytes 49160 | tf_op jit(solution)/shard_map/ppermute | solution.py:386
  28.5 5.4 %collective-permute-start.7 = (f32[24,1024]{1,0:T(8,128)S(1)}, f32[24,1024]{1,0:T(8,128)S(1)}, u32[]{:S(2)}, u32[]{:S(2)}) collective-permute-start(f32[24,1024]{1,0:T(8,128)S(1)} %slice_add_fusion), channel_id=1, source_target_pairs={{0,2},{1,3},{2,0},{3,1},{4,6},{5,7},{6,4},{7,5},{8,10},{9,11},{10,... | collective-permute-start | bytes 294920 | tf_op jit(solution)/shard_map/ppermute | solution.py:386
  30.3 3.8 %collective-permute-start.6 = (f32[16,256]{1,0:T(8,128)S(1)}, f32[16,256]{1,0:T(8,128)S(1)}, u32[]{:S(2)}, u32[]{:S(2)}) collective-permute-start(f32[16,256]{1,0:T(8,128)S(1)} %add.59.prices_a), channel_id=1, source_target_pairs={{0,2},{1,3},{2,0},{3,1},{4,6},{5,7},{6,4},{7,5},{8,10},{9,11},{10,... | collective-permute-start | bytes 49160 | tf_op jit(solution)/shard_map/ppermute | solution.py:386
  34.4 4.3 %collective-permute-start.8 = (f32[16,1024]{1,0:T(8,128)S(1)}, f32[16,1024]{1,0:T(8,128)S(1)}, u32[]{:S(2)}, u32[]{:S(2)}) collective-permute-start(f32[16,1024]{1,0:T(8,128)S(1)} %get-tuple-element.36), channel_id=1, source_target_pairs={{0,4},{1,5},{2,6},{3,7},{4,0},{5,1},{6,2},{7,3},{8,12},{9,13},{10,... | collective-permute-start | bytes 196616 | tf_op jit(solution)/shard_map/ppermute | solution.py:386
  38.7 5.2 %collective-permute-start.9 = (f32[16,1024]{1,0:T(8,128)S(1)}, f32[16,1024]{1,0:T(8,128)S(1)}, u32[]{:S(2)}, u32[]{:S(2)}) collective-permute-start(f32[16,1024]{1,0:T(8,128)S(1)} %add.65.flows_a), channel_id=1, source_target_pairs={{0,8},{1,9},{2,10},{3,11},{4,12},{5,13},{6,14},{7,15},{8,0},{9,1},... | collective-permute-start | bytes 196616 | tf_op jit(solution)/shard_map/ppermute | solution.py:386
  44.3 1.2 %collective-permute-start.10 = (f32[16,256]{1,0:T(8,128)S(1)}, f32[16,256]{1,0:T(8,128)S(1)}, u32[]{:S(2)}, u32[]{:S(2)}) collective-permute-start(f32[16,256]{1,0:T(8,128)S(1)} %get-tuple-element.38), channel_id=1, source_target_pairs={{0,1},{1,0},{2,3},{3,2},{4,5},{5,4},{6,7},{7,6},{8,9},{9,8},{10,11... | collective-permute-start | bytes 49160 | tf_op jit(solution)/shard_map/ppermute | solution.py:386
  45.5 4.0 %collective-permute-start.11 = (f32[16,256]{1,0:T(8,128)S(1)}, f32[16,256]{1,0:T(8,128)S(1)}, u32[]{:S(2)}, u32[]{:S(2)}) collective-permute-start(f32[16,256]{1,0:T(8,128)S(1)} %add.66.prices_a), channel_id=1, source_target_pairs={{0,2},{1,3},{2,0},{3,1},{4,6},{5,7},{6,4},{7,5},{8,10},{9,11},{10,... | collective-permute-start | bytes 49160 | tf_op jit(solution)/shard_map/ppermute | solution.py:386
  49.8 4.3 %collective-permute-start.12 = (f32[16,1024]{1,0:T(8,128)S(1)}, f32[16,1024]{1,0:T(8,128)S(1)}, u32[]{:S(2)}, u32[]{:S(2)}) collective-permute-start(f32[16,1024]{1,0:T(8,128)S(1)} %get-tuple-element.40), channel_id=1, source_target_pairs={{0,4},{1,5},{2,6},{3,7},{4,0},{5,1},{6,2},{7,3},{8,12},{9,13},{10,... | collective-permute-start | bytes 196616 | tf_op jit(solution)/shard_map/ppermute | solution.py:386
  54.1 5.2 %collective-permute-start.13 = (f32[16,1024]{1,0:T(8,128)S(1)}, f32[16,1024]{1,0:T(8,128)S(1)}, u32[]{:S(2)}, u32[]{:S(2)}) collective-permute-start(f32[16,1024]{1,0:T(8,128)S(1)} %add.67.flows_a), channel_id=1, source_target_pairs={{0,8},{1,9},{2,10},{3,11},{4,12},{5,13},{6,14},{7,15},{8,0},{9,1},... | collective-permute-start | bytes 196616 | tf_op jit(solution)/shard_map/ppermute | solution.py:386
  59.7 1.2 %collective-permute-start.14 = (f32[16,256]{1,0:T(8,128)S(1)}, f32[16,256]{1,0:T(8,128)S(1)}, u32[]{:S(2)}, u32[]{:S(2)}) collective-permute-start(f32[16,256]{1,0:T(8,128)S(1)} %get-tuple-element.41), channel_id=1, source_target_pairs={{0,1},{1,0},{2,3},{3,2},{4,5},{5,4},{6,7},{7,6},{8,9},{9,8},{10,11... | collective-permute-start | bytes 49160 | tf_op jit(solution)/shard_map/ppermute | solution.py:386
  60.9 4.4 %collective-permute-start.15 = (f32[16,256]{1,0:T(8,128)S(1)}, f32[16,256]{1,0:T(8,128)S(1)}, u32[]{:S(2)}, u32[]{:S(2)}) collective-permute-start(f32[16,256]{1,0:T(8,128)S(1)} %add.68.prices_a), channel_id=1, source_target_pairs={{0,2},{1,3},{2,0},{3,1},{4,6},{5,7},{6,4},{7,5},{8,10},{9,11},{10,... | collective-permute-start | bytes 49160 | tf_op jit(solution)/shard_map/ppermute | solution.py:386
  65.7 4.0 %collective-permute-start.16 = (f32[16,512]{1,0:T(8,128)S(1)}, f32[16,512]{1,0:T(8,128)S(1)}, u32[]{:S(2)}, u32[]{:S(2)}) collective-permute-start(f32[16,512]{1,0:T(8,128)S(1)} %slice.63), channel_id=1, source_target_pairs={{0,4},{1,5},{2,6},{3,7},{4,0},{5,1},{6,2},{7,3},{8,12},{9,13},{10,... | collective-permute-start | bytes 98312 | tf_op jit(solution)/shard_map/ppermute | solution.py:386
  69.7 4.7 %collective-permute-start.17 = (f32[16,256]{1,0:T(8,128)S(1)}, f32[16,256]{1,0:T(8,128)S(1)}, u32[]{:S(2)}, u32[]{:S(2)}) collective-permute-start(f32[16,256]{1,0:T(8,128)S(1)} %slice.74), channel_id=1, source_target_pairs={{0,8},{1,9},{2,10},{3,11},{4,12},{5,13},{6,14},{7,15},{8,0},{9,1},... | collective-permute-start | bytes 49160 | tf_op jit(solution)/shard_map/ppermute | solution.py:386

commit v2 on v1

--- a/solution.py
+++ b/solution.py
@@ -63,6 +63,13 @@
 
 whole_block = pl.BlockSpec(memory_space=pltpu.VMEM)
 grant = pltpu.CompilerParams(vmem_limit_bytes=24 << 20)
+
+
+def total(refs):
+    values = refs[0][...]
+    for ref in refs[1:]:
+        values = values + ref[...]
+    return values
 
 
 def as_column(row):
@@ -108,11 +115,14 @@
                     arrived.at[index],
                 )
             )
-    for copy in few + copies:
+    early = far if first_call else len(copies)
+    for copy in few + copies[:early]:
+        copy.start()
+    for copy in few:
+        copy.wait()
+    for copy in copies[early:]:
         copy.start()
     if first_call:
-        for copy in few:
-            copy.wait()
         weights[...] = build_weights(ids_a[...], ids_b[...], counts[...], own)
     rows_wanted = weights[...]
     horizon = rows_wanted.shape[0] - units
@@ -268,12 +278,14 @@
     )(*[near(block) for block in blocks], near(dual))
 
 
-def unit_kernel(
-    prices_a, prices_b, state, bounds, columns, base_flow, new_state, flows, *held_flows, order
-):
+def unit_kernel(*refs, shares, order):
+    prices_of, (state, bounds, columns, base_flow, new_state, flows, *held_flows) = (
+        refs[:shares],
+        refs[shares:],
+    )
     horizon = flows.shape[0]
     count, gens = new_state.shape
-    prices = prices_a[...] + prices_b[...]
+    prices = total(prices_of)
     now = state[...] if state.shape == new_state.shape else unfold(state[...], gens)[:count]
     old = now[:horizon]
     held = now[horizon : 2 * horizon]
@@ -314,46 +326,47 @@
     new_state[3 * horizon :, :] = now[3 * horizon :]
 
 
-def step_units(prices_a, prices_b, state, bounds, columns, base_flow, order=()):
+def step_units(prices, state, bounds, columns, base_flow, order=()):
     return pl.pallas_call(
-        functools.partial(unit_kernel, order=order),
-        in_specs=[whole_block] * 6,
+        functools.partial(unit_kernel, shares=len(prices), order=order),
+        in_specs=[whole_block] * (len(prices) + 4),
         out_specs=[whole_block] * 2,
         out_shape=[
-            near_array((3 * base_flow.shape[0] + 2, prices_a.shape[1] // 2)),
+            near_array((3 * base_flow.shape[0] + 2, prices[0].shape[1] // 2)),
             near_array(base_flow.shape),
         ],
         scratch_shapes=[pltpu.VMEM(base_flow.shape, jnp.float32)] if order else [],
         compiler_params=grant,
         name="step_units",
-    )(*[near(a) for a in (prices_a, prices_b, state, bounds, columns, base_flow)])
+    )(*[near(a) for a in (*prices, state, bounds, columns, base_flow)])
 
 
 def moved_dual(dual, limit, flows):
     return clip_dual(dual + dual_step * flows, dual_step, -limit, limit)
 
 
-def line_kernel(lines, flows_a, flows_b, columns, new_lines, prices):
-    horizon = flows_a.shape[0]
+def line_kernel(*refs, shares):
+    flows_of, (lines, columns, new_lines, prices) = refs[:shares], refs[shares:]
+    horizon = prices.shape[0]
     limit = lines[horizon:, :]
-    dual = moved_dual(lines[:horizon, :], limit, flows_a[...] + flows_b[...])
+    dual = moved_dual(lines[:horizon, :], limit, total(flows_of))
     new_lines[:horizon, :] = dual
     new_lines[horizon:, :] = limit
     prices[...] = local_prices(dual, columns[...])
 
 
-def step_lines(lines, flows_a, flows_b, columns):
+def step_lines(flows, lines, columns):
     return pl.pallas_call(
-        line_kernel,
-        in_specs=[whole_block] * 4,
+        functools.partial(line_kernel, shares=len(flows)),
+        in_specs=[whole_block] * (len(flows) + 2),
         out_specs=[whole_block] * 2,
         out_shape=[
             near_array(lines.shape),
-            near_array((flows_a.shape[0], columns.shape[0] // 2)),
+            near_array((flows[0].shape[0], columns.shape[0] // 2)),
         ],
         compiler_params=grant,
         name="step_lines",
-    )(*[near(a) for a in (lines, flows_a, flows_b, columns)])
+    )(*[near(a) for a in (*flows, lines, columns)])
 
 
 def on_device(
@@ -385,19 +398,32 @@
     def exchange(values, bit):
         return lax.ppermute(values, "bus", [(i, i ^ bit) for i in range(count)])
 
-    def half_sum(values, bits):
-        for bit in bits[:-1]:
-            values = values + exchange(values, bit)
-        return values, exchange(values, bits[-1])
+    def pairs_of(bits):
+        return [bits[first : first + 2] for first in range(0, len(bits), 2)]
+
+    def hops(bits):
+        found = [0]
+        for bit in bits if bits[0] < QUAD else reversed(bits):
+            found += [hop + bit for hop in found]
+        return found[1:]
+
+    def shares(values, bits):
+        for group in pairs_of(bits):
+            parts = [values]
+            for hop in hops(group):
+                parts.append(exchange(values, hop))
+            values = sum(parts)
+        return parts
 
     units = 2 * own_units
     scan = functools.partial(
         scan_factors, shift_factors, own_lines, far, units, horizon
     )
-    for_diagonal, demand_3, weights = scan(
-        (3,), sources=(generator_bus[None, :], storage_bus[None, :], load_units.T)
-    )
-    from_diagonal = exchange(for_diagonal, 3)
+    other, demand_3_2, weights = scan(
+        (3, 2), sources=(generator_bus[None, :], storage_bus[None, :], load_units.T)
+    )
+    from_diagonal = exchange(other[:units], 3)
+    from_y = exchange(other[units:], 2)
     state, lines = place(
         generation.T,
         charging,
@@ -408,16 +434,14 @@
         line_max[None, :],
         far,
     )
-    for bit in far_bits:
-        lines = lines + exchange(lines, bit)
-    for_y, demand_2 = scan((2,), weights=weights, after=for_diagonal)
-    from_y = exchange(for_y, 2)
-    rest, demand_1_0 = scan((0, 1), weights=weights, after=for_y)
+    lines = sum(shares(lines, far_bits))
+    rest, demand_0_1 = scan((0, 1), weights=weights, after=other)
     from_core = exchange(
-        jnp.concatenate([rest[units:], demand_1_0[horizon:], demand_3, state], axis=0), 1
-    )
-    kept = demand_1_0[:horizon] + from_core[units : units + horizon]
-    sent = jnp.concatenate([demand_2, state], axis=0) + from_core[units + horizon :]
+        jnp.concatenate([rest[units:], demand_0_1[horizon:], demand_3_2[:horizon], state], axis=0),
+        1,
+    )
+    kept = demand_0_1[:horizon] + from_core[units : units + horizon]
+    sent = jnp.concatenate([demand_3_2[horizon:], state], axis=0) + from_core[units + horizon :]
     from_y_too = exchange(sent, 2)
     base_flow = kept + from_y_too[:horizon]
     state = sent[horizon:] + from_y_too[horizon:]
@@ -430,8 +454,8 @@
 
     columns, prices = gather_columns((rest, from_core, from_y, from_diagonal), lines, horizon)
     for _ in range(ITERS - 1):
-        state, flows = step_units(*half_sum(prices, (1, 2)), state, bounds, columns, base_flow)
-        lines, prices = step_lines(lines, *half_sum(flows, far_bits), columns)
+        state, flows = step_units(shares(prices, (1, 2)), state, bounds, columns, base_flow)
+        lines, prices = step_lines(shares(flows, far_bits), lines, columns)
     mine = lambda a: lax.dynamic_slice_in_dim(a, place_of_quad * own_lines, own_lines, axis=1)
     if own_lines % 128 == 0:
         steps = len(far_bits)
@@ -440,13 +464,17 @@
         )
     else:
         order = ()
-    state, flows = step_units(*half_sum(prices, (1, 2)), state, bounds, columns, base_flow, order)
+    state, flows = step_units(shares(prices, (1, 2)), state, bounds, columns, base_flow, order)
     if order:
-        for bit in far_bits:
-            half = flows.shape[1] // 2
-            flows = flows[:, :half] + exchange(flows[:, half:], bit)
+        for group in pairs_of(far_bits):
+            width = flows.shape[1] >> len(group)
+            kept = flows[:, :width]
+            for hop in hops(group):
+                part = sum((hop // bit % 2) << k for k, bit in enumerate(reversed(group)))
+                kept = kept + exchange(flows[:, part * width : (part + 1) * width], hop)
+            flows = kept
     else:
-        flows = mine(sum(half_sum(flows, far_bits)))
+        flows = mine(sum(shares(flows, far_bits)))
     own_dual = moved_dual(mine(lines[:horizon]), mine(lines[horizon:]), flows)
     ends = lax.dynamic_slice_in_dim(state, member * own_units, own_units, axis=1)
     return (

time: 75.1 us -> 72.8 us (0.969)
  waiting for transfers between devices: 33.6 us -> 29.6 us
  starting transfers between devices: 25.5 us -> 28.8 us
  Pallas kernels: 13.3 us -> 11.8 us
    ppermute x18 -> x25, waiting for transfers between devices: 33.6 us -> 29.6 us  [exchange(): return lax.ppermute(values, 'bus', [(i, i ^ bit) for i in range(count)])]
    ppermute x18 -> x25, starting transfers between devices: 25.5 us -> 28.8 us  [exchange(): return lax.ppermute(values, 'bus', [(i, i ^ bit) for i in range(count)])]
    pallas_call x3 -> x2, Pallas kernels: 11.1 us -> 9.55 us  [scan_factors(): pl.pallas_call(functools.partial(scan_kernel, wanted=wanted, own_lines=ow...]
  transfers between devices with their start and end apart: 18 -> 25, of which waited for: 14 -> 18; matrix products, arithmetic and copies ran while one was open for 1% -> 1% of each run, Pallas kernels for 0% -> 1%
where the time goes in v2:
time: 72.8 us; the launch traced here: 72.7 us
  waiting for transfers between devices  29.6 us (41%)
  starting transfers between devices  28.8 us (40%)
  Pallas kernels  11.8 us (16%)
  between operations  0.92 us (1%)
  local copies, waits for them, and re-layouts  0.82 us (1%)
  other arithmetic  0.8 us (1%)
    ppermute x25, waiting for transfers between devices, exchange(): return lax.ppermute(values, 'bus', [(i, i ^ bit) for i in range(count)])  29.6 us
    ppermute x25, starting transfers between devices, exchange(): return lax.ppermute(values, 'bus', [(i, i ^ bit) for i in range(count)])  28.8 us
    pallas_call x2, Pallas kernels, scan_factors(): pl.pallas_call(functools.partial(scan_kernel, wanted=wanted, own_lines=ow...  9.55 us
  transfers between devices with their start and end apart: 25, of which 18 were waited for; matrix products, arithmetic and copies ran while one was open for 1% of the time, Pallas kernels for 1%

profile of v2, /device:TPU:0, one launch (start us, length us, event | category | flops | bytes accessed | tf_op | source)
XLA Modules:
  0.0 72.7 jit_solution(5039783224805820760)
XLA Ops:
  0.7 4.8 %scan_factors.2 = (f32[128,1024]{1,0:T(8,128)S(1)}, f32[32,1024]{1,0:T(8,128)S(1)}, bf16[80,1024]{1,0:T(8,128)(2,1)S(1)}) custom-call(s32[1,32]{1,0:T(1,128)} %bitcast.28, s32[1,32]{1,0:T(1,128)} %bitcast.29, s32[16,1024]{1,0:T(8,128)} %bitcast.22, f32[4096,1024]{1,0:T(8,128)} %refs_1_.1), custom_call_target="tpu_custom_call" | custom-call | tf_op jit(solution)/shard_map/scan_factors/pallas_call | solution.py:168
  5.6 4.7 %scan_factors.3 = (f32[128,1024]{1,0:T(8,128)S(1)}, f32[32,1024]{1,0:T(8,128)S(1)}) custom-call(bf16[80,1024]{1,0:T(8,128)(2,1)S(1)} %get-tuple-element.23.refs_0_, f32[4096,1024]{1,0:T(8,128)} %refs_1_.1, f32[128,1024]{1,0:T(8,128)S(1)} %get-tuple-element.24.refs_2_), custom_call_target="tpu_custom_call" | custom-call | tf_op jit(solution)/shard_map/scan_factors/pallas_call | solution.py:168
  10.4 0.1 place.1
  10.6 0.6 collective-permute-start
  11.1 4.7 %collective-permute-start.5 = (f32[17,1024]{1,0:T(8,128)S(1)}, f32[17,1024]{1,0:T(8,128)S(1)}, u32[]{:S(2)}, u32[]{:S(2)}) collective-permute-start(f32[17,1024]{1,0:T(8,128)S(1)} %get-tuple-element.29), channel_id=1, source_target_pairs={{0,12},{1,13},{2,14},{3,15},{4,8},{5,9},{6,10},{7,11},{8,4},{9,5},... | collective-permute-start | bytes 208904 | tf_op jit(solution)/shard_map/ppermute | solution.py:399
  15.8 0.6 collective-permute-start.3
  16.5 1.7 %collective-permute-start.1 = (f32[64,1024]{1,0:T(8,128)S(1)}, f32[64,1024]{1,0:T(8,128)S(1)}, u32[]{:S(2)}, u32[]{:S(2)}) collective-permute-start(f32[64,1024]{1,0:T(8,128)S(1)} %get-tuple-element.45), channel_id=1, source_target_pairs={{0,2},{1,3},{2,0},{3,1},{4,6},{5,7},{6,4},{7,5},{8,10},{9,11},{10,... | collective-permute-start | bytes 786440 | tf_op jit(solution)/shard_map/ppermute | solution.py:399
  18.2 0.1 fusion.1.refs_5_
  18.3 1.1 %collective-permute-done.5 = f32[17,1024]{1,0:T(8,128)S(1)} collective-permute-done((f32[17,1024]{1,0:T(8,128)S(1)}, f32[17,1024]{1,0:T(8,128)S(1)}, u32[]{:S(2)}, u32[]{:S(2)}) %collective-permute-start.5) | collective-permute-done | bytes 69664 | tf_op jit(solution)/shard_map/ppermute | solution.py:399
  19.5 1.7 %collective-permute-start.9 = (f32[24,1024]{1,0:T(8,128)S(1)}, f32[24,1024]{1,0:T(8,128)S(1)}, u32[]{:S(2)}, u32[]{:S(2)}) collective-permute-start(f32[24,1024]{1,0:T(8,128)S(1)} %slice_add_fusion), channel_id=1, source_target_pairs={{0,2},{1,3},{2,0},{3,1},{4,6},{5,7},{6,4},{7,5},{8,10},{9,11},{10,... | collective-permute-start | bytes 294920 | tf_op jit(solution)/shard_map/ppermute | solution.py:399
  21.2 1.2 %collective-permute-done.4 = f32[17,1024]{1,0:T(8,128)S(1)} collective-permute-done((f32[17,1024]{1,0:T(8,128)S(1)}, f32[17,1024]{1,0:T(8,128)S(1)}, u32[]{:S(2)}, u32[]{:S(2)}) %collective-permute-start.4) | collective-permute-done | bytes 69664 | tf_op jit(solution)/shard_map/ppermute | solution.py:399
  22.4 2.3 %collective-permute-done.3 = f32[17,1024]{1,0:T(8,128)S(1)} collective-permute-done((f32[17,1024]{1,0:T(8,128)S(1)}, f32[17,1024]{1,0:T(8,128)S(1)}, u32[]{:S(2)}, u32[]{:S(2)}) %collective-permute-start.3) | collective-permute-done | bytes 69664 | tf_op jit(solution)/shard_map/ppermute | solution.py:399
  24.7 1.0 %collective-permute-done.1.block2 = f32[64,1024]{1,0:T(8,128)S(1)} collective-permute-done((f32[64,1024]{1,0:T(8,128)S(1)}, f32[64,1024]{1,0:T(8,128)S(1)}, u32[]{:S(2)}, u32[]{:S(2)}) %collective-permute-start.1) | collective-permute-done | bytes 262176 | tf_op jit(solution)/shard_map/ppermute | solution.py:399
  25.7 4.5 %collective-permute-done.2.block3 = f32[64,1024]{1,0:T(8,128)S(1)} collective-permute-done((f32[64,1024]{1,0:T(8,128)S(1)}, f32[64,1024]{1,0:T(8,128)S(1)}, u32[]{:S(2)}, u32[]{:S(2)}) %collective-permute-start.2) | collective-permute-done | bytes 262176 | tf_op jit(solution)/shard_map/ppermute | solution.py:399
  30.2 0.6 gather_columns.1
  30.8 0.8 %collective-permute-start.6 = (f32[16,256]{1,0:T(8,128)S(1)}, f32[16,256]{1,0:T(8,128)S(1)}, u32[]{:S(2)}, u32[]{:S(2)}) collective-permute-start(f32[16,256]{1,0:T(8,128)S(1)} %get-tuple-element.30.refs_0_), channel_id=1, source_target_pairs={{0,1},{1,0},{2,3},{3,2},{4,5},{5,4},{6,7},{7,6},{8,9},{9,8},{10,11... | collective-permute-start | bytes 49160 | tf_op jit(solution)/shard_map/ppermute | solution.py:399
  31.7 1.5 %collective-permute-start.7 = (f32[16,256]{1,0:T(8,128)S(1)}, f32[16,256]{1,0:T(8,128)S(1)}, u32[]{:S(2)}, u32[]{:S(2)}) collective-permute-start(f32[16,256]{1,0:T(8,128)S(1)} %get-tuple-element.30.refs_0_), channel_id=1, source_target_pairs={{0,2},{1,3},{2,0},{3,1},{4,6},{5,7},{6,4},{7,5},{8,10},{9,11},{10,... | collective-permute-start | bytes 49160 | tf_op jit(solution)/shard_map/ppermute | solution.py:399
  33.2 2.2 %collective-permute-done.7.refs_2_ = f32[16,256]{1,0:T(8,128)S(1)} collective-permute-done((f32[16,256]{1,0:T(8,128)S(1)}, f32[16,256]{1,0:T(8,128)S(1)}, u32[]{:S(2)}, u32[]{:S(2)}) %collective-permute-start.7) | collective-permute-done | bytes 16416 | tf_op jit(solution)/shard_map/ppermute | solution.py:399
  35.4 1.1 %collective-permute-done.8.refs_3_ = f32[16,256]{1,0:T(8,128)S(1)} collective-permute-done((f32[16,256]{1,0:T(8,128)S(1)}, f32[16,256]{1,0:T(8,128)S(1)}, u32[]{:S(2)}, u32[]{:S(2)}) %collective-permute-start.8) | collective-permute-done | bytes 16416 | tf_op jit(solution)/shard_map/ppermute | solution.py:399
  36.5 0.3 step_units.3
  36.8 2.4 %collective-permute-start.10 = (f32[16,1024]{1,0:T(8,128)S(1)}, f32[16,1024]{1,0:T(8,128)S(1)}, u32[]{:S(2)}, u32[]{:S(2)}) collective-permute-start(f32[16,1024]{1,0:T(8,128)S(1)} %get-tuple-element.32.refs_0_), channel_id=1, source_target_pairs={{0,8},{1,9},{2,10},{3,11},{4,12},{5,13},{6,14},{7,15},{8,0},{9,1},... | collective-permute-start | bytes 196616 | tf_op jit(solution)/shard_map/ppermute | solution.py:399
  39.1 1.7 %collective-permute-start.11 = (f32[16,1024]{1,0:T(8,128)S(1)}, f32[16,1024]{1,0:T(8,128)S(1)}, u32[]{:S(2)}, u32[]{:S(2)}) collective-permute-start(f32[16,1024]{1,0:T(8,128)S(1)} %get-tuple-element.32.refs_0_), channel_id=1, source_target_pairs={{0,4},{1,5},{2,6},{3,7},{4,0},{5,1},{6,2},{7,3},{8,12},{9,13},{10,... | collective-permute-start | bytes 196616 | tf_op jit(solution)/shard_map/ppermute | solution.py:399
  40.9 0.3 collective-permute-start.12
  41.2 2.4 %collective-permute-done.10.refs_1_ = f32[16,1024]{1,0:T(8,128)S(1)} collective-permute-done((f32[16,1024]{1,0:T(8,128)S(1)}, f32[16,1024]{1,0:T(8,128)S(1)}, u32[]{:S(2)}, u32[]{:S(2)}) %collective-permute-start.10) | collective-permute-done | bytes 65568 | tf_op jit(solution)/shard_map/ppermute | solution.py:399
  43.6 3.3 %collective-permute-done.12.refs_3_ = f32[16,1024]{1,0:T(8,128)S(1)} collective-permute-done((f32[16,1024]{1,0:T(8,128)S(1)}, f32[16,1024]{1,0:T(8,128)S(1)}, u32[]{:S(2)}, u32[]{:S(2)}) %collective-permute-start.12) | collective-permute-done | bytes 65568 | tf_op jit(solution)/shard_map/ppermute | solution.py:399
  47.0 0.4 step_lines.2
  47.4 0.6 collective-permute-start.14
  48.0 1.2 %collective-permute-start.15 = (f32[16,256]{1,0:T(8,128)S(1)}, f32[16,256]{1,0:T(8,128)S(1)}, u32[]{:S(2)}, u32[]{:S(2)}) collective-permute-start(f32[16,256]{1,0:T(8,128)S(1)} %get-tuple-element.33.refs_0_), channel_id=1, source_target_pairs={{0,3},{1,2},{2,1},{3,0},{4,7},{5,6},{6,5},{7,4},{8,11},{9,10},{10,... | collective-permute-start | bytes 49160 | tf_op jit(solution)/shard_map/ppermute | solution.py:399
  49.2 2.1 %collective-permute-done.14.refs_2_ = f32[16,256]{1,0:T(8,128)S(1)} collective-permute-done((f32[16,256]{1,0:T(8,128)S(1)}, f32[16,256]{1,0:T(8,128)S(1)}, u32[]{:S(2)}, u32[]{:S(2)}) %collective-permute-start.14) | collective-permute-done | bytes 16416 | tf_op jit(solution)/shard_map/ppermute | solution.py:399
  51.3 0.3 step_units.4
  51.6 1.4 %collective-permute-start.16 = (f32[16,1024]{1,0:T(8,128)S(1)}, f32[16,1024]{1,0:T(8,128)S(1)}, u32[]{:S(2)}, u32[]{:S(2)}) collective-permute-start(f32[16,1024]{1,0:T(8,128)S(1)} %get-tuple-element.35.refs_0_), channel_id=1, source_target_pairs={{0,8},{1,9},{2,10},{3,11},{4,12},{5,13},{6,14},{7,15},{8,0},{9,1},... | collective-permute-start | bytes 196616 | tf_op jit(solution)/shard_map/ppermute | solution.py:399
  53.0 0.2 collective-permute-start.17
  53.3 2.8 %collective-permute-start.18 = (f32[16,1024]{1,0:T(8,128)S(1)}, f32[16,1024]{1,0:T(8,128)S(1)}, u32[]{:S(2)}, u32[]{:S(2)}) collective-permute-start(f32[16,1024]{1,0:T(8,128)S(1)} %get-tuple-element.35.refs_0_), channel_id=1, source_target_pairs={{0,12},{1,13},{2,14},{3,15},{4,8},{5,9},{6,10},{7,11},{8,4},{9,5},... | collective-permute-start | bytes 196616 | tf_op jit(solution)/shard_map/ppermute | solution.py:399
  56.0 2.1 %collective-permute-done.16.refs_1_ = f32[16,1024]{1,0:T(8,128)S(1)} collective-permute-done((f32[16,1024]{1,0:T(8,128)S(1)}, f32[16,1024]{1,0:T(8,128)S(1)}, u32[]{:S(2)}, u32[]{:S(2)}) %collective-permute-start.16) | collective-permute-done | bytes 65568 | tf_op jit(solution)/shard_map/ppermute | solution.py:399
  58.1 1.6 %collective-permute-done.17.refs_2_ = f32[16,1024]{1,0:T(8,128)S(1)} collective-permute-done((f32[16,1024]{1,0:T(8,128)S(1)}, f32[16,1024]{1,0:T(8,128)S(1)}, u32[]{:S(2)}, u32[]{:S(2)}) %collective-permute-start.17) | collective-permute-done | bytes 65568 | tf_op jit(solution)/shard_map/ppermute | solution.py:399
  59.7 0.4 step_lines.3
  60.1 1.4 %collective-permute-start.20 = (f32[16,256]{1,0:T(8,128)S(1)}, f32[16,256]{1,0:T(8,128)S(1)}, u32[]{:S(2)}, u32[]{:S(2)}) collective-permute-start(f32[16,256]{1,0:T(8,128)S(1)} %get-tuple-element.37.refs_0_), channel_id=1, source_target_pairs={{0,2},{1,3},{2,0},{3,1},{4,6},{5,7},{6,4},{7,5},{8,10},{9,11},{10,... | collective-permute-start | bytes 49160 | tf_op jit(solution)/shard_map/ppermute | solution.py:399
  61.5 0.5 collective-permute-start.21
  62.0 1.9 %collective-permute-done.20.refs_2_ = f32[16,256]{1,0:T(8,128)S(1)} collective-permute-done((f32[16,256]{1,0:T(8,128)S(1)}, f32[16,256]{1,0:T(8,128)S(1)}, u32[]{:S(2)}, u32[]{:S(2)}) %collective-permute-start.20) | collective-permute-done | bytes 16416 | tf_op jit(solution)/shard_map/ppermute | solution.py:399
  63.9 0.8 %collective-permute-done.21.refs_3_ = f32[16,256]{1,0:T(8,128)S(1)} collective-permute-done((f32[16,256]{1,0:T(8,128)S(1)}, f32[16,256]{1,0:T(8,128)S(1)}, u32[]{:S(2)}, u32[]{:S(2)}) %collective-permute-start.21) | collective-permute-done | bytes 16416 | tf_op jit(solution)/shard_map/ppermute | solution.py:399
  64.6 0.3 step_units.5
  64.9 2.5 %collective-permute-start.24 = (f32[16,256]{1,0:T(8,128)S(1)}, f32[16,256]{1,0:T(8,128)S(1)}, u32[]{:S(2)}, u32[]{:S(2)}) collective-permute-start(f32[16,256]{1,0:T(8,128)S(1)} %get-tuple-element.49), channel_id=1, source_target_pairs={{0,12},{1,13},{2,14},{3,15},{4,8},{5,9},{6,10},{7,11},{8,4},{9,5},... | collective-permute-start | bytes 49160 | tf_op jit(solution)/shard_map/ppermute | solution.py:399
  67.4 2.0 %collective-permute-start.22 = (f32[16,256]{1,0:T(8,128)S(1)}, f32[16,256]{1,0:T(8,128)S(1)}, u32[]{:S(2)}, u32[]{:S(2)}) collective-permute-start(f32[16,256]{1,0:T(8,128)S(1)} %get-tuple-element.48), channel_id=1, source_target_pairs={{0,8},{1,9},{2,10},{3,11},{4,12},{5,13},{6,14},{7,15},{8,0},{9,1},... | collective-permute-start | bytes 49160 | tf_op jit(solution)/shard_map/ppermute | solution.py:399
  69.4 0.7 fusion.6
  70.1 0.5 collective-permute-done.24
  70.5 0.6 collective-permute-done.23
  71.1 0.9 %collective-permute-done.22 = f32[16,256]{1,0:T(8,128)S(1)} collective-permute-done((f32[16,256]{1,0:T(8,128)S(1)}, f32[16,256]{1,0:T(8,128)S(1)}, u32[]{:S(2)}, u32[]{:S(2)}) %collective-permute-start.22) | collective-permute-done | bytes 16416 | tf_op jit(solution)/shard_map/ppermute | solution.py:399
  72.1 0.6 subtract_bitcast_fusion
  (47 shorter events, 0.5 us)
Async XLA Ops:
  0.6 9.7 %copy-start = (f32[256,16]{0,1:T(8,128)S(1)}, f32[256,16]{0,1:T(8,128)}, u32[]{:S(2)}) copy-start(f32[256,16]{0,1:T(8,128)} %param.16) | copy-start | bytes 49156
  0.6 9.7 %copy-start.1 = (f32[32,16]{0,1:T(8,128)S(1)}, f32[32,16]{0,1:T(8,128)}, u32[]{:S(2)}) copy-start(f32[32,16]{0,1:T(8,128)} %param.14) | copy-start | bytes 6148
  0.7 9.7 %copy-start.2 = (f32[16,32]{1,0:T(8,128)S(1)}, f32[16,32]{1,0:T(8,128)}, u32[]{:S(2)}) copy-start(f32[16,32]{1,0:T(8,128)} %charging.1) | copy-start | bytes 6148
  0.7 9.7 %copy-start.3 = (f32[16,32]{1,0:T(8,128)S(1)}, f32[16,32]{1,0:T(8,128)}, u32[]{:S(2)}) copy-start(f32[16,32]{1,0:T(8,128)} %energy_dual.1) | copy-start | bytes 6148
  0.7 9.7 %copy-start.4 = (f32[256]{0:T(256)S(1)}, f32[256]{0:T(256)}, u32[]{:S(2)}) copy-start(f32[256]{0:T(256)} %param.27) | copy-start | bytes 3076
  0.7 9.7 %copy-start.5 = (f32[32]{0:T(128)S(1)}, f32[32]{0:T(128)}, u32[]{:S(2)}) copy-start(f32[32]{0:T(128)} %param.22) | copy-start | bytes 388
  0.7 9.7 %copy-start.6 = (f32[32]{0:T(128)S(1)}, f32[32]{0:T(128)}, u32[]{:S(2)}) copy-start(f32[32]{0:T(128)} %param.23) | copy-start | bytes 388
  0.7 17.5 %copy-start.7 = (f32[512]{0:T(512)S(1)}, f32[512]{0:T(512)}, u32[]{:S(2)}) copy-start(f32[512]{0:T(512)} %param.24) | copy-start | bytes 6148
  0.7 17.5 %copy-start.8 = (f32[512]{0:T(512)S(1)}, f32[512]{0:T(512)}, u32[]{:S(2)}) copy-start(f32[512]{0:T(512)} %param.25) | copy-start | bytes 6148
  0.7 17.5 %copy-start.9 = (f32[512]{0:T(512)S(1)}, f32[512]{0:T(512)}, u32[]{:S(2)}) copy-start(f32[512]{0:T(512)} %param.26) | copy-start | bytes 6148
  10.6 7.7 %collective-permute-start = (f32[104,1024]{1,0:T(8,128)S(1)}, f32[104,1024]{1,0:T(8,128)S(1)}, u32[]{:S(2)}, u32[]{:S(2)}) collective-permute-start(f32[104,1024]{1,0:T(8,128)S(1)} %pad_maximum_fusion), channel_id=1, source_target_pairs={{0,1},{1,0},{2,3},{3,2},{4,5},{5,4},{6,7},{7,6},{8,9},{9,8},{10,11... | collective-permute-start | bytes 1277960 | tf_op jit(solution)/shard_map/ppermute | solution.py:399
  11.1 8.4 %collective-permute-start.5 = (f32[17,1024]{1,0:T(8,128)S(1)}, f32[17,1024]{1,0:T(8,128)S(1)}, u32[]{:S(2)}, u32[]{:S(2)}) collective-permute-start(f32[17,1024]{1,0:T(8,128)S(1)} %get-tuple-element.29), channel_id=1, source_target_pairs={{0,12},{1,13},{2,14},{3,15},{4,8},{5,9},{6,10},{7,11},{8,4},{9,5},... | collective-permute-start | bytes 208904 | tf_op jit(solution)/shard_map/ppermute | solution.py:399
  15.8 6.6 %collective-permute-start.4 = (f32[17,1024]{1,0:T(8,128)S(1)}, f32[17,1024]{1,0:T(8,128)S(1)}, u32[]{:S(2)}, u32[]{:S(2)}) collective-permute-start(f32[17,1024]{1,0:T(8,128)S(1)} %get-tuple-element.29), channel_id=1, source_target_pairs={{0,4},{1,5},{2,6},{3,7},{4,0},{5,1},{6,2},{7,3},{8,12},{9,13},{10,... | collective-permute-start | bytes 208904 | tf_op jit(solution)/shard_map/ppermute | solution.py:399
  15.8 8.9 %collective-permute-start.3 = (f32[17,1024]{1,0:T(8,128)S(1)}, f32[17,1024]{1,0:T(8,128)S(1)}, u32[]{:S(2)}, u32[]{:S(2)}) collective-permute-start(f32[17,1024]{1,0:T(8,128)S(1)} %get-tuple-element.29), channel_id=1, source_target_pairs={{0,8},{1,9},{2,10},{3,11},{4,12},{5,13},{6,14},{7,15},{8,0},{9,1},... | collective-permute-start | bytes 208904 | tf_op jit(solution)/shard_map/ppermute | solution.py:399
  16.5 9.2 %collective-permute-start.1 = (f32[64,1024]{1,0:T(8,128)S(1)}, f32[64,1024]{1,0:T(8,128)S(1)}, u32[]{:S(2)}, u32[]{:S(2)}) collective-permute-start(f32[64,1024]{1,0:T(8,128)S(1)} %get-tuple-element.45), channel_id=1, source_target_pairs={{0,2},{1,3},{2,0},{3,1},{4,6},{5,7},{6,4},{7,5},{8,10},{9,11},{10,... | collective-permute-start | bytes 786440 | tf_op jit(solution)/shard_map/ppermute | solution.py:399
  18.3 12.0 %collective-permute-start.2 = (f32[64,1024]{1,0:T(8,128)S(1)}, f32[64,1024]{1,0:T(8,128)S(1)}, u32[]{:S(2)}, u32[]{:S(2)}) collective-permute-start(f32[64,1024]{1,0:T(8,128)S(1)} %get-tuple-element.44), channel_id=1, source_target_pairs={{0,3},{1,2},{2,1},{3,0},{4,7},{5,6},{6,5},{7,4},{8,11},{9,10},{10,... | collective-permute-start | bytes 786440 | tf_op jit(solution)/shard_map/ppermute | solution.py:399
  19.5 13.7 %collective-permute-start.9 = (f32[24,1024]{1,0:T(8,128)S(1)}, f32[24,1024]{1,0:T(8,128)S(1)}, u32[]{:S(2)}, u32[]{:S(2)}) collective-permute-start(f32[24,1024]{1,0:T(8,128)S(1)} %slice_add_fusion), channel_id=1, source_target_pairs={{0,2},{1,3},{2,0},{3,1},{4,6},{5,7},{6,4},{7,5},{8,10},{9,11},{10,... | collective-permute-start | bytes 294920 | tf_op jit(solution)/shard_map/ppermute | solution.py:399
  30.8 2.4 %collective-permute-start.6 = (f32[16,256]{1,0:T(8,128)S(1)}, f32[16,256]{1,0:T(8,128)S(1)}, u32[]{:S(2)}, u32[]{:S(2)}) collective-permute-start(f32[16,256]{1,0:T(8,128)S(1)} %get-tuple-element.30.refs_0_), channel_id=1, source_target_pairs={{0,1},{1,0},{2,3},{3,2},{4,5},{5,4},{6,7},{7,6},{8,9},{9,8},{10,11... | collective-permute-start | bytes 49160 | tf_op jit(solution)/shard_map/ppermute | solution.py:399
  31.7 3.7 %collective-permute-start.7 = (f32[16,256]{1,0:T(8,128)S(1)}, f32[16,256]{1,0:T(8,128)S(1)}, u32[]{:S(2)}, u32[]{:S(2)}) collective-permute-start(f32[16,256]{1,0:T(8,128)S(1)} %get-tuple-element.30.refs_0_), channel_id=1, source_target_pairs={{0,2},{1,3},{2,0},{3,1},{4,6},{5,7},{6,4},{7,5},{8,10},{9,11},{10,... | collective-permute-start | bytes 49160 | tf_op jit(solution)/shard_map/ppermute | solution.py:399
  33.2 3.3 %collective-permute-start.8 = (f32[16,256]{1,0:T(8,128)S(1)}, f32[16,256]{1,0:T(8,128)S(1)}, u32[]{:S(2)}, u32[]{:S(2)}) collective-permute-start(f32[16,256]{1,0:T(8,128)S(1)} %get-tuple-element.30.refs_0_), channel_id=1, source_target_pairs={{0,3},{1,2},{2,1},{3,0},{4,7},{5,6},{6,5},{7,4},{8,11},{9,10},{10,... | collective-permute-start | bytes 49160 | tf_op jit(solution)/shard_map/ppermute | solution.py:399
  36.8 6.8 %collective-permute-start.10 = (f32[16,1024]{1,0:T(8,128)S(1)}, f32[16,1024]{1,0:T(8,128)S(1)}, u32[]{:S(2)}, u32[]{:S(2)}) collective-permute-start(f32[16,1024]{1,0:T(8,128)S(1)} %get-tuple-element.32.refs_0_), channel_id=1, source_target_pairs={{0,8},{1,9},{2,10},{3,11},{4,12},{5,13},{6,14},{7,15},{8,0},{9,1},... | collective-permute-start | bytes 196616 | tf_op jit(solution)/shard_map/ppermute | solution.py:399
  39.1 4.5 %collective-permute-start.11 = (f32[16,1024]{1,0:T(8,128)S(1)}, f32[16,1024]{1,0:T(8,128)S(1)}, u32[]{:S(2)}, u32[]{:S(2)}) collective-permute-start(f32[16,1024]{1,0:T(8,128)S(1)} %get-tuple-element.32.refs_0_), channel_id=1, source_target_pairs={{0,4},{1,5},{2,6},{3,7},{4,0},{5,1},{6,2},{7,3},{8,12},{9,13},{10,... | collective-permute-start | bytes 196616 | tf_op jit(solution)/shard_map/ppermute | solution.py:399
  40.9 6.1 %collective-permute-start.12 = (f32[16,1024]{1,0:T(8,128)S(1)}, f32[16,1024]{1,0:T(8,128)S(1)}, u32[]{:S(2)}, u32[]{:S(2)}) collective-permute-start(f32[16,1024]{1,0:T(8,128)S(1)} %get-tuple-element.32.refs_0_), channel_id=1, source_target_pairs={{0,12},{1,13},{2,14},{3,15},{4,8},{5,9},{6,10},{7,11},{8,4},{9,5},... | collective-permute-start | bytes 196616 | tf_op jit(solution)/shard_map/ppermute | solution.py:399
  47.3 1.9 %collective-permute-start.13 = (f32[16,256]{1,0:T(8,128)S(1)}, f32[16,256]{1,0:T(8,128)S(1)}, u32[]{:S(2)}, u32[]{:S(2)}) collective-permute-start(f32[16,256]{1,0:T(8,128)S(1)} %get-tuple-element.33.refs_0_), channel_id=1, source_target_pairs={{0,1},{1,0},{2,3},{3,2},{4,5},{5,4},{6,7},{7,6},{8,9},{9,8},{10,11... | collective-permute-start | bytes 49160 | tf_op jit(solution)/shard_map/ppermute | solution.py:399
  47.4 3.9 %collective-permute-start.14 = (f32[16,256]{1,0:T(8,128)S(1)}, f32[16,256]{1,0:T(8,128)S(1)}, u32[]{:S(2)}, u32[]{:S(2)}) collective-permute-start(f32[16,256]{1,0:T(8,128)S(1)} %get-tuple-element.33.refs_0_), channel_id=1, source_target_pairs={{0,2},{1,3},{2,0},{3,1},{4,6},{5,7},{6,4},{7,5},{8,10},{9,11},{10,... | collective-permute-start | bytes 49160 | tf_op jit(solution)/shard_map/ppermute | solution.py:399
  48.0 3.3 %collective-permute-start.15 = (f32[16,256]{1,0:T(8,128)S(1)}, f32[16,256]{1,0:T(8,128)S(1)}, u32[]{:S(2)}, u32[]{:S(2)}) collective-permute-start(f32[16,256]{1,0:T(8,128)S(1)} %get-tuple-element.33.refs_0_), channel_id=1, source_target_pairs={{0,3},{1,2},{2,1},{3,0},{4,7},{5,6},{6,5},{7,4},{8,11},{9,10},{10,... | collective-permute-start | bytes 49160 | tf_op jit(solution)/shard_map/ppermute | solution.py:399
  51.6 6.5 %collective-permute-start.16 = (f32[16,1024]{1,0:T(8,128)S(1)}, f32[16,1024]{1,0:T(8,128)S(1)}, u32[]{:S(2)}, u32[]{:S(2)}) collective-permute-start(f32[16,1024]{1,0:T(8,128)S(1)} %get-tuple-element.35.refs_0_), channel_id=1, source_target_pairs={{0,8},{1,9},{2,10},{3,11},{4,12},{5,13},{6,14},{7,15},{8,0},{9,1},... | collective-permute-start | bytes 196616 | tf_op jit(solution)/shard_map/ppermute | solution.py:399
  53.0 6.6 %collective-permute-start.17 = (f32[16,1024]{1,0:T(8,128)S(1)}, f32[16,1024]{1,0:T(8,128)S(1)}, u32[]{:S(2)}, u32[]{:S(2)}) collective-permute-start(f32[16,1024]{1,0:T(8,128)S(1)} %get-tuple-element.35.refs_0_), channel_id=1, source_target_pairs={{0,4},{1,5},{2,6},{3,7},{4,0},{5,1},{6,2},{7,3},{8,12},{9,13},{10,... | collective-permute-start | bytes 196616 | tf_op jit(solution)/shard_map/ppermute | solution.py:399
  53.3 6.4 %collective-permute-start.18 = (f32[16,1024]{1,0:T(8,128)S(1)}, f32[16,1024]{1,0:T(8,128)S(1)}, u32[]{:S(2)}, u32[]{:S(2)}) collective-permute-start(f32[16,1024]{1,0:T(8,128)S(1)} %get-tuple-element.35.refs_0_), channel_id=1, source_target_pairs={{0,12},{1,13},{2,14},{3,15},{4,8},{5,9},{6,10},{7,11},{8,4},{9,5},... | collective-permute-start | bytes 196616 | tf_op jit(solution)/shard_map/ppermute | solution.py:399
  60.0 1.9 %collective-permute-start.19 = (f32[16,256]{1,0:T(8,128)S(1)}, f32[16,256]{1,0:T(8,128)S(1)}, u32[]{:S(2)}, u32[]{:S(2)}) collective-permute-start(f32[16,256]{1,0:T(8,128)S(1)} %get-tuple-element.37.refs_0_), channel_id=1, source_target_pairs={{0,1},{1,0},{2,3},{3,2},{4,5},{5,4},{6,7},{7,6},{8,9},{9,8},{10,11... | collective-permute-start | bytes 49160 | tf_op jit(solution)/shard_map/ppermute | solution.py:399
  60.1 3.8 %collective-permute-start.20 = (f32[16,256]{1,0:T(8,128)S(1)}, f32[16,256]{1,0:T(8,128)S(1)}, u32[]{:S(2)}, u32[]{:S(2)}) collective-permute-start(f32[16,256]{1,0:T(8,128)S(1)} %get-tuple-element.37.refs_0_), channel_id=1, source_target_pairs={{0,2},{1,3},{2,0},{3,1},{4,6},{5,7},{6,4},{7,5},{8,10},{9,11},{10,... | collective-permute-start | bytes 49160 | tf_op jit(solution)/shard_map/ppermute | solution.py:399
  61.5 3.2 %collective-permute-start.21 = (f32[16,256]{1,0:T(8,128)S(1)}, f32[16,256]{1,0:T(8,128)S(1)}, u32[]{:S(2)}, u32[]{:S(2)}) collective-permute-start(f32[16,256]{1,0:T(8,128)S(1)} %get-tuple-element.37.refs_0_), channel_id=1, source_target_pairs={{0,3},{1,2},{2,1},{3,0},{4,7},{5,6},{6,5},{7,4},{8,11},{9,10},{10,... | collective-permute-start | bytes 49160 | tf_op jit(solution)/shard_map/ppermute | solution.py:399
  64.9 5.6 %collective-permute-start.24 = (f32[16,256]{1,0:T(8,128)S(1)}, f32[16,256]{1,0:T(8,128)S(1)}, u32[]{:S(2)}, u32[]{:S(2)}) collective-permute-start(f32[16,256]{1,0:T(8,128)S(1)} %get-tuple-element.49), channel_id=1, source_target_pairs={{0,12},{1,13},{2,14},{3,15},{4,8},{5,9},{6,10},{7,11},{8,4},{9,5},... | collective-permute-start | bytes 49160 | tf_op jit(solution)/shard_map/ppermute | solution.py:399
  67.4 3.7 %collective-permute-start.23 = (f32[16,256]{1,0:T(8,128)S(1)}, f32[16,256]{1,0:T(8,128)S(1)}, u32[]{:S(2)}, u32[]{:S(2)}) collective-permute-start(f32[16,256]{1,0:T(8,128)S(1)} %get-tuple-element.50), channel_id=1, source_target_pairs={{0,4},{1,5},{2,6},{3,7},{4,0},{5,1},{6,2},{7,3},{8,12},{9,13},{10,... | collective-permute-start | bytes 49160 | tf_op jit(solution)/shard_map/ppermute | solution.py:399
  67.4 4.6 %collective-permute-start.22 = (f32[16,256]{1,0:T(8,128)S(1)}, f32[16,256]{1,0:T(8,128)S(1)}, u32[]{:S(2)}, u32[]{:S(2)}) collective-permute-start(f32[16,256]{1,0:T(8,128)S(1)} %get-tuple-element.48), channel_id=1, source_target_pairs={{0,8},{1,9},{2,10},{3,11},{4,12},{5,13},{6,14},{7,15},{8,0},{9,1},... | collective-permute-start | bytes 49160 | tf_op jit(solution)/shard_map/ppermute | solution.py:399

commit v3 on v2

--- a/solution.py
+++ b/solution.py
@@ -94,7 +94,7 @@
         generator_bus, storage_bus, loads, factors, columns, demand, weights = refs[:7]
         stage, arrived, ids_a, ids_b, counts, small = refs[7:]
     else:
-        weights, factors, _, columns, demand, stage, arrived = refs
+        weights, factors, _, columns, demand = refs
     own = lax.axis_index("bus")
     member = own % QUAD
     few = []
@@ -103,26 +103,24 @@
             ((generator_bus, ids_a), (storage_bus, ids_b), (loads, counts))
         ):
             few.append(pltpu.make_async_copy(source, target, small.at[index]))
-    copies = []
-    for at, r in enumerate(wanted):
+    blocks = []
+    for r in wanted:
         for z in range(far):
             first = (z * QUAD + (member ^ r)) * own_lines
-            index = at * far + z
-            copies.append(
-                pltpu.make_async_copy(
-                    factors.at[pl.ds(pl.multiple_of(first, own_lines), own_lines)],
-                    stage.at[pl.ds(index * own_lines, own_lines)],
-                    arrived.at[index],
-                )
+            blocks.append(factors.at[pl.ds(pl.multiple_of(first, own_lines), own_lines)])
+    if first_call:
+        copies = [
+            pltpu.make_async_copy(
+                block, stage.at[pl.ds(index * own_lines, own_lines)], arrived.at[index]
             )
-    early = far if first_call else len(copies)
-    for copy in few + copies[:early]:
-        copy.start()
-    for copy in few:
-        copy.wait()
-    for copy in copies[early:]:
-        copy.start()
-    if first_call:
+            for index, block in enumerate(blocks)
+        ]
+        for copy in few + copies[:far]:
+            copy.start()
+        for copy in few:
+            copy.wait()
+        for copy in copies[far:]:
+            copy.start()
         weights[...] = build_weights(ids_a[...], ids_b[...], counts[...], own)
     rows_wanted = weights[...]
     horizon = rows_wanted.shape[0] - units
@@ -131,9 +129,15 @@
     per_tile = tile // own_lines
     for t in range(len(wanted) * quarter // tile):
         first = t * per_tile
-        for copy in copies[first : first + per_tile]:
-            copy.wait()
-        high, low = split_halves(stage[pl.ds(first * own_lines, tile), :])
+        if first_call:
+            for copy in copies[first : first + per_tile]:
+                copy.wait()
+            rows = stage[pl.ds(first * own_lines, tile), :]
+        else:
+            rows = jnp.concatenate(
+                [block[...] for block in blocks[first : first + per_tile]], axis=0
+            )
+        high, low = split_halves(rows)
         found = matmul(rows_wanted, high, rows_by_rows) + matmul(rows_wanted, low, rows_by_rows)
         at, lane = divmod(t * tile, quarter)
         spot = pl.ds(lane, tile)
@@ -152,19 +156,20 @@
         near_array((len(wanted) * units, quarter)),
         near_array((len(wanted) * horizon, quarter)),
     ]
-    scratch = [
-        pltpu.VMEM((copies * own_lines, factors.shape[1]), jnp.float32),
-        pltpu.SemaphoreType.DMA((copies,)),
-    ]
+    scratch = []
     if first_call:
+        scratch += [
+            pltpu.VMEM((copies * own_lines, factors.shape[1]), jnp.float32),
+            pltpu.SemaphoreType.DMA((copies,)),
+        ]
         in_specs = [distant] * 4
         arrays = [far_array(a) for a in (*sources, factors)]
         out_shape.append(near_array((units + horizon, factors.shape[1]), jnp.bfloat16))
         scratch += [pltpu.VMEM(a.shape, jnp.int32) for a in sources]
         scratch.append(pltpu.SemaphoreType.DMA((3,)))
     else:
-        in_specs = [whole_block, distant, pl.BlockSpec(memory_space=pl.ANY)]
-        arrays = [near(weights), far_array(factors), after]
+        in_specs = [whole_block, whole_block, pl.BlockSpec(memory_space=pl.ANY)]
+        arrays = [near(weights), near(factors), after]
     return pl.pallas_call(
         functools.partial(
             scan_kernel,
@@ -220,10 +225,13 @@
     rows = jnp.concatenate(rows, axis=0)
     state[...] = fold(spread(rows, QUAD, own % QUAD), state.shape[1])
     own_lines = jnp.concatenate([dual[...], limit[...]], axis=0)
-    lines[...] = spread(own_lines, lines.shape[1] // own_lines.shape[1], own // QUAD)
-
-
-def place(generation, charging, energy_dual, cost, ceiling, dual, limit, far):
+    if lines.shape == own_lines.shape:
+        lines[...] = own_lines
+    else:
+        lines[...] = spread(own_lines, lines.shape[1] // own_lines.shape[1], own // QUAD)
+
+
+def place(generation, charging, energy_dual, cost, ceiling, dual, limit, far, alone):
     horizon, gens = generation.shape
     quarter = far * dual.shape[1]
     pieces = (3 * horizon + 2 + 7) // 8
@@ -232,7 +240,10 @@
     return pl.pallas_call(
         place_kernel,
         out_specs=[whole_block] * 2,
-        out_shape=[near_array((8 * groups, quarter)), near_array((horizon + 1, quarter))],
+        out_shape=[
+            near_array((8 * groups, quarter)),
+            near_array((horizon + 1, dual.shape[1] if alone else quarter)),
+        ],
         compiler_params=grant,
         name="place",
     )(generation, charging, energy_dual, cost, ceiling, dual, limit)
@@ -246,8 +257,16 @@
     return parts[:horizon, :units] + parts[:horizon, units:] + parts[horizon:, :units]
 
 
-def gather_kernel(block0, block1, block2, block3, dual, columns, prices):
+def gather_kernel(block0, block1, block2, block3, *refs, hops):
+    parts, (lines, columns, prices) = refs[:-3], refs[-3:]
     horizon = prices.shape[0]
+    for hop, part in zip(hops, parts):
+        if part.shape == lines.shape:
+            lines[...] = part[...]
+        else:
+            width = part.shape[1]
+            first = pl.multiple_of((lax.axis_index("bus") // QUAD ^ hop) * width, width)
+            lines[:, pl.ds(first, width)] = part[...]
     units = columns.shape[0] // (2 * QUAD)
     group = units // 2
     member = lax.axis_index("bus") % QUAD
@@ -260,22 +279,24 @@
             first = first + QUAD * units
             spot = pl.ds(pl.multiple_of(first, group), group)
             columns[spot, :] = low[kind * group : (kind + 1) * group]
-    prices[...] = local_prices(dual[:horizon, :], columns[...])
-
-
-def gather_columns(blocks, dual, horizon):
+    prices[...] = local_prices(lines[:horizon, :], columns[...])
+
+
+def gather_columns(blocks, parts, hops, horizon):
     units, quarter = blocks[3].shape
+    arrays = [near(a) for a in (*blocks, *parts)]
     return pl.pallas_call(
-        gather_kernel,
-        in_specs=[whole_block] * 5,
-        out_specs=[whole_block] * 2,
+        functools.partial(gather_kernel, hops=hops),
+        in_specs=[whole_block] * len(arrays),
+        out_specs=[whole_block] * 3,
         out_shape=[
+            near_array((horizon + 1, quarter)),
             near_array((2 * QUAD * units, quarter), jnp.bfloat16),
             near_array((horizon, QUAD * units)),
         ],
         compiler_params=grant,
         name="gather_columns",
-    )(*[near(block) for block in blocks], near(dual))
+    )(*arrays)
 
 
 def unit_kernel(*refs, shares, order):
@@ -402,10 +423,10 @@
         return [bits[first : first + 2] for first in range(0, len(bits), 2)]
 
     def hops(bits):
-        found = [0]
-        for bit in bits if bits[0] < QUAD else reversed(bits):
-            found += [hop + bit for hop in found]
-        return found[1:]
+        if len(bits) < 2:
+            return list(bits)
+        low, high = bits
+        return [low + high, high, low] if low < QUAD else [high, low, low + high]
 
     def shares(values, bits):
         for group in pairs_of(bits):
@@ -415,6 +436,7 @@
             values = sum(parts)
         return parts
 
+    alone = own_lines % 128 == 0 and len(far_bits) <= 2
     units = 2 * own_units
     scan = functools.partial(
         scan_factors, shift_factors, own_lines, far, units, horizon
@@ -422,8 +444,8 @@
     other, demand_3_2, weights = scan(
         (3, 2), sources=(generator_bus[None, :], storage_bus[None, :], load_units.T)
     )
+    from_y = exchange(other[units:], 2)
     from_diagonal = exchange(other[:units], 3)
-    from_y = exchange(other[units:], 2)
     state, lines = place(
         generation.T,
         charging,
@@ -433,8 +455,13 @@
         flow_dual.T,
         line_max[None, :],
         far,
-    )
-    lines = sum(shares(lines, far_bits))
+        alone,
+    )
+    if alone:
+        line_parts, line_hops = shares(lines, far_bits), [0, *hops(far_bits)]
+        line_hops = [hop // QUAD for hop in line_hops]
+    else:
+        line_parts, line_hops = [sum(shares(lines, far_bits))], [0]
     rest, demand_0_1 = scan((0, 1), weights=weights, after=other)
     from_core = exchange(
         jnp.concatenate([rest[units:], demand_0_1[horizon:], demand_3_2[:horizon], state], axis=0),
@@ -452,7 +479,9 @@
         axis=1,
     )
 
-    columns, prices = gather_columns((rest, from_core, from_y, from_diagonal), lines, horizon)
+    lines, columns, prices = gather_columns(
+        (rest, from_core, from_y, from_diagonal), line_parts, line_hops, horizon
+    )
     for _ in range(ITERS - 1):
         state, flows = step_units(shares(prices, (1, 2)), state, bounds, columns, base_flow)
         lines, prices = step_lines(shares(flows, far_bits), lines, columns)

time: 72.8 us -> 73.2 us (level)
  local copies, waits for them, and re-layouts: 0.82 us -> 4.05 us
  Pallas kernels: 11.8 us -> 9.79 us
    unnamed x20 -> x22, local copies, waits for them, and re-layouts: 0.04 us -> 3.27 us
    pallas_call x2, Pallas kernels: 9.55 us -> 7.56 us  [scan_factors(): pl.pallas_call(functools.partial(scan_kernel, wanted=wanted, own_lines=ow...]
  transfers between devices with their start and end apart: 25 -> 25, of which waited for: 18 -> 17; matrix products, arithmetic and copies ran while one was open for 1% -> 1% of each run, Pallas kernels for 1% -> 1%
where the time goes in v3:
time: 73.2 us; the launch traced here: 73.1 us
  waiting for transfers between devices  29.4 us (40%)
  starting transfers between devices  28.2 us (39%)
  Pallas kernels  9.79 us (13%)
  local copies, waits for them, and re-layouts  4.05 us (6%)
  between operations  0.91 us (1%)
  other arithmetic  0.76 us (1%)
    ppermute x25, waiting for transfers between devices, exchange(): return lax.ppermute(values, 'bus', [(i, i ^ bit) for i in range(count)])  29.4 us
    ppermute x25, starting transfers between devices, exchange(): return lax.ppermute(values, 'bus', [(i, i ^ bit) for i in range(count)])  28.2 us
    pallas_call x2, Pallas kernels, scan_factors(): pl.pallas_call(functools.partial(scan_kernel, wanted=wanted, own_lines=ow...  7.56 us
    unnamed x22, local copies, waits for them, and re-layouts  3.27 us
  transfers between devices with their start and end apart: 25, of which 17 were waited for; matrix products, arithmetic and copies ran while one was open for 1% of the time, Pallas kernels for 1%

profile of v3, /device:TPU:0, one launch (start us, length us, event | category | flops | bytes accessed | tf_op | source)
XLA Modules:
  0.0 73.1 jit_solution(17513557972820370243)
XLA Ops:
  0.7 4.9 %scan_factors.2 = (f32[128,1024]{1,0:T(8,128)S(1)}, f32[32,1024]{1,0:T(8,128)S(1)}, bf16[80,1024]{1,0:T(8,128)(2,1)S(1)}) custom-call(s32[1,32]{1,0:T(1,128)} %bitcast.28, s32[1,32]{1,0:T(1,128)} %bitcast.29, s32[16,1024]{1,0:T(8,128)} %bitcast.22, f32[4096,1024]{1,0:T(8,128)} %refs_1_.1), custom_call_target="tpu_custom_call" | custom-call | tf_op jit(solution)/shard_map/scan_factors/pallas_call | solution.py:173
  5.7 3.2 %copy-done = f32[4096,1024]{1,0:T(8,128)S(1)} copy-done((f32[4096,1024]{1,0:T(8,128)S(1)}, f32[4096,1024]{1,0:T(8,128)}, u32[]{:S(2)}) %copy-start) | copy-done | bytes 16777240
  8.9 2.7 %scan_factors.3 = (f32[128,1024]{1,0:T(8,128)S(1)}, f32[32,1024]{1,0:T(8,128)S(1)}) custom-call(bf16[80,1024]{1,0:T(8,128)(2,1)S(1)} %get-tuple-element.24.refs_0_, f32[4096,1024]{1,0:T(8,128)S(1)} %copy-done, f32[128,1024]{1,0:T(8,128)S(1)} %get-tuple-element.25.refs_2_), custom_call_target="tpu_custom_call" | custom-call | tf_op jit(solution)/shard_map/scan_factors/pallas_call | solution.py:173
  11.7 0.1 place.1
  11.8 0.6 collective-permute-start
  12.4 3.6 %collective-permute-start.3 = (f32[17,256]{1,0:T(8,128)S(1)}, f32[17,256]{1,0:T(8,128)S(1)}, u32[]{:S(2)}, u32[]{:S(2)}) collective-permute-start(f32[17,256]{1,0:T(8,128)S(1)} %get-tuple-element.30.refs_0_), channel_id=1, source_target_pairs={{0,8},{1,9},{2,10},{3,11},{4,12},{5,13},{6,14},{7,15},{8,0},{9,1},... | collective-permute-start | bytes 52232 | tf_op jit(solution)/shard_map/ppermute | solution.py:420
  16.0 1.6 %collective-permute-start.4 = (f32[17,256]{1,0:T(8,128)S(1)}, f32[17,256]{1,0:T(8,128)S(1)}, u32[]{:S(2)}, u32[]{:S(2)}) collective-permute-start(f32[17,256]{1,0:T(8,128)S(1)} %get-tuple-element.30.refs_0_), channel_id=1, source_target_pairs={{0,4},{1,5},{2,6},{3,7},{4,0},{5,1},{6,2},{7,3},{8,12},{9,13},{10,... | collective-permute-start | bytes 52232 | tf_op jit(solution)/shard_map/ppermute | solution.py:420
  17.6 1.8 %collective-permute-start.1 = (f32[64,1024]{1,0:T(8,128)S(1)}, f32[64,1024]{1,0:T(8,128)S(1)}, u32[]{:S(2)}, u32[]{:S(2)}) collective-permute-start(f32[64,1024]{1,0:T(8,128)S(1)} %get-tuple-element.47), channel_id=1, source_target_pairs={{0,2},{1,3},{2,0},{3,1},{4,6},{5,7},{6,4},{7,5},{8,10},{9,11},{10,... | collective-permute-start | bytes 786440 | tf_op jit(solution)/shard_map/ppermute | solution.py:420
  19.5 1.1 %collective-permute-start.9 = (f32[24,1024]{1,0:T(8,128)S(1)}, f32[24,1024]{1,0:T(8,128)S(1)}, u32[]{:S(2)}, u32[]{:S(2)}) collective-permute-start(f32[24,1024]{1,0:T(8,128)S(1)} %slice_add_fusion), channel_id=1, source_target_pairs={{0,2},{1,3},{2,0},{3,1},{4,6},{5,7},{6,4},{7,5},{8,10},{9,11},{10,... | collective-permute-start | bytes 294920 | tf_op jit(solution)/shard_map/ppermute | solution.py:420
  20.6 0.1 fusion.1.refs_5_
  20.6 2.6 %collective-permute-done.5.refs_3_ = f32[17,256]{1,0:T(8,128)S(1)} collective-permute-done((f32[17,256]{1,0:T(8,128)S(1)}, f32[17,256]{1,0:T(8,128)S(1)}, u32[]{:S(2)}, u32[]{:S(2)}) %collective-permute-start.5) | collective-permute-done | bytes 17440 | tf_op jit(solution)/shard_map/ppermute | solution.py:420
  23.2 3.7 %collective-permute-done.1.block2 = f32[64,1024]{1,0:T(8,128)S(1)} collective-permute-done((f32[64,1024]{1,0:T(8,128)S(1)}, f32[64,1024]{1,0:T(8,128)S(1)}, u32[]{:S(2)}, u32[]{:S(2)}) %collective-permute-start.1) | collective-permute-done | bytes 262176 | tf_op jit(solution)/shard_map/ppermute | solution.py:420
  26.9 4.6 %collective-permute-done.2.block3 = f32[64,1024]{1,0:T(8,128)S(1)} collective-permute-done((f32[64,1024]{1,0:T(8,128)S(1)}, f32[64,1024]{1,0:T(8,128)S(1)}, u32[]{:S(2)}, u32[]{:S(2)}) %collective-permute-start.2) | collective-permute-done | bytes 262176 | tf_op jit(solution)/shard_map/ppermute | solution.py:420
  31.5 0.6 gather_columns.1
  32.1 2.0 %collective-permute-start.6 = (f32[16,256]{1,0:T(8,128)S(1)}, f32[16,256]{1,0:T(8,128)S(1)}, u32[]{:S(2)}, u32[]{:S(2)}) collective-permute-start(f32[16,256]{1,0:T(8,128)S(1)} %get-tuple-element.31.refs_0_), channel_id=1, source_target_pairs={{0,3},{1,2},{2,1},{3,0},{4,7},{5,6},{6,5},{7,4},{8,11},{9,10},{10,... | collective-permute-start | bytes 49160 | tf_op jit(solution)/shard_map/ppermute | solution.py:420
  34.0 0.5 collective-permute-start.7
  34.6 0.9 %collective-permute-done.6.refs_1_ = f32[16,256]{1,0:T(8,128)S(1)} collective-permute-done((f32[16,256]{1,0:T(8,128)S(1)}, f32[16,256]{1,0:T(8,128)S(1)}, u32[]{:S(2)}, u32[]{:S(2)}) %collective-permute-start.6) | collective-permute-done | bytes 16416 | tf_op jit(solution)/shard_map/ppermute | solution.py:420
  35.5 2.3 %collective-permute-done.7.refs_2_ = f32[16,256]{1,0:T(8,128)S(1)} collective-permute-done((f32[16,256]{1,0:T(8,128)S(1)}, f32[16,256]{1,0:T(8,128)S(1)}, u32[]{:S(2)}, u32[]{:S(2)}) %collective-permute-start.7) | collective-permute-done | bytes 16416 | tf_op jit(solution)/shard_map/ppermute | solution.py:420
  37.8 0.3 step_units.3
  38.1 1.6 %collective-permute-start.10 = (f32[16,1024]{1,0:T(8,128)S(1)}, f32[16,1024]{1,0:T(8,128)S(1)}, u32[]{:S(2)}, u32[]{:S(2)}) collective-permute-start(f32[16,1024]{1,0:T(8,128)S(1)} %get-tuple-element.33.refs_0_), channel_id=1, source_target_pairs={{0,8},{1,9},{2,10},{3,11},{4,12},{5,13},{6,14},{7,15},{8,0},{9,1},... | collective-permute-start | bytes 196616 | tf_op jit(solution)/shard_map/ppermute | solution.py:420
  39.7 2.5 %collective-permute-start.11 = (f32[16,1024]{1,0:T(8,128)S(1)}, f32[16,1024]{1,0:T(8,128)S(1)}, u32[]{:S(2)}, u32[]{:S(2)}) collective-permute-start(f32[16,1024]{1,0:T(8,128)S(1)} %get-tuple-element.33.refs_0_), channel_id=1, source_target_pairs={{0,4},{1,5},{2,6},{3,7},{4,0},{5,1},{6,2},{7,3},{8,12},{9,13},{10,... | collective-permute-start | bytes 196616 | tf_op jit(solution)/shard_map/ppermute | solution.py:420
  42.2 0.3 collective-permute-start.12
  42.5 2.0 %collective-permute-done.10.refs_1_ = f32[16,1024]{1,0:T(8,128)S(1)} collective-permute-done((f32[16,1024]{1,0:T(8,128)S(1)}, f32[16,1024]{1,0:T(8,128)S(1)}, u32[]{:S(2)}, u32[]{:S(2)}) %collective-permute-start.10) | collective-permute-done | bytes 65568 | tf_op jit(solution)/shard_map/ppermute | solution.py:420
  44.5 1.0 %collective-permute-done.11.refs_2_ = f32[16,1024]{1,0:T(8,128)S(1)} collective-permute-done((f32[16,1024]{1,0:T(8,128)S(1)}, f32[16,1024]{1,0:T(8,128)S(1)}, u32[]{:S(2)}, u32[]{:S(2)}) %collective-permute-start.11) | collective-permute-done | bytes 65568 | tf_op jit(solution)/shard_map/ppermute | solution.py:420
  45.5 2.8 %collective-permute-done.12.refs_3_ = f32[16,1024]{1,0:T(8,128)S(1)} collective-permute-done((f32[16,1024]{1,0:T(8,128)S(1)}, f32[16,1024]{1,0:T(8,128)S(1)}, u32[]{:S(2)}, u32[]{:S(2)}) %collective-permute-start.12) | collective-permute-done | bytes 65568 | tf_op jit(solution)/shard_map/ppermute | solution.py:420
  48.2 0.4 step_lines.2
  48.7 0.6 collective-permute-start.14
  49.2 1.3 %collective-permute-start.15 = (f32[16,256]{1,0:T(8,128)S(1)}, f32[16,256]{1,0:T(8,128)S(1)}, u32[]{:S(2)}, u32[]{:S(2)}) collective-permute-start(f32[16,256]{1,0:T(8,128)S(1)} %get-tuple-element.35.refs_0_), channel_id=1, source_target_pairs={{0,1},{1,0},{2,3},{3,2},{4,5},{5,4},{6,7},{7,6},{8,9},{9,8},{10,11... | collective-permute-start | bytes 49160 | tf_op jit(solution)/shard_map/ppermute | solution.py:420
  50.5 1.3 %collective-permute-done.13.refs_1_ = f32[16,256]{1,0:T(8,128)S(1)} collective-permute-done((f32[16,256]{1,0:T(8,128)S(1)}, f32[16,256]{1,0:T(8,128)S(1)}, u32[]{:S(2)}, u32[]{:S(2)}) %collective-permute-start.13) | collective-permute-done | bytes 16416 | tf_op jit(solution)/shard_map/ppermute | solution.py:420
  51.8 0.6 collective-permute-done.14.refs_2_
  52.5 0.3 step_units.4
  52.8 1.3 %collective-permute-start.17 = (f32[16,1024]{1,0:T(8,128)S(1)}, f32[16,1024]{1,0:T(8,128)S(1)}, u32[]{:S(2)}, u32[]{:S(2)}) collective-permute-start(f32[16,1024]{1,0:T(8,128)S(1)} %get-tuple-element.37.refs_0_), channel_id=1, source_target_pairs={{0,4},{1,5},{2,6},{3,7},{4,0},{5,1},{6,2},{7,3},{8,12},{9,13},{10,... | collective-permute-start | bytes 196616 | tf_op jit(solution)/shard_map/ppermute | solution.py:420
  54.0 3.1 %collective-permute-start.18 = (f32[16,1024]{1,0:T(8,128)S(1)}, f32[16,1024]{1,0:T(8,128)S(1)}, u32[]{:S(2)}, u32[]{:S(2)}) collective-permute-start(f32[16,1024]{1,0:T(8,128)S(1)} %get-tuple-element.37.refs_0_), channel_id=1, source_target_pairs={{0,12},{1,13},{2,14},{3,15},{4,8},{5,9},{6,10},{7,11},{8,4},{9,5},... | collective-permute-start | bytes 196616 | tf_op jit(solution)/shard_map/ppermute | solution.py:420
  57.2 1.5 %collective-permute-done.16.refs_1_ = f32[16,1024]{1,0:T(8,128)S(1)} collective-permute-done((f32[16,1024]{1,0:T(8,128)S(1)}, f32[16,1024]{1,0:T(8,128)S(1)}, u32[]{:S(2)}, u32[]{:S(2)}) %collective-permute-start.16) | collective-permute-done | bytes 65568 | tf_op jit(solution)/shard_map/ppermute | solution.py:420
  58.7 1.4 %collective-permute-done.18.refs_3_ = f32[16,1024]{1,0:T(8,128)S(1)} collective-permute-done((f32[16,1024]{1,0:T(8,128)S(1)}, f32[16,1024]{1,0:T(8,128)S(1)}, u32[]{:S(2)}, u32[]{:S(2)}) %collective-permute-start.18) | collective-permute-done | bytes 65568 | tf_op jit(solution)/shard_map/ppermute | solution.py:420
  60.1 0.4 step_lines.3
  60.5 1.1 %collective-permute-start.20 = (f32[16,256]{1,0:T(8,128)S(1)}, f32[16,256]{1,0:T(8,128)S(1)}, u32[]{:S(2)}, u32[]{:S(2)}) collective-permute-start(f32[16,256]{1,0:T(8,128)S(1)} %get-tuple-element.39.refs_0_), channel_id=1, source_target_pairs={{0,2},{1,3},{2,0},{3,1},{4,6},{5,7},{6,4},{7,5},{8,10},{9,11},{10,... | collective-permute-start | bytes 49160 | tf_op jit(solution)/shard_map/ppermute | solution.py:420
  61.7 0.7 collective-permute-start.21
  62.4 1.3 %collective-permute-done.19.refs_1_ = f32[16,256]{1,0:T(8,128)S(1)} collective-permute-done((f32[16,256]{1,0:T(8,128)S(1)}, f32[16,256]{1,0:T(8,128)S(1)}, u32[]{:S(2)}, u32[]{:S(2)}) %collective-permute-start.19) | collective-permute-done | bytes 16416 | tf_op jit(solution)/shard_map/ppermute | solution.py:420
  63.7 0.7 collective-permute-done.20.refs_2_
  64.4 0.3 step_units.5
  64.7 3.1 %collective-permute-start.24 = (f32[16,256]{1,0:T(8,128)S(1)}, f32[16,256]{1,0:T(8,128)S(1)}, u32[]{:S(2)}, u32[]{:S(2)}) collective-permute-start(f32[16,256]{1,0:T(8,128)S(1)} %get-tuple-element.51), channel_id=1, source_target_pairs={{0,12},{1,13},{2,14},{3,15},{4,8},{5,9},{6,10},{7,11},{8,4},{9,5},... | collective-permute-start | bytes 49160 | tf_op jit(solution)/shard_map/ppermute | solution.py:420
  67.8 1.3 %collective-permute-start.22 = (f32[16,256]{1,0:T(8,128)S(1)}, f32[16,256]{1,0:T(8,128)S(1)}, u32[]{:S(2)}, u32[]{:S(2)}) collective-permute-start(f32[16,256]{1,0:T(8,128)S(1)} %get-tuple-element.50), channel_id=1, source_target_pairs={{0,8},{1,9},{2,10},{3,11},{4,12},{5,13},{6,14},{7,15},{8,0},{9,1},... | collective-permute-start | bytes 49160 | tf_op jit(solution)/shard_map/ppermute | solution.py:420
  69.1 0.7 fusion.6
  69.8 0.5 collective-permute-done.24
  70.3 1.3 %collective-permute-done.23 = f32[16,256]{1,0:T(8,128)S(1)} collective-permute-done((f32[16,256]{1,0:T(8,128)S(1)}, f32[16,256]{1,0:T(8,128)S(1)}, u32[]{:S(2)}, u32[]{:S(2)}) %collective-permute-start.23) | collective-permute-done | bytes 16416 | tf_op jit(solution)/shard_map/ppermute | solution.py:420
  71.6 0.9 %collective-permute-done.22 = f32[16,256]{1,0:T(8,128)S(1)} collective-permute-done((f32[16,256]{1,0:T(8,128)S(1)}, f32[16,256]{1,0:T(8,128)S(1)}, u32[]{:S(2)}, u32[]{:S(2)}) %collective-permute-start.22) | collective-permute-done | bytes 16416 | tf_op jit(solution)/shard_map/ppermute | solution.py:420
  72.5 0.6 subtract_bitcast_fusion
  (48 shorter events, 0.3 us)
Async XLA Ops:
  0.6 8.3 %copy-start = (f32[4096,1024]{1,0:T(8,128)S(1)}, f32[4096,1024]{1,0:T(8,128)}, u32[]{:S(2)}) copy-start(f32[4096,1024]{1,0:T(8,128)} %refs_1_.1) | copy-start | bytes 50331652
  0.6 11.0 %copy-start.1 = (f32[256,16]{0,1:T(8,128)S(1)}, f32[256,16]{0,1:T(8,128)}, u32[]{:S(2)}) copy-start(f32[256,16]{0,1:T(8,128)} %param.16) | copy-start | bytes 49156
  0.7 11.0 %copy-start.2 = (f32[32,16]{0,1:T(8,128)S(1)}, f32[32,16]{0,1:T(8,128)}, u32[]{:S(2)}) copy-start(f32[32,16]{0,1:T(8,128)} %param.14) | copy-start | bytes 6148
  0.7 11.0 %copy-start.3 = (f32[16,32]{1,0:T(8,128)S(1)}, f32[16,32]{1,0:T(8,128)}, u32[]{:S(2)}) copy-start(f32[16,32]{1,0:T(8,128)} %charging.1) | copy-start | bytes 6148
  0.7 11.0 %copy-start.4 = (f32[16,32]{1,0:T(8,128)S(1)}, f32[16,32]{1,0:T(8,128)}, u32[]{:S(2)}) copy-start(f32[16,32]{1,0:T(8,128)} %energy_dual.1) | copy-start | bytes 6148
  0.7 11.0 %copy-start.5 = (f32[256]{0:T(256)S(1)}, f32[256]{0:T(256)}, u32[]{:S(2)}) copy-start(f32[256]{0:T(256)} %param.27) | copy-start | bytes 3076
  0.7 11.0 %copy-start.6 = (f32[32]{0:T(128)S(1)}, f32[32]{0:T(128)}, u32[]{:S(2)}) copy-start(f32[32]{0:T(128)} %param.22) | copy-start | bytes 388
  0.7 11.0 %copy-start.7 = (f32[32]{0:T(128)S(1)}, f32[32]{0:T(128)}, u32[]{:S(2)}) copy-start(f32[32]{0:T(128)} %param.23) | copy-start | bytes 388
  0.7 19.8 %copy-start.8 = (f32[512]{0:T(512)S(1)}, f32[512]{0:T(512)}, u32[]{:S(2)}) copy-start(f32[512]{0:T(512)} %param.24) | copy-start | bytes 6148
  0.7 19.8 %copy-start.9 = (f32[512]{0:T(512)S(1)}, f32[512]{0:T(512)}, u32[]{:S(2)}) copy-start(f32[512]{0:T(512)} %param.25) | copy-start | bytes 6148
  0.7 19.8 %copy-start.10 = (f32[512]{0:T(512)S(1)}, f32[512]{0:T(512)}, u32[]{:S(2)}) copy-start(f32[512]{0:T(512)} %param.26) | copy-start | bytes 6148
  11.8 7.6 %collective-permute-start = (f32[104,1024]{1,0:T(8,128)S(1)}, f32[104,1024]{1,0:T(8,128)S(1)}, u32[]{:S(2)}, u32[]{:S(2)}) collective-permute-start(f32[104,1024]{1,0:T(8,128)S(1)} %pad_maximum_fusion), channel_id=1, source_target_pairs={{0,1},{1,0},{2,3},{3,2},{4,5},{5,4},{6,7},{7,6},{8,9},{9,8},{10,11... | collective-permute-start | bytes 1277960 | tf_op jit(solution)/shard_map/ppermute | solution.py:420
  12.4 7.1 %collective-permute-start.3 = (f32[17,256]{1,0:T(8,128)S(1)}, f32[17,256]{1,0:T(8,128)S(1)}, u32[]{:S(2)}, u32[]{:S(2)}) collective-permute-start(f32[17,256]{1,0:T(8,128)S(1)} %get-tuple-element.30.refs_0_), channel_id=1, source_target_pairs={{0,8},{1,9},{2,10},{3,11},{4,12},{5,13},{6,14},{7,15},{8,0},{9,1},... | collective-permute-start | bytes 52232 | tf_op jit(solution)/shard_map/ppermute | solution.py:420
  16.0 4.6 %collective-permute-start.4 = (f32[17,256]{1,0:T(8,128)S(1)}, f32[17,256]{1,0:T(8,128)S(1)}, u32[]{:S(2)}, u32[]{:S(2)}) collective-permute-start(f32[17,256]{1,0:T(8,128)S(1)} %get-tuple-element.30.refs_0_), channel_id=1, source_target_pairs={{0,4},{1,5},{2,6},{3,7},{4,0},{5,1},{6,2},{7,3},{8,12},{9,13},{10,... | collective-permute-start | bytes 52232 | tf_op jit(solution)/shard_map/ppermute | solution.py:420
  17.6 5.6 %collective-permute-start.5 = (f32[17,256]{1,0:T(8,128)S(1)}, f32[17,256]{1,0:T(8,128)S(1)}, u32[]{:S(2)}, u32[]{:S(2)}) collective-permute-start(f32[17,256]{1,0:T(8,128)S(1)} %get-tuple-element.30.refs_0_), channel_id=1, source_target_pairs={{0,12},{1,13},{2,14},{3,15},{4,8},{5,9},{6,10},{7,11},{8,4},{9,5},... | collective-permute-start | bytes 52232 | tf_op jit(solution)/shard_map/ppermute | solution.py:420
  17.6 9.2 %collective-permute-start.1 = (f32[64,1024]{1,0:T(8,128)S(1)}, f32[64,1024]{1,0:T(8,128)S(1)}, u32[]{:S(2)}, u32[]{:S(2)}) collective-permute-start(f32[64,1024]{1,0:T(8,128)S(1)} %get-tuple-element.47), channel_id=1, source_target_pairs={{0,2},{1,3},{2,0},{3,1},{4,6},{5,7},{6,4},{7,5},{8,10},{9,11},{10,... | collective-permute-start | bytes 786440 | tf_op jit(solution)/shard_map/ppermute | solution.py:420
  19.4 12.1 %collective-permute-start.2 = (f32[64,1024]{1,0:T(8,128)S(1)}, f32[64,1024]{1,0:T(8,128)S(1)}, u32[]{:S(2)}, u32[]{:S(2)}) collective-permute-start(f32[64,1024]{1,0:T(8,128)S(1)} %get-tuple-element.46), channel_id=1, source_target_pairs={{0,3},{1,2},{2,1},{3,0},{4,7},{5,6},{6,5},{7,4},{8,11},{9,10},{10,... | collective-permute-start | bytes 786440 | tf_op jit(solution)/shard_map/ppermute | solution.py:420
  19.5 15.1 %collective-permute-start.9 = (f32[24,1024]{1,0:T(8,128)S(1)}, f32[24,1024]{1,0:T(8,128)S(1)}, u32[]{:S(2)}, u32[]{:S(2)}) collective-permute-start(f32[24,1024]{1,0:T(8,128)S(1)} %slice_add_fusion), channel_id=1, source_target_pairs={{0,2},{1,3},{2,0},{3,1},{4,6},{5,7},{6,4},{7,5},{8,10},{9,11},{10,... | collective-permute-start | bytes 294920 | tf_op jit(solution)/shard_map/ppermute | solution.py:420
  32.1 3.4 %collective-permute-start.6 = (f32[16,256]{1,0:T(8,128)S(1)}, f32[16,256]{1,0:T(8,128)S(1)}, u32[]{:S(2)}, u32[]{:S(2)}) collective-permute-start(f32[16,256]{1,0:T(8,128)S(1)} %get-tuple-element.31.refs_0_), channel_id=1, source_target_pairs={{0,3},{1,2},{2,1},{3,0},{4,7},{5,6},{6,5},{7,4},{8,11},{9,10},{10,... | collective-permute-start | bytes 49160 | tf_op jit(solution)/shard_map/ppermute | solution.py:420
  34.0 3.7 %collective-permute-start.7 = (f32[16,256]{1,0:T(8,128)S(1)}, f32[16,256]{1,0:T(8,128)S(1)}, u32[]{:S(2)}, u32[]{:S(2)}) collective-permute-start(f32[16,256]{1,0:T(8,128)S(1)} %get-tuple-element.31.refs_0_), channel_id=1, source_target_pairs={{0,2},{1,3},{2,0},{3,1},{4,6},{5,7},{6,4},{7,5},{8,10},{9,11},{10,... | collective-permute-start | bytes 49160 | tf_op jit(solution)/shard_map/ppermute | solution.py:420
  34.6 3.2 %collective-permute-start.8 = (f32[16,256]{1,0:T(8,128)S(1)}, f32[16,256]{1,0:T(8,128)S(1)}, u32[]{:S(2)}, u32[]{:S(2)}) collective-permute-start(f32[16,256]{1,0:T(8,128)S(1)} %get-tuple-element.31.refs_0_), channel_id=1, source_target_pairs={{0,1},{1,0},{2,3},{3,2},{4,5},{5,4},{6,7},{7,6},{8,9},{9,8},{10,11... | collective-permute-start | bytes 49160 | tf_op jit(solution)/shard_map/ppermute | solution.py:420
  38.1 6.4 %collective-permute-start.10 = (f32[16,1024]{1,0:T(8,128)S(1)}, f32[16,1024]{1,0:T(8,128)S(1)}, u32[]{:S(2)}, u32[]{:S(2)}) collective-permute-start(f32[16,1024]{1,0:T(8,128)S(1)} %get-tuple-element.33.refs_0_), channel_id=1, source_target_pairs={{0,8},{1,9},{2,10},{3,11},{4,12},{5,13},{6,14},{7,15},{8,0},{9,1},... | collective-permute-start | bytes 196616 | tf_op jit(solution)/shard_map/ppermute | solution.py:420
  39.7 5.8 %collective-permute-start.11 = (f32[16,1024]{1,0:T(8,128)S(1)}, f32[16,1024]{1,0:T(8,128)S(1)}, u32[]{:S(2)}, u32[]{:S(2)}) collective-permute-start(f32[16,1024]{1,0:T(8,128)S(1)} %get-tuple-element.33.refs_0_), channel_id=1, source_target_pairs={{0,4},{1,5},{2,6},{3,7},{4,0},{5,1},{6,2},{7,3},{8,12},{9,13},{10,... | collective-permute-start | bytes 196616 | tf_op jit(solution)/shard_map/ppermute | solution.py:420
  42.2 6.1 %collective-permute-start.12 = (f32[16,1024]{1,0:T(8,128)S(1)}, f32[16,1024]{1,0:T(8,128)S(1)}, u32[]{:S(2)}, u32[]{:S(2)}) collective-permute-start(f32[16,1024]{1,0:T(8,128)S(1)} %get-tuple-element.33.refs_0_), channel_id=1, source_target_pairs={{0,12},{1,13},{2,14},{3,15},{4,8},{5,9},{6,10},{7,11},{8,4},{9,5},... | collective-permute-start | bytes 196616 | tf_op jit(solution)/shard_map/ppermute | solution.py:420
  48.6 3.2 %collective-permute-start.13 = (f32[16,256]{1,0:T(8,128)S(1)}, f32[16,256]{1,0:T(8,128)S(1)}, u32[]{:S(2)}, u32[]{:S(2)}) collective-permute-start(f32[16,256]{1,0:T(8,128)S(1)} %get-tuple-element.35.refs_0_), channel_id=1, source_target_pairs={{0,3},{1,2},{2,1},{3,0},{4,7},{5,6},{6,5},{7,4},{8,11},{9,10},{10,... | collective-permute-start | bytes 49160 | tf_op jit(solution)/shard_map/ppermute | solution.py:420
  48.7 3.8 %collective-permute-start.14 = (f32[16,256]{1,0:T(8,128)S(1)}, f32[16,256]{1,0:T(8,128)S(1)}, u32[]{:S(2)}, u32[]{:S(2)}) collective-permute-start(f32[16,256]{1,0:T(8,128)S(1)} %get-tuple-element.35.refs_0_), channel_id=1, source_target_pairs={{0,2},{1,3},{2,0},{3,1},{4,6},{5,7},{6,4},{7,5},{8,10},{9,11},{10,... | collective-permute-start | bytes 49160 | tf_op jit(solution)/shard_map/ppermute | solution.py:420
  49.2 3.2 %collective-permute-start.15 = (f32[16,256]{1,0:T(8,128)S(1)}, f32[16,256]{1,0:T(8,128)S(1)}, u32[]{:S(2)}, u32[]{:S(2)}) collective-permute-start(f32[16,256]{1,0:T(8,128)S(1)} %get-tuple-element.35.refs_0_), channel_id=1, source_target_pairs={{0,1},{1,0},{2,3},{3,2},{4,5},{5,4},{6,7},{7,6},{8,9},{9,8},{10,11... | collective-permute-start | bytes 49160 | tf_op jit(solution)/shard_map/ppermute | solution.py:420
  52.8 6.0 %collective-permute-start.16 = (f32[16,1024]{1,0:T(8,128)S(1)}, f32[16,1024]{1,0:T(8,128)S(1)}, u32[]{:S(2)}, u32[]{:S(2)}) collective-permute-start(f32[16,1024]{1,0:T(8,128)S(1)} %get-tuple-element.37.refs_0_), channel_id=1, source_target_pairs={{0,8},{1,9},{2,10},{3,11},{4,12},{5,13},{6,14},{7,15},{8,0},{9,1},... | collective-permute-start | bytes 196616 | tf_op jit(solution)/shard_map/ppermute | solution.py:420
  52.8 6.0 %collective-permute-start.17 = (f32[16,1024]{1,0:T(8,128)S(1)}, f32[16,1024]{1,0:T(8,128)S(1)}, u32[]{:S(2)}, u32[]{:S(2)}) collective-permute-start(f32[16,1024]{1,0:T(8,128)S(1)} %get-tuple-element.37.refs_0_), channel_id=1, source_target_pairs={{0,4},{1,5},{2,6},{3,7},{4,0},{5,1},{6,2},{7,3},{8,12},{9,13},{10,... | collective-permute-start | bytes 196616 | tf_op jit(solution)/shard_map/ppermute | solution.py:420
  54.0 6.1 %collective-permute-start.18 = (f32[16,1024]{1,0:T(8,128)S(1)}, f32[16,1024]{1,0:T(8,128)S(1)}, u32[]{:S(2)}, u32[]{:S(2)}) collective-permute-start(f32[16,1024]{1,0:T(8,128)S(1)} %get-tuple-element.37.refs_0_), channel_id=1, source_target_pairs={{0,12},{1,13},{2,14},{3,15},{4,8},{5,9},{6,10},{7,11},{8,4},{9,5},... | collective-permute-start | bytes 196616 | tf_op jit(solution)/shard_map/ppermute | solution.py:420
  60.5 3.2 %collective-permute-start.19 = (f32[16,256]{1,0:T(8,128)S(1)}, f32[16,256]{1,0:T(8,128)S(1)}, u32[]{:S(2)}, u32[]{:S(2)}) collective-permute-start(f32[16,256]{1,0:T(8,128)S(1)} %get-tuple-element.39.refs_0_), channel_id=1, source_target_pairs={{0,3},{1,2},{2,1},{3,0},{4,7},{5,6},{6,5},{7,4},{8,11},{9,10},{10,... | collective-permute-start | bytes 49160 | tf_op jit(solution)/shard_map/ppermute | solution.py:420
  60.5 3.8 %collective-permute-start.20 = (f32[16,256]{1,0:T(8,128)S(1)}, f32[16,256]{1,0:T(8,128)S(1)}, u32[]{:S(2)}, u32[]{:S(2)}) collective-permute-start(f32[16,256]{1,0:T(8,128)S(1)} %get-tuple-element.39.refs_0_), channel_id=1, source_target_pairs={{0,2},{1,3},{2,0},{3,1},{4,6},{5,7},{6,4},{7,5},{8,10},{9,11},{10,... | collective-permute-start | bytes 49160 | tf_op jit(solution)/shard_map/ppermute | solution.py:420
  61.7 2.7 %collective-permute-start.21 = (f32[16,256]{1,0:T(8,128)S(1)}, f32[16,256]{1,0:T(8,128)S(1)}, u32[]{:S(2)}, u32[]{:S(2)}) collective-permute-start(f32[16,256]{1,0:T(8,128)S(1)} %get-tuple-element.39.refs_0_), channel_id=1, source_target_pairs={{0,1},{1,0},{2,3},{3,2},{4,5},{5,4},{6,7},{7,6},{8,9},{9,8},{10,11... | collective-permute-start | bytes 49160 | tf_op jit(solution)/shard_map/ppermute | solution.py:420
  64.7 5.6 %collective-permute-start.24 = (f32[16,256]{1,0:T(8,128)S(1)}, f32[16,256]{1,0:T(8,128)S(1)}, u32[]{:S(2)}, u32[]{:S(2)}) collective-permute-start(f32[16,256]{1,0:T(8,128)S(1)} %get-tuple-element.51), channel_id=1, source_target_pairs={{0,12},{1,13},{2,14},{3,15},{4,8},{5,9},{6,10},{7,11},{8,4},{9,5},... | collective-permute-start | bytes 49160 | tf_op jit(solution)/shard_map/ppermute | solution.py:420
  67.8 3.7 %collective-permute-start.23 = (f32[16,256]{1,0:T(8,128)S(1)}, f32[16,256]{1,0:T(8,128)S(1)}, u32[]{:S(2)}, u32[]{:S(2)}) collective-permute-start(f32[16,256]{1,0:T(8,128)S(1)} %get-tuple-element.52), channel_id=1, source_target_pairs={{0,4},{1,5},{2,6},{3,7},{4,0},{5,1},{6,2},{7,3},{8,12},{9,13},{10,... | collective-permute-start | bytes 49160 | tf_op jit(solution)/shard_map/ppermute | solution.py:420
  67.8 4.6 %collective-permute-start.22 = (f32[16,256]{1,0:T(8,128)S(1)}, f32[16,256]{1,0:T(8,128)S(1)}, u32[]{:S(2)}, u32[]{:S(2)}) collective-permute-start(f32[16,256]{1,0:T(8,128)S(1)} %get-tuple-element.50), channel_id=1, source_target_pairs={{0,8},{1,9},{2,10},{3,11},{4,12},{5,13},{6,14},{7,15},{8,0},{9,1},... | collective-permute-start | bytes 49160 | tf_op jit(solution)/shard_map/ppermute | solution.py:420

commit v4 on v3

--- a/solution.py
+++ b/solution.py
@@ -428,10 +428,10 @@
         low, high = bits
         return [low + high, high, low] if low < QUAD else [high, low, low + high]
 
-    def shares(values, bits):
+    def shares(values, bits, listed=()):
         for group in pairs_of(bits):
             parts = [values]
-            for hop in hops(group):
+            for hop in listed or hops(group):
                 parts.append(exchange(values, hop))
             values = sum(parts)
         return parts
@@ -482,8 +482,10 @@
     lines, columns, prices = gather_columns(
         (rest, from_core, from_y, from_diagonal), line_parts, line_hops, horizon
     )
-    for _ in range(ITERS - 1):
-        state, flows = step_units(shares(prices, (1, 2)), state, bounds, columns, base_flow)
+    for iteration in range(ITERS - 1):
+        state, flows = step_units(
+            shares(prices, (1, 2), (2, 3, 1) if iteration == 0 else ()), state, bounds, columns, base_flow
+        )
         lines, prices = step_lines(shares(flows, far_bits), lines, columns)
     mine = lambda a: lax.dynamic_slice_in_dim(a, place_of_quad * own_lines, own_lines, axis=1)
     if own_lines % 128 == 0:

time: 73.2 us -> 72.1 us (0.985)
  waiting for transfers between devices: 29.4 us -> 28.5 us
    ppermute x25, waiting for transfers between devices: 29.4 us -> 28.5 us  [exchange(): return lax.ppermute(values, 'bus', [(i, i ^ bit) for i in range(count)])]
where the time goes in v4:
time: 72.1 us; the launch traced here: 72 us
  waiting for transfers between devices  28.5 us (40%)
  starting transfers between devices  27.9 us (39%)
  Pallas kernels  9.79 us (14%)
  local copies, waits for them, and re-layouts  4.05 us (6%)
  between operations  0.91 us (1%)
  other arithmetic  0.76 us (1%)
    ppermute x25, waiting for transfers between devices, exchange(): return lax.ppermute(values, 'bus', [(i, i ^ bit) for i in range(count)])  28.5 us
    ppermute x25, starting transfers between devices, exchange(): return lax.ppermute(values, 'bus', [(i, i ^ bit) for i in range(count)])  27.9 us
    pallas_call x2, Pallas kernels, scan_factors(): pl.pallas_call(functools.partial(scan_kernel, wanted=wanted, own_lines=ow...  7.56 us
    unnamed x22, local copies, waits for them, and re-layouts  3.27 us
  transfers between devices with their start and end apart: 25, of which 17 were waited for; matrix products, arithmetic and copies ran while one was open for 1% of the time, Pallas kernels for 1%

profile of v4, /device:TPU:0, one launch (start us, length us, event | category | flops | bytes accessed | tf_op | source)
XLA Modules:
  0.0 72.0 jit_solution(3370729583979988766)
XLA Ops:
  0.7 4.9 %scan_factors.2 = (f32[128,1024]{1,0:T(8,128)S(1)}, f32[32,1024]{1,0:T(8,128)S(1)}, bf16[80,1024]{1,0:T(8,128)(2,1)S(1)}) custom-call(s32[1,32]{1,0:T(1,128)} %bitcast.28, s32[1,32]{1,0:T(1,128)} %bitcast.29, s32[16,1024]{1,0:T(8,128)} %bitcast.22, f32[4096,1024]{1,0:T(8,128)} %refs_1_.1), custom_call_target="tpu_custom_call" | custom-call | tf_op jit(solution)/shard_map/scan_factors/pallas_call | solution.py:173
  5.7 3.2 %copy-done = f32[4096,1024]{1,0:T(8,128)S(1)} copy-done((f32[4096,1024]{1,0:T(8,128)S(1)}, f32[4096,1024]{1,0:T(8,128)}, u32[]{:S(2)}) %copy-start) | copy-done | bytes 16777240
  8.9 2.7 %scan_factors.3 = (f32[128,1024]{1,0:T(8,128)S(1)}, f32[32,1024]{1,0:T(8,128)S(1)}) custom-call(bf16[80,1024]{1,0:T(8,128)(2,1)S(1)} %get-tuple-element.24.refs_0_, f32[4096,1024]{1,0:T(8,128)S(1)} %copy-done, f32[128,1024]{1,0:T(8,128)S(1)} %get-tuple-element.25.refs_2_), custom_call_target="tpu_custom_call" | custom-call | tf_op jit(solution)/shard_map/scan_factors/pallas_call | solution.py:173
  11.7 0.1 place.1
  11.8 0.6 collective-permute-start
  12.4 3.6 %collective-permute-start.3 = (f32[17,256]{1,0:T(8,128)S(1)}, f32[17,256]{1,0:T(8,128)S(1)}, u32[]{:S(2)}, u32[]{:S(2)}) collective-permute-start(f32[17,256]{1,0:T(8,128)S(1)} %get-tuple-element.30.refs_0_), channel_id=1, source_target_pairs={{0,8},{1,9},{2,10},{3,11},{4,12},{5,13},{6,14},{7,15},{8,0},{9,1},... | collective-permute-start | bytes 52232 | tf_op jit(solution)/shard_map/ppermute | solution.py:420
  16.0 1.6 %collective-permute-start.4 = (f32[17,256]{1,0:T(8,128)S(1)}, f32[17,256]{1,0:T(8,128)S(1)}, u32[]{:S(2)}, u32[]{:S(2)}) collective-permute-start(f32[17,256]{1,0:T(8,128)S(1)} %get-tuple-element.30.refs_0_), channel_id=1, source_target_pairs={{0,4},{1,5},{2,6},{3,7},{4,0},{5,1},{6,2},{7,3},{8,12},{9,13},{10,... | collective-permute-start | bytes 52232 | tf_op jit(solution)/shard_map/ppermute | solution.py:420
  17.6 1.8 %collective-permute-start.1 = (f32[64,1024]{1,0:T(8,128)S(1)}, f32[64,1024]{1,0:T(8,128)S(1)}, u32[]{:S(2)}, u32[]{:S(2)}) collective-permute-start(f32[64,1024]{1,0:T(8,128)S(1)} %get-tuple-element.47), channel_id=1, source_target_pairs={{0,2},{1,3},{2,0},{3,1},{4,6},{5,7},{6,4},{7,5},{8,10},{9,11},{10,... | collective-permute-start | bytes 786440 | tf_op jit(solution)/shard_map/ppermute | solution.py:420
  19.5 1.1 %collective-permute-start.9 = (f32[24,1024]{1,0:T(8,128)S(1)}, f32[24,1024]{1,0:T(8,128)S(1)}, u32[]{:S(2)}, u32[]{:S(2)}) collective-permute-start(f32[24,1024]{1,0:T(8,128)S(1)} %slice_add_fusion), channel_id=1, source_target_pairs={{0,2},{1,3},{2,0},{3,1},{4,6},{5,7},{6,4},{7,5},{8,10},{9,11},{10,... | collective-permute-start | bytes 294920 | tf_op jit(solution)/shard_map/ppermute | solution.py:420
  20.6 2.6 %collective-permute-done.5.refs_3_ = f32[17,256]{1,0:T(8,128)S(1)} collective-permute-done((f32[17,256]{1,0:T(8,128)S(1)}, f32[17,256]{1,0:T(8,128)S(1)}, u32[]{:S(2)}, u32[]{:S(2)}) %collective-permute-start.5) | collective-permute-done | bytes 17440 | tf_op jit(solution)/shard_map/ppermute | solution.py:420
  23.2 3.7 %collective-permute-done.1.block2 = f32[64,1024]{1,0:T(8,128)S(1)} collective-permute-done((f32[64,1024]{1,0:T(8,128)S(1)}, f32[64,1024]{1,0:T(8,128)S(1)}, u32[]{:S(2)}, u32[]{:S(2)}) %collective-permute-start.1) | collective-permute-done | bytes 262176 | tf_op jit(solution)/shard_map/ppermute | solution.py:420
  26.9 4.6 %collective-permute-done.2.block3 = f32[64,1024]{1,0:T(8,128)S(1)} collective-permute-done((f32[64,1024]{1,0:T(8,128)S(1)}, f32[64,1024]{1,0:T(8,128)S(1)}, u32[]{:S(2)}, u32[]{:S(2)}) %collective-permute-start.2) | collective-permute-done | bytes 262176 | tf_op jit(solution)/shard_map/ppermute | solution.py:420
  31.5 0.6 gather_columns.1
  32.1 0.6 collective-permute-start.6
  32.7 1.6 %collective-permute-start.7 = (f32[16,256]{1,0:T(8,128)S(1)}, f32[16,256]{1,0:T(8,128)S(1)}, u32[]{:S(2)}, u32[]{:S(2)}) collective-permute-start(f32[16,256]{1,0:T(8,128)S(1)} %get-tuple-element.31.refs_0_), channel_id=1, source_target_pairs={{0,3},{1,2},{2,1},{3,0},{4,7},{5,6},{6,5},{7,4},{8,11},{9,10},{10,... | collective-permute-start | bytes 49160 | tf_op jit(solution)/shard_map/ppermute | solution.py:420
  34.3 1.7 %collective-permute-done.6.refs_1_ = f32[16,256]{1,0:T(8,128)S(1)} collective-permute-done((f32[16,256]{1,0:T(8,128)S(1)}, f32[16,256]{1,0:T(8,128)S(1)}, u32[]{:S(2)}, u32[]{:S(2)}) %collective-permute-start.6) | collective-permute-done | bytes 16416 | tf_op jit(solution)/shard_map/ppermute | solution.py:420
  36.0 0.3 step_units.3
  36.3 1.6 %collective-permute-start.10 = (f32[16,1024]{1,0:T(8,128)S(1)}, f32[16,1024]{1,0:T(8,128)S(1)}, u32[]{:S(2)}, u32[]{:S(2)}) collective-permute-start(f32[16,1024]{1,0:T(8,128)S(1)} %get-tuple-element.33.refs_0_), channel_id=1, source_target_pairs={{0,8},{1,9},{2,10},{3,11},{4,12},{5,13},{6,14},{7,15},{8,0},{9,1},... | collective-permute-start | bytes 196616 | tf_op jit(solution)/shard_map/ppermute | solution.py:420
  38.0 2.5 %collective-permute-start.11 = (f32[16,1024]{1,0:T(8,128)S(1)}, f32[16,1024]{1,0:T(8,128)S(1)}, u32[]{:S(2)}, u32[]{:S(2)}) collective-permute-start(f32[16,1024]{1,0:T(8,128)S(1)} %get-tuple-element.33.refs_0_), channel_id=1, source_target_pairs={{0,4},{1,5},{2,6},{3,7},{4,0},{5,1},{6,2},{7,3},{8,12},{9,13},{10,... | collective-permute-start | bytes 196616 | tf_op jit(solution)/shard_map/ppermute | solution.py:420
  40.4 0.3 collective-permute-start.12
  40.7 2.5 %collective-permute-done.10.refs_1_ = f32[16,1024]{1,0:T(8,128)S(1)} collective-permute-done((f32[16,1024]{1,0:T(8,128)S(1)}, f32[16,1024]{1,0:T(8,128)S(1)}, u32[]{:S(2)}, u32[]{:S(2)}) %collective-permute-start.10) | collective-permute-done | bytes 65568 | tf_op jit(solution)/shard_map/ppermute | solution.py:420
  43.2 0.5 collective-permute-done.11.refs_2_
  43.7 3.2 %collective-permute-done.12.refs_3_ = f32[16,1024]{1,0:T(8,128)S(1)} collective-permute-done((f32[16,1024]{1,0:T(8,128)S(1)}, f32[16,1024]{1,0:T(8,128)S(1)}, u32[]{:S(2)}, u32[]{:S(2)}) %collective-permute-start.12) | collective-permute-done | bytes 65568 | tf_op jit(solution)/shard_map/ppermute | solution.py:420
  47.0 0.4 step_lines.2
  47.4 1.5 %collective-permute-start.14 = (f32[16,256]{1,0:T(8,128)S(1)}, f32[16,256]{1,0:T(8,128)S(1)}, u32[]{:S(2)}, u32[]{:S(2)}) collective-permute-start(f32[16,256]{1,0:T(8,128)S(1)} %get-tuple-element.35.refs_0_), channel_id=1, source_target_pairs={{0,2},{1,3},{2,0},{3,1},{4,6},{5,7},{6,4},{7,5},{8,10},{9,11},{10,... | collective-permute-start | bytes 49160 | tf_op jit(solution)/shard_map/ppermute | solution.py:420
  48.9 0.4 collective-permute-start.15
  49.2 1.4 %collective-permute-done.13.refs_1_ = f32[16,256]{1,0:T(8,128)S(1)} collective-permute-done((f32[16,256]{1,0:T(8,128)S(1)}, f32[16,256]{1,0:T(8,128)S(1)}, u32[]{:S(2)}, u32[]{:S(2)}) %collective-permute-start.13) | collective-permute-done | bytes 16416 | tf_op jit(solution)/shard_map/ppermute | solution.py:420
  50.7 0.6 collective-permute-done.14.refs_2_
  51.3 0.3 step_units.4
  51.6 1.3 %collective-permute-start.16 = (f32[16,1024]{1,0:T(8,128)S(1)}, f32[16,1024]{1,0:T(8,128)S(1)}, u32[]{:S(2)}, u32[]{:S(2)}) collective-permute-start(f32[16,1024]{1,0:T(8,128)S(1)} %get-tuple-element.37.refs_0_), channel_id=1, source_target_pairs={{0,8},{1,9},{2,10},{3,11},{4,12},{5,13},{6,14},{7,15},{8,0},{9,1},... | collective-permute-start | bytes 196616 | tf_op jit(solution)/shard_map/ppermute | solution.py:420
  52.9 0.8 %collective-permute-start.17 = (f32[16,1024]{1,0:T(8,128)S(1)}, f32[16,1024]{1,0:T(8,128)S(1)}, u32[]{:S(2)}, u32[]{:S(2)}) collective-permute-start(f32[16,1024]{1,0:T(8,128)S(1)} %get-tuple-element.37.refs_0_), channel_id=1, source_target_pairs={{0,4},{1,5},{2,6},{3,7},{4,0},{5,1},{6,2},{7,3},{8,12},{9,13},{10,... | collective-permute-start | bytes 196616 | tf_op jit(solution)/shard_map/ppermute | solution.py:420
  53.8 2.2 %collective-permute-start.18 = (f32[16,1024]{1,0:T(8,128)S(1)}, f32[16,1024]{1,0:T(8,128)S(1)}, u32[]{:S(2)}, u32[]{:S(2)}) collective-permute-start(f32[16,1024]{1,0:T(8,128)S(1)} %get-tuple-element.37.refs_0_), channel_id=1, source_target_pairs={{0,12},{1,13},{2,14},{3,15},{4,8},{5,9},{6,10},{7,11},{8,4},{9,5},... | collective-permute-start | bytes 196616 | tf_op jit(solution)/shard_map/ppermute | solution.py:420
  56.0 2.2 %collective-permute-done.16.refs_1_ = f32[16,1024]{1,0:T(8,128)S(1)} collective-permute-done((f32[16,1024]{1,0:T(8,128)S(1)}, f32[16,1024]{1,0:T(8,128)S(1)}, u32[]{:S(2)}, u32[]{:S(2)}) %collective-permute-start.16) | collective-permute-done | bytes 65568 | tf_op jit(solution)/shard_map/ppermute | solution.py:420
  58.2 0.2 collective-permute-done.17.refs_2_
  58.4 1.4 %collective-permute-done.18.refs_3_ = f32[16,1024]{1,0:T(8,128)S(1)} collective-permute-done((f32[16,1024]{1,0:T(8,128)S(1)}, f32[16,1024]{1,0:T(8,128)S(1)}, u32[]{:S(2)}, u32[]{:S(2)}) %collective-permute-start.18) | collective-permute-done | bytes 65568 | tf_op jit(solution)/shard_map/ppermute | solution.py:420
  59.8 0.4 step_lines.3
  60.3 1.7 %collective-permute-start.20 = (f32[16,256]{1,0:T(8,128)S(1)}, f32[16,256]{1,0:T(8,128)S(1)}, u32[]{:S(2)}, u32[]{:S(2)}) collective-permute-start(f32[16,256]{1,0:T(8,128)S(1)} %get-tuple-element.39.refs_0_), channel_id=1, source_target_pairs={{0,2},{1,3},{2,0},{3,1},{4,6},{5,7},{6,4},{7,5},{8,10},{9,11},{10,... | collective-permute-start | bytes 49160 | tf_op jit(solution)/shard_map/ppermute | solution.py:420
  62.0 0.2 collective-permute-start.21
  62.1 1.3 %collective-permute-done.19.refs_1_ = f32[16,256]{1,0:T(8,128)S(1)} collective-permute-done((f32[16,256]{1,0:T(8,128)S(1)}, f32[16,256]{1,0:T(8,128)S(1)}, u32[]{:S(2)}, u32[]{:S(2)}) %collective-permute-start.19) | collective-permute-done | bytes 16416 | tf_op jit(solution)/shard_map/ppermute | solution.py:420
  63.4 0.6 collective-permute-done.20.refs_2_
  64.1 0.3 step_units.5
  64.4 2.3 %collective-permute-start.24 = (f32[16,256]{1,0:T(8,128)S(1)}, f32[16,256]{1,0:T(8,128)S(1)}, u32[]{:S(2)}, u32[]{:S(2)}) collective-permute-start(f32[16,256]{1,0:T(8,128)S(1)} %get-tuple-element.51), channel_id=1, source_target_pairs={{0,12},{1,13},{2,14},{3,15},{4,8},{5,9},{6,10},{7,11},{8,4},{9,5},... | collective-permute-start | bytes 49160 | tf_op jit(solution)/shard_map/ppermute | solution.py:420
  66.7 2.1 %collective-permute-start.22 = (f32[16,256]{1,0:T(8,128)S(1)}, f32[16,256]{1,0:T(8,128)S(1)}, u32[]{:S(2)}, u32[]{:S(2)}) collective-permute-start(f32[16,256]{1,0:T(8,128)S(1)} %get-tuple-element.50), channel_id=1, source_target_pairs={{0,8},{1,9},{2,10},{3,11},{4,12},{5,13},{6,14},{7,15},{8,0},{9,1},... | collective-permute-start | bytes 49160 | tf_op jit(solution)/shard_map/ppermute | solution.py:420
  68.8 0.7 fusion.6
  69.5 0.5 collective-permute-done.24
  70.0 0.4 collective-permute-done.23
  70.4 0.9 %collective-permute-done.22 = f32[16,256]{1,0:T(8,128)S(1)} collective-permute-done((f32[16,256]{1,0:T(8,128)S(1)}, f32[16,256]{1,0:T(8,128)S(1)}, u32[]{:S(2)}, u32[]{:S(2)}) %collective-permute-start.22) | collective-permute-done | bytes 16416 | tf_op jit(solution)/shard_map/ppermute | solution.py:420
  71.3 0.6 subtract_bitcast_fusion
  (48 shorter events, 0.4 us)
Async XLA Ops:
  0.6 8.3 %copy-start = (f32[4096,1024]{1,0:T(8,128)S(1)}, f32[4096,1024]{1,0:T(8,128)}, u32[]{:S(2)}) copy-start(f32[4096,1024]{1,0:T(8,128)} %refs_1_.1) | copy-start | bytes 50331652
  0.6 11.0 %copy-start.1 = (f32[256,16]{0,1:T(8,128)S(1)}, f32[256,16]{0,1:T(8,128)}, u32[]{:S(2)}) copy-start(f32[256,16]{0,1:T(8,128)} %param.16) | copy-start | bytes 49156
  0.7 11.0 %copy-start.2 = (f32[32,16]{0,1:T(8,128)S(1)}, f32[32,16]{0,1:T(8,128)}, u32[]{:S(2)}) copy-start(f32[32,16]{0,1:T(8,128)} %param.14) | copy-start | bytes 6148
  0.7 11.0 %copy-start.3 = (f32[16,32]{1,0:T(8,128)S(1)}, f32[16,32]{1,0:T(8,128)}, u32[]{:S(2)}) copy-start(f32[16,32]{1,0:T(8,128)} %charging.1) | copy-start | bytes 6148
  0.7 11.0 %copy-start.4 = (f32[16,32]{1,0:T(8,128)S(1)}, f32[16,32]{1,0:T(8,128)}, u32[]{:S(2)}) copy-start(f32[16,32]{1,0:T(8,128)} %energy_dual.1) | copy-start | bytes 6148
  0.7 11.0 %copy-start.5 = (f32[256]{0:T(256)S(1)}, f32[256]{0:T(256)}, u32[]{:S(2)}) copy-start(f32[256]{0:T(256)} %param.27) | copy-start | bytes 3076
  0.7 11.0 %copy-start.6 = (f32[32]{0:T(128)S(1)}, f32[32]{0:T(128)}, u32[]{:S(2)}) copy-start(f32[32]{0:T(128)} %param.22) | copy-start | bytes 388
  0.7 11.0 %copy-start.7 = (f32[32]{0:T(128)S(1)}, f32[32]{0:T(128)}, u32[]{:S(2)}) copy-start(f32[32]{0:T(128)} %param.23) | copy-start | bytes 388
  0.7 19.8 %copy-start.8 = (f32[512]{0:T(512)S(1)}, f32[512]{0:T(512)}, u32[]{:S(2)}) copy-start(f32[512]{0:T(512)} %param.24) | copy-start | bytes 6148
  0.7 19.8 %copy-start.9 = (f32[512]{0:T(512)S(1)}, f32[512]{0:T(512)}, u32[]{:S(2)}) copy-start(f32[512]{0:T(512)} %param.25) | copy-start | bytes 6148
  0.7 19.8 %copy-start.10 = (f32[512]{0:T(512)S(1)}, f32[512]{0:T(512)}, u32[]{:S(2)}) copy-start(f32[512]{0:T(512)} %param.26) | copy-start | bytes 6148
  11.8 7.6 %collective-permute-start = (f32[104,1024]{1,0:T(8,128)S(1)}, f32[104,1024]{1,0:T(8,128)S(1)}, u32[]{:S(2)}, u32[]{:S(2)}) collective-permute-start(f32[104,1024]{1,0:T(8,128)S(1)} %pad_maximum_fusion), channel_id=1, source_target_pairs={{0,1},{1,0},{2,3},{3,2},{4,5},{5,4},{6,7},{7,6},{8,9},{9,8},{10,11... | collective-permute-start | bytes 1277960 | tf_op jit(solution)/shard_map/ppermute | solution.py:420
  12.4 7.1 %collective-permute-start.3 = (f32[17,256]{1,0:T(8,128)S(1)}, f32[17,256]{1,0:T(8,128)S(1)}, u32[]{:S(2)}, u32[]{:S(2)}) collective-permute-start(f32[17,256]{1,0:T(8,128)S(1)} %get-tuple-element.30.refs_0_), channel_id=1, source_target_pairs={{0,8},{1,9},{2,10},{3,11},{4,12},{5,13},{6,14},{7,15},{8,0},{9,1},... | collective-permute-start | bytes 52232 | tf_op jit(solution)/shard_map/ppermute | solution.py:420
  16.0 4.6 %collective-permute-start.4 = (f32[17,256]{1,0:T(8,128)S(1)}, f32[17,256]{1,0:T(8,128)S(1)}, u32[]{:S(2)}, u32[]{:S(2)}) collective-permute-start(f32[17,256]{1,0:T(8,128)S(1)} %get-tuple-element.30.refs_0_), channel_id=1, source_target_pairs={{0,4},{1,5},{2,6},{3,7},{4,0},{5,1},{6,2},{7,3},{8,12},{9,13},{10,... | collective-permute-start | bytes 52232 | tf_op jit(solution)/shard_map/ppermute | solution.py:420
  17.6 5.6 %collective-permute-start.5 = (f32[17,256]{1,0:T(8,128)S(1)}, f32[17,256]{1,0:T(8,128)S(1)}, u32[]{:S(2)}, u32[]{:S(2)}) collective-permute-start(f32[17,256]{1,0:T(8,128)S(1)} %get-tuple-element.30.refs_0_), channel_id=1, source_target_pairs={{0,12},{1,13},{2,14},{3,15},{4,8},{5,9},{6,10},{7,11},{8,4},{9,5},... | collective-permute-start | bytes 52232 | tf_op jit(solution)/shard_map/ppermute | solution.py:420
  17.6 9.2 %collective-permute-start.1 = (f32[64,1024]{1,0:T(8,128)S(1)}, f32[64,1024]{1,0:T(8,128)S(1)}, u32[]{:S(2)}, u32[]{:S(2)}) collective-permute-start(f32[64,1024]{1,0:T(8,128)S(1)} %get-tuple-element.47), channel_id=1, source_target_pairs={{0,2},{1,3},{2,0},{3,1},{4,6},{5,7},{6,4},{7,5},{8,10},{9,11},{10,... | collective-permute-start | bytes 786440 | tf_op jit(solution)/shard_map/ppermute | solution.py:420
  19.4 12.1 %collective-permute-start.2 = (f32[64,1024]{1,0:T(8,128)S(1)}, f32[64,1024]{1,0:T(8,128)S(1)}, u32[]{:S(2)}, u32[]{:S(2)}) collective-permute-start(f32[64,1024]{1,0:T(8,128)S(1)} %get-tuple-element.46), channel_id=1, source_target_pairs={{0,3},{1,2},{2,1},{3,0},{4,7},{5,6},{6,5},{7,4},{8,11},{9,10},{10,... | collective-permute-start | bytes 786440 | tf_op jit(solution)/shard_map/ppermute | solution.py:420
  19.5 14.8 %collective-permute-start.9 = (f32[24,1024]{1,0:T(8,128)S(1)}, f32[24,1024]{1,0:T(8,128)S(1)}, u32[]{:S(2)}, u32[]{:S(2)}) collective-permute-start(f32[24,1024]{1,0:T(8,128)S(1)} %slice_add_fusion), channel_id=1, source_target_pairs={{0,2},{1,3},{2,0},{3,1},{4,6},{5,7},{6,4},{7,5},{8,10},{9,11},{10,... | collective-permute-start | bytes 294920 | tf_op jit(solution)/shard_map/ppermute | solution.py:420
  32.1 4.0 %collective-permute-start.6 = (f32[16,256]{1,0:T(8,128)S(1)}, f32[16,256]{1,0:T(8,128)S(1)}, u32[]{:S(2)}, u32[]{:S(2)}) collective-permute-start(f32[16,256]{1,0:T(8,128)S(1)} %get-tuple-element.31.refs_0_), channel_id=1, source_target_pairs={{0,2},{1,3},{2,0},{3,1},{4,6},{5,7},{6,4},{7,5},{8,10},{9,11},{10,... | collective-permute-start | bytes 49160 | tf_op jit(solution)/shard_map/ppermute | solution.py:420
  32.7 3.4 %collective-permute-start.7 = (f32[16,256]{1,0:T(8,128)S(1)}, f32[16,256]{1,0:T(8,128)S(1)}, u32[]{:S(2)}, u32[]{:S(2)}) collective-permute-start(f32[16,256]{1,0:T(8,128)S(1)} %get-tuple-element.31.refs_0_), channel_id=1, source_target_pairs={{0,3},{1,2},{2,1},{3,0},{4,7},{5,6},{6,5},{7,4},{8,11},{9,10},{10,... | collective-permute-start | bytes 49160 | tf_op jit(solution)/shard_map/ppermute | solution.py:420
  34.3 1.8 %collective-permute-start.8 = (f32[16,256]{1,0:T(8,128)S(1)}, f32[16,256]{1,0:T(8,128)S(1)}, u32[]{:S(2)}, u32[]{:S(2)}) collective-permute-start(f32[16,256]{1,0:T(8,128)S(1)} %get-tuple-element.31.refs_0_), channel_id=1, source_target_pairs={{0,1},{1,0},{2,3},{3,2},{4,5},{5,4},{6,7},{7,6},{8,9},{9,8},{10,11... | collective-permute-start | bytes 49160 | tf_op jit(solution)/shard_map/ppermute | solution.py:420
  36.3 6.9 %collective-permute-start.10 = (f32[16,1024]{1,0:T(8,128)S(1)}, f32[16,1024]{1,0:T(8,128)S(1)}, u32[]{:S(2)}, u32[]{:S(2)}) collective-permute-start(f32[16,1024]{1,0:T(8,128)S(1)} %get-tuple-element.33.refs_0_), channel_id=1, source_target_pairs={{0,8},{1,9},{2,10},{3,11},{4,12},{5,13},{6,14},{7,15},{8,0},{9,1},... | collective-permute-start | bytes 196616 | tf_op jit(solution)/shard_map/ppermute | solution.py:420
  38.0 5.8 %collective-permute-start.11 = (f32[16,1024]{1,0:T(8,128)S(1)}, f32[16,1024]{1,0:T(8,128)S(1)}, u32[]{:S(2)}, u32[]{:S(2)}) collective-permute-start(f32[16,1024]{1,0:T(8,128)S(1)} %get-tuple-element.33.refs_0_), channel_id=1, source_target_pairs={{0,4},{1,5},{2,6},{3,7},{4,0},{5,1},{6,2},{7,3},{8,12},{9,13},{10,... | collective-permute-start | bytes 196616 | tf_op jit(solution)/shard_map/ppermute | solution.py:420
  40.4 6.5 %collective-permute-start.12 = (f32[16,1024]{1,0:T(8,128)S(1)}, f32[16,1024]{1,0:T(8,128)S(1)}, u32[]{:S(2)}, u32[]{:S(2)}) collective-permute-start(f32[16,1024]{1,0:T(8,128)S(1)} %get-tuple-element.33.refs_0_), channel_id=1, source_target_pairs={{0,12},{1,13},{2,14},{3,15},{4,8},{5,9},{6,10},{7,11},{8,4},{9,5},... | collective-permute-start | bytes 196616 | tf_op jit(solution)/shard_map/ppermute | solution.py:420
  47.3 3.4 %collective-permute-start.13 = (f32[16,256]{1,0:T(8,128)S(1)}, f32[16,256]{1,0:T(8,128)S(1)}, u32[]{:S(2)}, u32[]{:S(2)}) collective-permute-start(f32[16,256]{1,0:T(8,128)S(1)} %get-tuple-element.35.refs_0_), channel_id=1, source_target_pairs={{0,3},{1,2},{2,1},{3,0},{4,7},{5,6},{6,5},{7,4},{8,11},{9,10},{10,... | collective-permute-start | bytes 49160 | tf_op jit(solution)/shard_map/ppermute | solution.py:420
  47.4 3.9 %collective-permute-start.14 = (f32[16,256]{1,0:T(8,128)S(1)}, f32[16,256]{1,0:T(8,128)S(1)}, u32[]{:S(2)}, u32[]{:S(2)}) collective-permute-start(f32[16,256]{1,0:T(8,128)S(1)} %get-tuple-element.35.refs_0_), channel_id=1, source_target_pairs={{0,2},{1,3},{2,0},{3,1},{4,6},{5,7},{6,4},{7,5},{8,10},{9,11},{10,... | collective-permute-start | bytes 49160 | tf_op jit(solution)/shard_map/ppermute | solution.py:420
  48.9 2.5 %collective-permute-start.15 = (f32[16,256]{1,0:T(8,128)S(1)}, f32[16,256]{1,0:T(8,128)S(1)}, u32[]{:S(2)}, u32[]{:S(2)}) collective-permute-start(f32[16,256]{1,0:T(8,128)S(1)} %get-tuple-element.35.refs_0_), channel_id=1, source_target_pairs={{0,1},{1,0},{2,3},{3,2},{4,5},{5,4},{6,7},{7,6},{8,9},{9,8},{10,11... | collective-permute-start | bytes 49160 | tf_op jit(solution)/shard_map/ppermute | solution.py:420
  51.6 6.6 %collective-permute-start.16 = (f32[16,1024]{1,0:T(8,128)S(1)}, f32[16,1024]{1,0:T(8,128)S(1)}, u32[]{:S(2)}, u32[]{:S(2)}) collective-permute-start(f32[16,1024]{1,0:T(8,128)S(1)} %get-tuple-element.37.refs_0_), channel_id=1, source_target_pairs={{0,8},{1,9},{2,10},{3,11},{4,12},{5,13},{6,14},{7,15},{8,0},{9,1},... | collective-permute-start | bytes 196616 | tf_op jit(solution)/shard_map/ppermute | solution.py:420
  52.9 5.5 %collective-permute-start.17 = (f32[16,1024]{1,0:T(8,128)S(1)}, f32[16,1024]{1,0:T(8,128)S(1)}, u32[]{:S(2)}, u32[]{:S(2)}) collective-permute-start(f32[16,1024]{1,0:T(8,128)S(1)} %get-tuple-element.37.refs_0_), channel_id=1, source_target_pairs={{0,4},{1,5},{2,6},{3,7},{4,0},{5,1},{6,2},{7,3},{8,12},{9,13},{10,... | collective-permute-start | bytes 196616 | tf_op jit(solution)/shard_map/ppermute | solution.py:420
  53.8 6.1 %collective-permute-start.18 = (f32[16,1024]{1,0:T(8,128)S(1)}, f32[16,1024]{1,0:T(8,128)S(1)}, u32[]{:S(2)}, u32[]{:S(2)}) collective-permute-start(f32[16,1024]{1,0:T(8,128)S(1)} %get-tuple-element.37.refs_0_), channel_id=1, source_target_pairs={{0,12},{1,13},{2,14},{3,15},{4,8},{5,9},{6,10},{7,11},{8,4},{9,5},... | collective-permute-start | bytes 196616 | tf_op jit(solution)/shard_map/ppermute | solution.py:420
  60.2 3.2 %collective-permute-start.19 = (f32[16,256]{1,0:T(8,128)S(1)}, f32[16,256]{1,0:T(8,128)S(1)}, u32[]{:S(2)}, u32[]{:S(2)}) collective-permute-start(f32[16,256]{1,0:T(8,128)S(1)} %get-tuple-element.39.refs_0_), channel_id=1, source_target_pairs={{0,3},{1,2},{2,1},{3,0},{4,7},{5,6},{6,5},{7,4},{8,11},{9,10},{10,... | collective-permute-start | bytes 49160 | tf_op jit(solution)/shard_map/ppermute | solution.py:420
  60.3 3.8 %collective-permute-start.20 = (f32[16,256]{1,0:T(8,128)S(1)}, f32[16,256]{1,0:T(8,128)S(1)}, u32[]{:S(2)}, u32[]{:S(2)}) collective-permute-start(f32[16,256]{1,0:T(8,128)S(1)} %get-tuple-element.39.refs_0_), channel_id=1, source_target_pairs={{0,2},{1,3},{2,0},{3,1},{4,6},{5,7},{6,4},{7,5},{8,10},{9,11},{10,... | collective-permute-start | bytes 49160 | tf_op jit(solution)/shard_map/ppermute | solution.py:420
  62.0 2.1 %collective-permute-start.21 = (f32[16,256]{1,0:T(8,128)S(1)}, f32[16,256]{1,0:T(8,128)S(1)}, u32[]{:S(2)}, u32[]{:S(2)}) collective-permute-start(f32[16,256]{1,0:T(8,128)S(1)} %get-tuple-element.39.refs_0_), channel_id=1, source_target_pairs={{0,1},{1,0},{2,3},{3,2},{4,5},{5,4},{6,7},{7,6},{8,9},{9,8},{10,11... | collective-permute-start | bytes 49160 | tf_op jit(solution)/shard_map/ppermute | solution.py:420
  64.4 5.6 %collective-permute-start.24 = (f32[16,256]{1,0:T(8,128)S(1)}, f32[16,256]{1,0:T(8,128)S(1)}, u32[]{:S(2)}, u32[]{:S(2)}) collective-permute-start(f32[16,256]{1,0:T(8,128)S(1)} %get-tuple-element.51), channel_id=1, source_target_pairs={{0,12},{1,13},{2,14},{3,15},{4,8},{5,9},{6,10},{7,11},{8,4},{9,5},... | collective-permute-start | bytes 49160 | tf_op jit(solution)/shard_map/ppermute | solution.py:420
  66.7 3.7 %collective-permute-start.23 = (f32[16,256]{1,0:T(8,128)S(1)}, f32[16,256]{1,0:T(8,128)S(1)}, u32[]{:S(2)}, u32[]{:S(2)}) collective-permute-start(f32[16,256]{1,0:T(8,128)S(1)} %get-tuple-element.52), channel_id=1, source_target_pairs={{0,4},{1,5},{2,6},{3,7},{4,0},{5,1},{6,2},{7,3},{8,12},{9,13},{10,... | collective-permute-start | bytes 49160 | tf_op jit(solution)/shard_map/ppermute | solution.py:420
  66.7 4.6 %collective-permute-start.22 = (f32[16,256]{1,0:T(8,128)S(1)}, f32[16,256]{1,0:T(8,128)S(1)}, u32[]{:S(2)}, u32[]{:S(2)}) collective-permute-start(f32[16,256]{1,0:T(8,128)S(1)} %get-tuple-element.50), channel_id=1, source_target_pairs={{0,8},{1,9},{2,10},{3,11},{4,12},{5,13},{6,14},{7,15},{8,0},{9,1},... | collective-permute-start | bytes 49160 | tf_op jit(solution)/shard_map/ppermute | solution.py:420
